TPU v7x, 256 devices: a whole 4x4x8 slice. The times are simulated.
256 devices in a mesh: row: 8 (over x, core), col: 32 (over z, y).
Axes of the slice: x: 4, y: 4, z: 8, core: 2. Of those that a mesh axis runs over, the one named last changes fastest.
Arguments:
- blocks: bfloat16 [12288, 27, 48, 48], P(('row', 'col')), may hold values from -0.59765625 to 0.59765625
- prolong: bfloat16 [12288, 48, 48], P(('row', 'col')), may hold values from -0.875 to 0.875
- columns: int32 [12288, 27], P(('row', 'col')), may hold values from 0 to 383
- aggregate: int32 [12288], P(('row', 'col')), may hold values from 0 to 15
- slots: int32 [12288, 27], P(('row', 'col')), may hold values from 0 to 26
Outputs:
- coarse: float32 [128, 27, 2304], P('row', None, 'col')
Inputs may be any that keep to these rules, and one draw needn't show every extreme that they name: `columns`: a fine block row's neighbours all lie in its column tile: the fine block rows of the devices with the same col index, in order of their row index.
All inputs are finite; a program needn't handle non-finite values.
Results may differ from a plain program's by a relative error of at most 0.0029.
Values may be sent and summed in bfloat16 or wider, within the bound.
No kernel may reach another device: no remote copies, remote signals or barrier semaphores. Data moves between devices by JAX's collectives and lax.ppermute only.
A program may use at most 192 MiB of HBM per device.

v0:
```python
import jax
import jax.numpy as jnp
from jax import lax
from jax.sharding import PartitionSpec as P

KC = 27
CR_SLAB = 16


def shards(blocks, prolong, columns, aggregate, slots):
    width = blocks.shape[2]
    tile = lax.all_gather(prolong, "row", axis=0, tiled=True)
    picked = jnp.take(tile, columns, axis=0)
    product = jnp.einsum(
        "rkab,rkbc->rkac", blocks, picked, preferred_element_type=jnp.float32
    ).astype(jnp.bfloat16)
    term = jnp.einsum("rba,rkbc->rkac", prolong, product, preferred_element_type=jnp.float32)
    target = (aggregate[:, None] * KC + slots).reshape(-1)
    partial_value = jax.ops.segment_sum(
        term.reshape(-1, width * width), target, num_segments=CR_SLAB * KC
    )
    partial_value = partial_value.reshape(CR_SLAB, KC, width * width)
    summed = lax.psum(partial_value, "col")
    share = width * width // lax.axis_size("col")
    result = lax.dynamic_slice_in_dim(summed, lax.axis_index("col") * share, share, 2)
    return result


def solution(mesh):
    return jax.shard_map(
        shards,
        mesh=mesh,
        in_specs=(
            P(("row", "col"), None, None, None),
            P(("row", "col"), None, None),
            P(("row", "col"), None),
            P(("row", "col")),
            P(("row", "col"), None),
        ),
        out_specs=P("row", None, "col"),
        check_vma=False,
    )
```

profile of v0, /device:TPU:2, one launch (start us, length us, event | category | flops | bytes accessed | tf_op | source)
XLA Modules:
  0.0 371.9 jit_solution(16122000803956569116)
XLA Ops:
  6.5 0.0 all-gather.2.cloned.1.call-start
  6.5 0.7 all-gather.2.cloned.1.call-update
  7.3 0.0 all-reduce.2.cloned.1.call-start
  7.3 0.7 compare_select_fusion
  8.0 0.1 copy.14
  8.1 0.1 reshape.17
  8.2 0.7 compare_and_fusion
  9.0 0.1 copy.13
  9.1 0.7 broadcast_multiply_fusion
  9.7 0.7 broadcast_add_fusion
  10.4 0.1 copy.12
  10.5 0.1 reshape.25
  10.7 37.4 %all-gather.2.cloned.1.call-done = bf16[384,48,48]{2,1,0:T(8,128)(2,1)} async-done(((bf16[48,48,48]{2,1,0:T(8,128)(2,1)}), bf16[384,48,48]{2,1,0:T(8,128)(2,1)}) %all-gather.2.cloned.1.call-update) | async-done | bytes 1769488 | tf_op jit(solution)/shard_map/all_gather | solution.py:12
  48.0 10.4 %gather_fusion = bf16[1296,48,48]{2,1,0:T(8,128)(2,1)} fusion(bf16[384,48,48]{2,1,0:T(8,128)(2,1)} %all-gather.2.cloned.1.call-done, s32[2048]{0:T(1024)S(1)} %pad_clamp_fusion), kind=kCustom, calls=%fused_computation | custom fusion | bytes 11949120 | tf_op jit(solution)/shard_map/jit(_take)/gather | solution.py:13
  58.5 0.0 copy-start
  58.5 22.0 %copy.15 = bf16[48,27,48,48]{2,3,1,0:T(8,128)(2,1)} copy(bf16[48,27,48,48]{3,2,1,0:T(8,128)(2,1)} %bitcast.16) | data formatting | bytes 11943936 | tf_op jit(solution)/shard_map/jit(_take)/gather | solution.py:13
  80.4 0.0 copy-done
  80.4 27.9 %fusion.10 = f32[48,27,48,48]{2,3,1,0:T(8,128)} fusion(bf16[48,27,48,48]{3,2,1,0:T(8,128)(2,1)} %param.5, bf16[48,27,48,48]{2,3,1,0:T(8,128)(2,1)} %copy.15, pred[48,27]{1,0:T(8,128)(4,1)S(1)} %copy.13, bf16[48,48,48]{2,1,0:T(8,128)(2,1)S(1)} %copy-done), kind=kOutput, calls=%fused_computation.8 | convolution fusion | flops 579280896 | bytes 24110352 | tf_op jit(solution)/shard_map/rba,rkbc->rkac/dot_general | solution.py:17
  108.3 32.6 %copy.16 = f32[48,27,48,48]{3,2,1,0:T(8,128)} copy(f32[48,27,48,48]{2,3,1,0:T(8,128)} %fusion.10) | data formatting | bytes 23887872 | tf_op jit(solution)/shard_map/rba,rkbc->rkac/transpose | solution.py:17
  140.9 25.7 %reshape.27 = f32[1296,2304]{1,0:T(8,128)} reshape(f32[48,27,48,48]{3,2,1,0:T(8,128)} %copy.16) | data formatting | bytes 23887872 | tf_op jit(solution)/shard_map/reshape | solution.py:20
  166.6 24.2 %scatter_custom_fusion = f32[432,2304]{1,0:T(8,128)} fusion(s32[1296]{0:T(1024)S(1)} %reshape.25, f32[1296,2304]{1,0:T(8,128)} %reshape.27, f32[]{:T(128)} %constant.9.clone.1), kind=kCustom, calls=%fused_computation.10 | custom fusion | flops 2985984 | bytes 3981824 | tf_op jit(solution)/shard_map/scatter-add | solution.py:19
  190.8 3.9 %reshape.14 = f32[16,27,2304]{2,1,0:T(8,128)} reshape(f32[432,2304]{1,0:T(8,128)} %scatter_custom_fusion) | data formatting | bytes 7962624 | tf_op jit(solution)/shard_map/reshape | solution.py:22
  194.7 0.0 all-reduce.2.cloned.1.call-update
  194.8 168.3 %all-reduce.2.cloned.1.call-done = f32[16,27,2304]{2,1,0:T(8,128)} async-done(((f32[16,27,2304]{2,1,0:T(8,128)}), f32[16,27,2304]{2,1,0:T(8,128)}) %all-reduce.2.cloned.1.call-update) | async-done | bytes 3981328 | tf_op jit(solution)/shard_map/psum | solution.py:23
  363.1 1.2 constant_dynamic-slice_fusion
  364.3 0.8 copy.17
  (1 shorter events, 0.0 us)
Async XLA Ops:
  6.5 41.5 %all-gather.2.cloned.1.call-start = ((), (), s32[]{:S(2)}) async-start(), calls=%async_computation | async-start | bytes 5308416 | tf_op jit(solution)/shard_map/all_gather | solution.py:12
  7.3 355.8 %all-reduce.2.cloned.1.call-start = ((), (), s32[]{:S(2)}) async-start(), calls=%async_computation.1 | async-start | bytes 9437184 | tf_op jit(solution)/shard_map/psum | solution.py:23
  58.5 22.0 %copy-start = (bf16[48,48,48]{2,1,0:T(8,128)(2,1)S(1)}, bf16[48,48,48]{2,1,0:T(8,128)(2,1)}, u32[]{:S(2)}) copy-start(bf16[48,48,48]{2,1,0:T(8,128)(2,1)} %param.6) | copy-start | bytes 663556
Sparse Core Ops, SparseCore 0:
  9.2 38.8 all-gather.1
  194.9 168.1 all-reduce.1
where the time goes:
time: 374 us; the launch traced here: 372 us
  waiting for transfers between devices  206 us (55%)
  local copies, waits for them, and re-layouts  97.1 us (26%)
  matrix products  27.9 us (7%)
  other arithmetic  27.1 us (7%)
  between operations  13.4 us (4%)
    psum x1, waiting for transfers between devices, shards(): summed = lax.psum(partial_value, 'col')  168 us
    all_gather x1, waiting for transfers between devices, shards(): tile = lax.all_gather(prolong, 'row', axis=0, tiled=True)  37.4 us
    transpose x1, local copies, waits for them, and re-layouts, shards(): jnp.einsum('rba,rkbc->rkac', prolong, product, preferred_element_type=jnp...  32.6 us
    gather x2, local copies, waits for them, and re-layouts, shards(): picked = jnp.take(tile, columns, axis=0)  32.4 us
    dot_general x1, matrix products, shards(): jnp.einsum('rba,rkbc->rkac', prolong, product, preferred_element_type=jnp...  27.9 us
    reshape x1, local copies, waits for them, and re-layouts, shards(): term.reshape(-1, width * width)  25.7 us
    scatter-add x1, other arithmetic, shards(): jax.ops.segment_sum(term.reshape(-1, width * width), target, num_segments...  24.2 us
  transfers between devices with their start and end apart: 2, of which 2 were waited for; matrix products, arithmetic and copies ran while one was open for 1% of the time, Pallas kernels for 0%

commit v1 on v0

v1 whole, which is shorter than its diff:
```python
import functools
import jax, jax.numpy as jnp
from jax import lax
from jax.experimental import pallas as pl
from jax.experimental.pallas import tpu as pltpu
bf, f32 = jnp.bfloat16, jnp.float32
B, K, KC, CR, R = 48, 27, 27, 16, 48
T = KC * CR
H = B // 2
HALF = T * H
PAIRS = (K + 1) // 2
PLACES = [[(0, 0), (0, 1), (1, 0)], [(0, 2), (1, 1), (1, 2)], [(0, 3), (0, 4), (1, 3)], [(0, 5), (1, 4), (1, 5)]]

def pack_kernel(p_ref, o_ref):
    for g in range(R // 8):
        o_ref[g * B:(g + 1) * B, :] = jnp.concatenate(
            [p_ref[8 * g + m].astype(f32).T for m in range(8)], axis=1).astype(bf)

def pack(p):
    return pl.pallas_call(pack_kernel, out_shape=jax.ShapeDtypeStruct((R // 8 * B, 8 * B), bf))(p)

def main_kernel(G, cols, slots, agg, blk_hbm, pro, pg, out, blk, plo, phi, alo, ahi, bufa, bufb, ta, tb, sems):
    CH = 4
    def copy(n):
        return pltpu.make_async_copy(blk_hbm.at[pl.ds(n * CH, CH)], blk.at[pl.ds(n * CH, CH)], sems.at[n])
    for n in range(R // CH):
        copy(n).start()
    if True:
        for m in range(8):
            first = (48 * m // 128) * 128
            wide = min(256, 384 - first)
            row = lax.broadcasted_iota(jnp.int32, (wide, 256), 0) + first - 48 * m
            lane = lax.broadcasted_iota(jnp.int32, (wide, 256), 1)
            inside = (row >= 0) & (row < 48)
            pick = (inside & ((lane == row) | (lane == row + 128 + 48))).astype(f32).astype(bf)
            def unpack(n, c):
                x = pg[pl.ds(pl.multiple_of(n * 192, 192), 192), first:first + wide]
                y = jnp.dot(x, pick, preferred_element_type=f32).astype(bf)
                at = pl.multiple_of(m * 48 * B + n * 192, 192)
                plo[pl.ds(at, 192), :] = y[:, :128]
                phi[pl.ds(at, 192), :] = y[:, 128:]
                z = pl.multiple_of((m * 12 + n) * 216, 8)
                alo[pl.ds(z, 216), :] = jnp.zeros((216, 128), f32)
                ahi[pl.ds(z, 216), :] = jnp.zeros((216, 128), f32)
                return c
            lax.fori_loop(0, 12, unpack, 0)

    bufa[:, 96:] = jnp.zeros((PAIRS * B, 32), bf)
    bufb[:, 96:] = jnp.zeros((PAIRS * B, 32), bf)

    def phase1(i, n, buf):
        two = range(2 * n, min(2 * n + 2, K))
        at = []
        for k in two:
            j = cols[k, i]
            at.append(pl.multiple_of(((j & 7) * 48 + (j >> 3)) * B, B))
        lhs = plo[pl.ds(at[0], B), :]
        zero = jnp.zeros((B, B), bf)
        if len(two) == 2:
            lhs = lhs + phi[pl.ds(at[1], B), :]
            w = jnp.concatenate([jnp.concatenate([blk[i, two[0]], zero], axis=1),
                                 jnp.concatenate([zero, blk[i, two[1]]], axis=1)], axis=0)
            p = lax.dot_general(lhs[:, :96], w, (((1,), (1,)), ((), ())), preferred_element_type=f32)
        else:
            w = jnp.concatenate([jnp.concatenate([blk[i, two[0]], zero], axis=1), jnp.zeros((B, 2 * B), bf)], axis=0)
            p = lax.dot_general(lhs[:, :96], w, (((1,), (1,)), ((), ())), preferred_element_type=f32)
        buf[n * B:(n + 1) * B, :96] = p.astype(bf)

    def phase2(w, n, buf, tbuf):
        tbuf[n * B:(n + G) * B, :] = jnp.dot(buf[n * B:(n + G) * B, :], w, preferred_element_type=f32)

    def add(i, base, n, tbuf):
        for k in range(2 * n, min(2 * n + 2, K)):
            at = pl.multiple_of((slots[k, i] * CR + base) * H, 8)
            acc = ahi if k & 1 else alo
            for h in range(2):
                acc[pl.ds(at + h * HALF, H), :] += tbuf[n * B + h * H:n * B + (h + 1) * H, :]

    def both(i1, buf1, i2, buf2, tbuf):
        w = pro[i2]
        base = agg[i2]
        for n in range(PAIRS):
            if n % G == 0:
                phase2(w, n, buf2, tbuf)
            if True:
                phase1(i1, n, buf1)
            if True:
                add(i2, base, n, tbuf)

    if True:
        copy(0).wait()
        for n in range(PAIRS):
            phase1(0, n, bufa)

        def rows(q, c):
            both(2 * q + 1, bufb, 2 * q, bufa, ta)
            @pl.when((q & 1 == 1) & (q < 23))
            def _():
                copy((q + 1) // 2).wait()
            both(jnp.minimum(2 * q + 2, R - 1), bufa, 2 * q + 1, bufb, tb)
            return c
        lax.fori_loop(0, R // 2, rows, 0)
    else:
        for n in range(R // CH):
            copy(n).wait()

    if True:
        def flush(n, c):
            low = lax.broadcasted_iota(jnp.int32, (128, 128), 1) < B
            halves = []
            for h in range(2):
                at = pl.multiple_of(h * HALF + n * 128, 128)
                x = jnp.where(low, alo[pl.ds(at, 128), :], ahi[pl.ds(at, 128), :]).T
                halves.append(x[:B] + x[B:2 * B])
            at = pl.multiple_of(n * 128, 128)
            for y in range(4):
                rows = [halves[h][8 * u:8 * u + 8] for h, u in PLACES[y]]
                out[y, :, pl.ds(at, 128)] = jnp.concatenate(rows, axis=0).astype(bf)
            return c
        lax.fori_loop(0, HALF // 128, flush, 0)

def main(colsT, slotsT, agg, blocks, wide, pg, G=14):
    return pl.pallas_call(
        functools.partial(main_kernel, G),
        out_shape=jax.ShapeDtypeStruct((4, 24, HALF), bf),
        in_specs=[pl.BlockSpec(memory_space=pltpu.SMEM)] * 3 + [pl.BlockSpec(memory_space=pl.ANY)] + [pl.BlockSpec(memory_space=pltpu.VMEM)] * 2,
        out_specs=pl.BlockSpec(memory_space=pltpu.VMEM),
        scratch_shapes=[pltpu.VMEM((R, K, B, B), bf)] + [pltpu.VMEM((384 * B, 128), bf)] * 2 + [pltpu.VMEM((2 * HALF, 128), f32)] * 2
            + [pltpu.VMEM((PAIRS * B, 128), bf)] * 2 + [pltpu.VMEM((PAIRS * B, 128), f32)] * 2 + [pltpu.SemaphoreType.DMA((12,))],
        compiler_params=pltpu.CompilerParams(vmem_limit_bytes=63 << 20),
    )(colsT, slotsT, agg, blocks, wide, pg)

def weights_kernel(p_ref, o_ref):
    a = lax.broadcasted_iota(jnp.int32, (B, 128), 0)
    lane = lax.broadcasted_iota(jnp.int32, (B, 128), 1)
    place = (a % 6) * 8 + a // 6
    first = (lane == place).astype(f32).astype(bf)
    second = (lane == place + B).astype(f32).astype(bf)
    o_ref[:, 2 * B:, :] = jnp.zeros((R, 128 - 2 * B, 128), bf)
    def body(i, c):
        p = p_ref[i]
        o_ref[i, :B, :] = jnp.dot(p, first, preferred_element_type=f32).astype(bf)
        o_ref[i, B:2 * B, :] = jnp.dot(p, second, preferred_element_type=f32).astype(bf)
        return c
    lax.fori_loop(0, R, body, 0, unroll=4)

def weights(p):
    return pl.pallas_call(weights_kernel, out_shape=jax.ShapeDtypeStruct((R, 128, 128), bf))(p)

BLK = HALF // 128

def sum_kernel(x_ref, o_ref, buf):
    def body(b, c):
        at = pl.multiple_of(b * 128, 128)
        s = x_ref[0, :, pl.ds(at, 128)].astype(f32)
        for y in range(1, 4):
            s = s + x_ref[y, :, pl.ds(at, 128)].astype(f32)
        for g in range(3):
            buf[pl.ds(g * BLK + b, 8, stride=256), :] = s[8 * g:8 * g + 8]
        return c
    lax.fori_loop(0, BLK, body, 0, unroll=3)
    for z in range(8):
        o_ref[z] = buf[z * 256:(z + 1) * 256, :].astype(bf)

def sum_y(x):
    return pl.pallas_call(sum_kernel, out_shape=jax.ShapeDtypeStruct((8, 256, 128), bf),
                          scratch_shapes=[pltpu.VMEM((8 * 256, 128), f32)])(x)

def final_kernel(par_ref, x_ref, o_ref, tot):
    tot[...] = functools.reduce(lambda p, q: p + q, [x_ref[z].astype(f32) for z in range(8)])
    odd = par_ref[0]
    acc = jnp.zeros((T, 128), f32)
    lane = lax.broadcasted_iota(jnp.int32, (KC, CR, 128), 2)
    agg = lax.broadcasted_iota(jnp.int32, (KC, CR, 128), 1)
    l0 = lax.broadcasted_iota(jnp.int32, (128, 128), 0)
    l1 = lax.broadcasted_iota(jnp.int32, (128, 128), 1)
    for w in range(3):
        mask = (lane + w * 128) // H == agg
        for g in range(3):
            place = jnp.where(odd == 1, (1, 0, 2)[g], (0, 2, 1)[g])
            pick = ((l0 + w * 128) % H + place * H == l1).astype(f32).astype(bf)
            x = tot[pl.ds(g * BLK + w, KC, stride=3), :]
            for _ in range(3):
                top = x.astype(bf).astype(f32)
                x = x - top
                wide = jnp.where(mask, jnp.broadcast_to(top[:, None, :], (KC, CR, 128)), 0.0).reshape(T, 128).astype(bf)
                acc = acc + jnp.dot(wide, pick, preferred_element_type=f32)
    o_ref[...] = acc[:, :72].reshape(KC, CR, 72)

def final(par, x):
    return pl.pallas_call(final_kernel, out_shape=jax.ShapeDtypeStruct((KC, CR, 72), f32),
                          in_specs=[pl.BlockSpec(memory_space=pltpu.SMEM), pl.BlockSpec(memory_space=pltpu.VMEM)],
                          scratch_shapes=[pltpu.VMEM((256, 128), f32)])(par, x)

YG = [[z * 4 + y for y in range(4)] for z in range(8)]
ZG = [[z * 4 + y for z in range(8)] for y in range(4)]

def shards(blocks, prolong, columns, aggregate, slots):
    packed = pack(prolong)
    tile = lax.all_gather(packed, "row", axis=0, tiled=True)
    part = main(columns.T, slots.T, aggregate, blocks, weights(prolong), tile)
    part = lax.all_to_all(part, "col", 0, 0, axis_index_groups=YG, tiled=True)
    part = sum_y(part)
    part = lax.all_to_all(part, "col", 0, 0, axis_index_groups=ZG, tiled=True)
    odd = lax.axis_index("col") & 1
    return final(odd.reshape(1), part).transpose(1, 0, 2)


def solution(mesh):
    return jax.shard_map(
        shards,
        mesh=mesh,
        in_specs=(
            jax.sharding.PartitionSpec(("row", "col"), None, None, None),
            jax.sharding.PartitionSpec(("row", "col"), None, None),
            jax.sharding.PartitionSpec(("row", "col"), None),
            jax.sharding.PartitionSpec(("row", "col")),
            jax.sharding.PartitionSpec(("row", "col"), None),
        ),
        out_specs=jax.sharding.PartitionSpec("row", None, "col"),
        check_vma=False,
    )
```

time: 374 us -> 156 us (0.42)
  waiting for transfers between devices: 206 us -> 41.6 us
  local copies, waits for them, and re-layouts: 97.1 us -> 0.79 us
  Pallas kernels: 0 us -> 61.6 us
  blocking collectives: 0 us -> 30.4 us
  matrix products: 27.9 us -> 0 us
  other arithmetic: 27.1 us -> 0 us
  starting transfers between devices: 0.04 us -> 6.98 us
    psum x1 -> x0, waiting for transfers between devices: 168 us -> none  [shards(): summed = lax.psum(partial_value, 'col')]
    pallas_call x0 -> x5, Pallas kernels: none -> 61.6 us  [the longest x1 48.2 us: main(): pl.pallas_call(functools.partial(main_kernel, G), out_shape=jax.ShapeDtyp...]
    transpose x1 -> x0, local copies, waits for them, and re-layouts: 32.6 us -> none  [shards(): jnp.einsum('rba,rkbc->rkac', prolong, product, preferred_element_type=jnp...]
    gather x2 -> x0, local copies, waits for them, and re-layouts: 32.4 us -> none  [shards(): picked = jnp.take(tile, columns, axis=0)]
    all_to_all x0 -> x1, blocking collectives: none -> 30.4 us  [shards(): part = lax.all_to_all(part, 'col', 0, 0, axis_index_groups=YG, tiled=True)]
    reshape x2 -> x0, local copies, waits for them, and re-layouts: 29.6 us -> none  [the longest x1 25.7 us: shards(): term.reshape(-1, width * width)]
    dot_general x1 -> x0, matrix products: 27.9 us -> none  [shards(): jnp.einsum('rba,rkbc->rkac', prolong, product, preferred_element_type=jnp...]
    scatter-add x1 -> x0, other arithmetic: 24.2 us -> none  [shards(): jax.ops.segment_sum(term.reshape(-1, width * width), target, num_segments...]
  transfers between devices with their start and end apart: 2 -> 2, of which waited for: 2 -> 2; matrix products, arithmetic and copies ran while one was open for 1% -> 0% of each run, Pallas kernels for 0% -> 3%
where the time goes in v1:
time: 156 us; the launch traced here: 155 us
  Pallas kernels  61.6 us (39%)
  waiting for transfers between devices  41.6 us (27%)
  blocking collectives  30.4 us (19%)
  between operations  13.4 us (9%)
  starting transfers between devices  6.98 us (4%)
    pallas_call x1, Pallas kernels, main(): pl.pallas_call(functools.partial(main_kernel, G), out_shape=jax.ShapeDtyp...  48.2 us
    all_to_all x1, blocking collectives, shards(): part = lax.all_to_all(part, 'col', 0, 0, axis_index_groups=YG, tiled=True)  30.4 us
    all_gather x1, waiting for transfers between devices, shards(): tile = lax.all_gather(packed, 'row', axis=0, tiled=True)  24.8 us
    all_to_all x1, waiting for transfers between devices, shards(): part = lax.all_to_all(part, 'col', 0, 0, axis_index_groups=ZG, tiled=True)  16.8 us
    all_to_all x1, starting transfers between devices, shards(): part = lax.all_to_all(part, 'col', 0, 0, axis_index_groups=ZG, tiled=True)  6.98 us
    pallas_call x1, Pallas kernels, weights(): pl.pallas_call(weights_kernel, out_shape=jax.ShapeDtypeStruct((R, 128, 12...  4.49 us
    pallas_call x1, Pallas kernels, final(): pl.pallas_call(final_kernel, out_shape=jax.ShapeDtypeStruct((KC, CR, 72),...  3.5 us
    pallas_call x1, Pallas kernels, sum_y(): pl.pallas_call(sum_kernel, out_shape=jax.ShapeDtypeStruct((8, 256, 128),...  3.19 us
  transfers between devices with their start and end apart: 2, of which 2 were waited for; matrix products, arithmetic and copies ran while one was open for 0% of the time, Pallas kernels for 3%

profile of v1, /device:TPU:2, one launch (start us, length us, event | category | flops | bytes accessed | tf_op | source)
XLA Modules:
  0.0 154.7 jit_solution(865148802585847907)
XLA Ops:
  6.5 0.0 all-gather.2.cloned.1.call-start
  6.5 2.1 %shard_map.56 = bf16[288,384]{1,0:T(8,128)(2,1)} custom-call(bf16[48,48,48]{2,1,0:T(8,128)(2,1)} %p_ref.3), custom_call_target="tpu_custom_call" | custom-call | tf_op jit(solution)/shard_map/pallas_call | solution.py:20
  8.7 0.0 all-gather.2.cloned.1.call-update
  8.7 4.5 %shard_map.55.pro = bf16[48,128,128]{2,1,0:T(8,128)(2,1)} custom-call(bf16[48,48,48]{2,1,0:T(8,128)(2,1)} %p_ref.3), custom_call_target="tpu_custom_call" | custom-call | tf_op jit(solution)/shard_map/pallas_call | solution.py:148
  13.2 24.8 %all-gather.2.cloned.1.call-done.pg = bf16[2304,384]{1,0:T(8,128)(2,1)} async-done(((bf16[288,384]{1,0:T(8,128)(2,1)}), bf16[2304,384]{1,0:T(8,128)(2,1)}) %all-gather.2.cloned.1.call-update) | async-done | bytes 1769488 | tf_op jit(solution)/shard_map/all_gather | solution.py:200
  37.9 48.2 %shard_map.57 = bf16[4,24,10368]{2,1,0:T(8,128)(2,1)} custom-call(s32[27,48]{1,0:T(8,128)} %bitcast.4, s32[27,48]{1,0:T(8,128)} %bitcast.5, s32[48]{0:T(128)} %agg.1, bf16[48,27,48,48]{3,2,1,0:T(8,128)(2,1)} %blk_hbm.1, bf16[48,128,128]{2,1,0:T(8,128)(2,1)} %shard_map.55.pro, bf16[2304,384]{1,0:T(8,128)(2,1)} %all-gather.2.cloned.1.call-done.pg), custom_call_target="tpu_custom_call" | custom-call | tf_op jit(solution)/shard_map/pallas_call | solution.py:123
  86.2 30.4 %all_to_all.10.x_ref = bf16[4,24,10368]{2,1,0:T(8,128)(2,1)} all-to-all(bf16[4,24,10368]{2,1,0:T(8,128)(2,1)} %shard_map.57), channel_id=1, replica_groups={{0,1,2,3},{4,5,6,7},{8,9,10,11},{12,13,14,15},{16,17,18,19},{20,21,22,2..., dimensions={0} | all-to-all | bytes 3981312 | tf_op jit(solution)/shard_map/all_to_all | solution.py:202
  116.6 3.2 %shard_map.58 = bf16[8,256,128]{2,1,0:T(8,128)(2,1)} custom-call(bf16[4,24,10368]{2,1,0:T(8,128)(2,1)} %all_to_all.10.x_ref), custom_call_target="tpu_custom_call" | custom-call | tf_op jit(solution)/shard_map/pallas_call | solution.py:166
  119.8 7.0 %all-to-all-start.1 = ((bf16[8,256,128]{2,1,0:T(8,128)(2,1)}), bf16[8,256,128]{2,1,0:T(8,128)(2,1)S(1)}, u32[]{:S(2)}, u32[]{:S(2)}) async-start(bf16[8,256,128]{2,1,0:T(8,128)(2,1)} %shard_map.58), calls=%async_computation.1 | async-start | bytes 1048576 | tf_op jit(solution)/shard_map/all_to_all | solution.py:204
  126.7 16.8 %all-to-all-done.1.x_ref = bf16[8,256,128]{2,1,0:T(8,128)(2,1)S(1)} async-done(((bf16[8,256,128]{2,1,0:T(8,128)(2,1)}), bf16[8,256,128]{2,1,0:T(8,128)(2,1)S(1)}, u32[]{:S(2)}, u32[]{:S(2)}) %all-to-all-start.1) | async-done | bytes 524320 | tf_op jit(solution)/shard_map/all_to_all | solution.py:204
  143.6 0.0 copy-start
  143.6 0.8 copy-done
  144.3 3.5 %shard_map.59 = f32[27,16,72]{2,1,0:T(8,128)} custom-call(s32[1]{0:T(128)} %bitcast.par_ref, bf16[8,256,128]{2,1,0:T(8,128)(2,1)} %copy-done), custom_call_target="tpu_custom_call" | custom-call | tf_op jit(solution)/shard_map/pallas_call | solution.py:191
Async XLA Ops:
  6.5 31.4 %all-gather.2.cloned.1.call-start = ((), (), s32[]{:S(2)}) async-start(), calls=%async_computation.2 | async-start | bytes 1990656 | tf_op jit(solution)/shard_map/all_gather | solution.py:200
  119.8 23.8 %all-to-all-start.1 = ((bf16[8,256,128]{2,1,0:T(8,128)(2,1)}), bf16[8,256,128]{2,1,0:T(8,128)(2,1)S(1)}, u32[]{:S(2)}, u32[]{:S(2)}) async-start(bf16[8,256,128]{2,1,0:T(8,128)(2,1)} %shard_map.58), calls=%async_computation.1 | async-start | bytes 1048576 | tf_op jit(solution)/shard_map/all_to_all | solution.py:204
  143.6 0.8 copy-start
Sparse Core Ops, SparseCore 0:
  9.2 28.7 all-gather.1

commit v2 on v1

--- a/solution.py
+++ b/solution.py
@@ -9,62 +9,65 @@
 H = B // 2
 HALF = T * H
 PAIRS = (K + 1) // 2
+PIECE = R // 2 * B
 PLACES = [[(0, 0), (0, 1), (1, 0)], [(0, 2), (1, 1), (1, 2)], [(0, 3), (0, 4), (1, 3)], [(0, 5), (1, 4), (1, 5)]]
 
 def pack_kernel(p_ref, o_ref):
-    for g in range(R // 8):
-        o_ref[g * B:(g + 1) * B, :] = jnp.concatenate(
-            [p_ref[8 * g + m].astype(f32).T for m in range(8)], axis=1).astype(bf)
+    pad = jnp.zeros((B, 128 - 2 * B), f32)
+    for n in range(R // 2):
+        two = [p_ref[2 * n + m].astype(f32).T for m in range(2)]
+        o_ref[n * B:(n + 1) * B, :] = jnp.concatenate(two + [pad], axis=1).astype(bf)
 
 def pack(p):
-    return pl.pallas_call(pack_kernel, out_shape=jax.ShapeDtypeStruct((R // 8 * B, 8 * B), bf))(p)
-
-def main_kernel(G, cols, slots, agg, blk_hbm, pro, pg, out, blk, plo, phi, alo, ahi, bufa, bufb, ta, tb, sems):
+    return pl.pallas_call(pack_kernel, out_shape=jax.ShapeDtypeStruct((PIECE, 128), bf))(p)
+
+def main_kernel(G, opt, cols, slots, agg, blk_hbm, pro_hbm, *rest):
+    pieces, (out, blk, pro, tile, alo, ahi, bufa, bufb, ta, tb, sems, psems) = rest[:-12], rest[-12:]
     CH = 4
     def copy(n):
         return pltpu.make_async_copy(blk_hbm.at[pl.ds(n * CH, CH)], blk.at[pl.ds(n * CH, CH)], sems.at[n])
+    first = []
+    rows0 = 0
+    for n, piece in enumerate(pieces):
+        size = piece.shape[0]
+        first.append(pltpu.make_async_copy(piece, tile.at[pl.ds(rows0, size)], psems.at[n]))
+        rows0 += size
+    first.append(pltpu.make_async_copy(pro_hbm, pro, psems.at[len(pieces)]))
+    for c in first:
+        c.start()
     for n in range(R // CH):
         copy(n).start()
-    if True:
-        for m in range(8):
-            first = (48 * m // 128) * 128
-            wide = min(256, 384 - first)
-            row = lax.broadcasted_iota(jnp.int32, (wide, 256), 0) + first - 48 * m
-            lane = lax.broadcasted_iota(jnp.int32, (wide, 256), 1)
-            inside = (row >= 0) & (row < 48)
-            pick = (inside & ((lane == row) | (lane == row + 128 + 48))).astype(f32).astype(bf)
-            def unpack(n, c):
-                x = pg[pl.ds(pl.multiple_of(n * 192, 192), 192), first:first + wide]
-                y = jnp.dot(x, pick, preferred_element_type=f32).astype(bf)
-                at = pl.multiple_of(m * 48 * B + n * 192, 192)
-                plo[pl.ds(at, 192), :] = y[:, :128]
-                phi[pl.ds(at, 192), :] = y[:, 128:]
-                z = pl.multiple_of((m * 12 + n) * 216, 8)
-                alo[pl.ds(z, 216), :] = jnp.zeros((216, 128), f32)
-                ahi[pl.ds(z, 216), :] = jnp.zeros((216, 128), f32)
-                return c
-            lax.fori_loop(0, 12, unpack, 0)
-
-    bufa[:, 96:] = jnp.zeros((PAIRS * B, 32), bf)
-    bufb[:, 96:] = jnp.zeros((PAIRS * B, 32), bf)
+
+    def zero(n, c):
+        z = pl.multiple_of(n * 648, 8)
+        alo[pl.ds(z, 648), :] = jnp.zeros((648, 128), f32)
+        ahi[pl.ds(z, 648), :] = jnp.zeros((648, 128), f32)
+        return c
+    if 'noinit' not in opt:
+        lax.fori_loop(0, 32, zero, 0)
+
+    bufa[...] = jnp.zeros((PAIRS * B, 128), bf)
+    bufb[...] = jnp.zeros((PAIRS * B, 128), bf)
+
+    lane = lax.broadcasted_iota(jnp.int32, (B, 128), 1)
 
     def phase1(i, n, buf):
-        two = range(2 * n, min(2 * n + 2, K))
-        at = []
-        for k in two:
+        lhs, rhs = [], []
+        for k in range(2 * n, min(2 * n + 2, K)):
             j = cols[k, i]
-            at.append(pl.multiple_of(((j & 7) * 48 + (j >> 3)) * B, B))
-        lhs = plo[pl.ds(at[0], B), :]
-        zero = jnp.zeros((B, B), bf)
-        if len(two) == 2:
-            lhs = lhs + phi[pl.ds(at[1], B), :]
-            w = jnp.concatenate([jnp.concatenate([blk[i, two[0]], zero], axis=1),
-                                 jnp.concatenate([zero, blk[i, two[1]]], axis=1)], axis=0)
-            p = lax.dot_general(lhs[:, :96], w, (((1,), (1,)), ((), ())), preferred_element_type=f32)
+            lhs.append(tile[pl.ds(pl.multiple_of((j >> 1) * B, B), B), :])
+            a = blk[i, k]
+            a = jnp.concatenate([a, a, jnp.zeros((B, 128 - 2 * B), bf)], axis=1)
+            odd = j & 1
+            rhs.append(jnp.where((lane >= B * odd) & (lane < B * odd + B), a, jnp.zeros((B, 128), bf)))
+        if len(lhs) == 2:
+            zero = jnp.zeros((B, 128), bf)
+            w = jnp.concatenate([jnp.concatenate([rhs[0], zero], axis=1), jnp.concatenate([zero, rhs[1]], axis=1)], axis=0)
+            p = lax.dot_general(jnp.concatenate(lhs, axis=1), w, (((1,), (1,)), ((), ())), preferred_element_type=f32)
+            buf[n * B:(n + 1) * B, :96] = p.astype(bf)
         else:
-            w = jnp.concatenate([jnp.concatenate([blk[i, two[0]], zero], axis=1), jnp.zeros((B, 2 * B), bf)], axis=0)
-            p = lax.dot_general(lhs[:, :96], w, (((1,), (1,)), ((), ())), preferred_element_type=f32)
-        buf[n * B:(n + 1) * B, :96] = p.astype(bf)
+            p = lax.dot_general(lhs[0], rhs[0], (((1,), (1,)), ((), ())), preferred_element_type=f32)
+            buf[n * B:(n + 1) * B, :48] = p.astype(bf)
 
     def phase2(w, n, buf, tbuf):
         tbuf[n * B:(n + G) * B, :] = jnp.dot(buf[n * B:(n + G) * B, :], w, preferred_element_type=f32)
@@ -80,14 +83,16 @@
         w = pro[i2]
         base = agg[i2]
         for n in range(PAIRS):
-            if n % G == 0:
+            if 'nop2' not in opt and n % G == 0:
                 phase2(w, n, buf2, tbuf)
-            if True:
+            if 'nop1' not in opt:
                 phase1(i1, n, buf1)
-            if True:
+            if 'noacc' not in opt:
                 add(i2, base, n, tbuf)
 
     if True:
+        for c in first:
+            c.wait()
         copy(0).wait()
         for n in range(PAIRS):
             phase1(0, n, bufa)
@@ -99,7 +104,8 @@
                 copy((q + 1) // 2).wait()
             both(jnp.minimum(2 * q + 2, R - 1), bufa, 2 * q + 1, bufb, tb)
             return c
-        lax.fori_loop(0, R // 2, rows, 0)
+        if 'norows' not in opt:
+            lax.fori_loop(0, R // 2, rows, 0)
     else:
         for n in range(R // CH):
             copy(n).wait()
@@ -117,18 +123,20 @@
                 rows = [halves[h][8 * u:8 * u + 8] for h, u in PLACES[y]]
                 out[y, :, pl.ds(at, 128)] = jnp.concatenate(rows, axis=0).astype(bf)
             return c
-        lax.fori_loop(0, HALF // 128, flush, 0)
-
-def main(colsT, slotsT, agg, blocks, wide, pg, G=14):
+        lax.fori_loop(0, HALF // 128 if 'noflush' not in opt else 1, flush, 0)
+
+def main(colsT, slotsT, agg, blocks, wide, pieces, G=14, opt=()):
+    hbm = pl.BlockSpec(memory_space=pl.ANY)
     return pl.pallas_call(
-        functools.partial(main_kernel, G),
+        functools.partial(main_kernel, G, opt),
         out_shape=jax.ShapeDtypeStruct((4, 24, HALF), bf),
-        in_specs=[pl.BlockSpec(memory_space=pltpu.SMEM)] * 3 + [pl.BlockSpec(memory_space=pl.ANY)] + [pl.BlockSpec(memory_space=pltpu.VMEM)] * 2,
+        in_specs=[pl.BlockSpec(memory_space=pltpu.SMEM)] * 3 + [hbm] * (2 + len(pieces)),
         out_specs=pl.BlockSpec(memory_space=pltpu.VMEM),
-        scratch_shapes=[pltpu.VMEM((R, K, B, B), bf)] + [pltpu.VMEM((384 * B, 128), bf)] * 2 + [pltpu.VMEM((2 * HALF, 128), f32)] * 2
-            + [pltpu.VMEM((PAIRS * B, 128), bf)] * 2 + [pltpu.VMEM((PAIRS * B, 128), f32)] * 2 + [pltpu.SemaphoreType.DMA((12,))],
+        scratch_shapes=[pltpu.VMEM((R, K, B, B), bf), pltpu.VMEM((R, 128, 128), bf), pltpu.VMEM((8 * PIECE, 128), bf)]
+            + [pltpu.VMEM((2 * HALF, 128), f32)] * 2 + [pltpu.VMEM((PAIRS * B, 128), bf)] * 2
+            + [pltpu.VMEM((PAIRS * B, 128), f32)] * 2 + [pltpu.SemaphoreType.DMA((12,)), pltpu.SemaphoreType.DMA((len(pieces) + 1,))],
         compiler_params=pltpu.CompilerParams(vmem_limit_bytes=63 << 20),
-    )(colsT, slotsT, agg, blocks, wide, pg)
+    )(colsT, slotsT, agg, blocks, wide, *pieces)
 
 def weights_kernel(p_ref, o_ref):
     a = lax.broadcasted_iota(jnp.int32, (B, 128), 0)
@@ -195,10 +203,27 @@
 YG = [[z * 4 + y for y in range(4)] for z in range(8)]
 ZG = [[z * 4 + y for z in range(8)] for y in range(4)]
 
+def gather(p):
+    def along(x, by):
+        return lax.ppermute(x, "row", [(i, (i + 2 * by) % 8) for i in range(8)])
+    def across(x):
+        return lax.ppermute(x, "row", [(i, i ^ 1) for i in range(8)])
+    half = PIECE // 2
+    left, right = along(p, 1), along(p, -1)
+    far = [along(left[:half], 1), along(right[half:], -1)]
+    mine = [p, right, left] + far
+    return mine + [across(q) for q in mine]
+
+def places(columns):
+    row = lax.axis_index("row")
+    owner = columns // R
+    apart = (owner // 2 - row // 2) & 3
+    at = jnp.where(apart == 3, 2, jnp.where(apart == 2, 3, apart)) + 4 * ((owner ^ row) & 1)
+    return at * R + columns % R
+
 def shards(blocks, prolong, columns, aggregate, slots):
-    packed = pack(prolong)
-    tile = lax.all_gather(packed, "row", axis=0, tiled=True)
-    part = main(columns.T, slots.T, aggregate, blocks, weights(prolong), tile)
+    pieces = gather(pack(prolong))
+    part = main(places(columns).T, slots.T, aggregate, blocks, weights(prolong), pieces)
     part = lax.all_to_all(part, "col", 0, 0, axis_index_groups=YG, tiled=True)
     part = sum_y(part)
     part = lax.all_to_all(part, "col", 0, 0, axis_index_groups=ZG, tiled=True)

time: 156 us -> 126 us (0.81)
  waiting for transfers between devices: 41.6 us -> 24.2 us
  between operations: 13.4 us -> 0.05 us
  Pallas kernels: 61.6 us -> 52.5 us
  starting transfers between devices: 6.98 us -> 14 us
    all_gather x1 -> x0, waiting for transfers between devices: 24.8 us -> none  [shards(): tile = lax.all_gather(packed, 'row', axis=0, tiled=True)]
    pallas_call x2, Pallas kernels: 50.4 us -> 41.3 us  [the longest x1 39.1 us: main(): pl.pallas_call(functools.partial(main_kernel, G, opt), out_shape=jax.Shap...]
    ppermute x0 -> x9, waiting for transfers between devices: none -> 7.31 us  [the longest x4 6.69 us: along(): return lax.ppermute(x, 'row', [(i, (i + 2 * by) % 8) for i in range(8)])]
    ppermute x0 -> x9, starting transfers between devices: none -> 5.58 us  [the longest x4 4.45 us: along(): return lax.ppermute(x, 'row', [(i, (i + 2 * by) % 8) for i in range(8)])]
  transfers between devices with their start and end apart: 2 -> 10, of which waited for: 2 -> 4; matrix products, arithmetic and copies ran while one was open for 0% -> 1% of each run, Pallas kernels for 3% -> 4%
where the time goes in v2:
time: 126 us; the launch traced here: 124 us
  Pallas kernels  52.5 us (42%)
  blocking collectives  30.4 us (24%)
  waiting for transfers between devices  24.2 us (19%)
  starting transfers between devices  14 us (11%)
  local copies, waits for them, and re-layouts  2.19 us (2%)
    pallas_call x1, Pallas kernels, main(): pl.pallas_call(functools.partial(main_kernel, G, opt), out_shape=jax.Shap...  39.1 us
    all_to_all x1, blocking collectives, shards(): part = lax.all_to_all(part, 'col', 0, 0, axis_index_groups=YG, tiled=True)  30.4 us
    all_to_all x1, waiting for transfers between devices, shards(): part = lax.all_to_all(part, 'col', 0, 0, axis_index_groups=ZG, tiled=True)  16.9 us
    all_to_all x1, starting transfers between devices, shards(): part = lax.all_to_all(part, 'col', 0, 0, axis_index_groups=ZG, tiled=True)  8.45 us
    ppermute x4, waiting for transfers between devices, along(): return lax.ppermute(x, 'row', [(i, (i + 2 * by) % 8) for i in range(8)])  6.69 us
    pallas_call x1, Pallas kernels, weights(): pl.pallas_call(weights_kernel, out_shape=jax.ShapeDtypeStruct((R, 128, 12...  4.5 us
    ppermute x4, starting transfers between devices, along(): return lax.ppermute(x, 'row', [(i, (i + 2 * by) % 8) for i in range(8)])  4.45 us
    pallas_call x1, Pallas kernels, final(): pl.pallas_call(final_kernel, out_shape=jax.ShapeDtypeStruct((KC, CR, 72),...  3.5 us
  transfers between devices with their start and end apart: 10, of which 4 were waited for; matrix products, arithmetic and copies ran while one was open for 1% of the time, Pallas kernels for 4%

profile of v2, /device:TPU:2, one launch (start us, length us, event | category | flops | bytes accessed | tf_op | source)
XLA Modules:
  0.0 124.0 jit_solution(2446861243207567705)
XLA Ops:
  0.0 2.1 %shard_map.56.rest_0_ = bf16[1152,128]{1,0:T(8,128)(2,1)} custom-call(bf16[48,48,48]{2,1,0:T(8,128)(2,1)} %p_ref.3), custom_call_target="tpu_custom_call" | custom-call | tf_op jit(solution)/shard_map/pallas_call | solution.py:22
  2.1 1.5 %collective-permute-start.1 = (bf16[1152,128]{1,0:T(8,128)(2,1)}, bf16[1152,128]{1,0:T(8,128)(2,1)S(1)}, u32[]{:S(2)}, u32[]{:S(2)}) collective-permute-start(bf16[1152,128]{1,0:T(8,128)(2,1)} %shard_map.56.rest_0_), channel_id=1, source_target_pairs={{0,64},{32,96},{64,128},{96,160},{128,192},{160,224},{192,0},{224,... | collective-permute-start | bytes 884744 | tf_op jit(solution)/shard_map/ppermute | solution.py:208
  3.6 0.8 collective-permute-start
  4.4 6.7 %collective-permute-done.1.rest_2_ = bf16[1152,128]{1,0:T(8,128)(2,1)S(1)} collective-permute-done((bf16[1152,128]{1,0:T(8,128)(2,1)}, bf16[1152,128]{1,0:T(8,128)(2,1)S(1)}, u32[]{:S(2)}, u32[]{:S(2)}) %collective-permute-start.1) | collective-permute-done | bytes 294944 | tf_op jit(solution)/shard_map/ppermute | solution.py:208
  11.1 1.6 %collective-permute-start.2 = (bf16[576,128]{1,0:T(8,128)(2,1)S(1)}, bf16[576,128]{1,0:T(8,128)(2,1)S(1)}, u32[]{:S(2)}, u32[]{:S(2)}) collective-permute-start(bf16[576,128]{1,0:T(8,128)(2,1)S(1)} %slice.8), channel_id=1, source_target_pairs={{0,64},{32,96},{64,128},{96,160},{128,192},{160,224},{192,0},{224,... | collective-permute-start | bytes 442376 | tf_op jit(solution)/shard_map/ppermute | solution.py:208
  12.7 0.0 collective-permute-done.rest_1_
  12.7 0.6 collective-permute-start.3
  13.3 0.0 collective-permute-start.4
  13.3 0.5 collective-permute-start.6
  13.8 0.0 collective-permute-start.5
  13.8 4.5 %shard_map.55.pro_hbm = bf16[48,128,128]{2,1,0:T(8,128)(2,1)} custom-call(bf16[48,48,48]{2,1,0:T(8,128)(2,1)} %p_ref.3), custom_call_target="tpu_custom_call" | custom-call | tf_op jit(solution)/shard_map/pallas_call | solution.py:156
  18.3 0.0 collective-permute-done.2.rest_3_
  18.3 0.5 collective-permute-start.7
  18.9 0.0 collective-permute-done.3.rest_4_
  18.9 0.1 collective-permute-start.8
  19.0 0.6 fusion.4.cols
  19.6 0.0 collective-permute-done.4.rest_5_
  19.6 0.2 collective-permute-done.7.rest_8_
  19.9 0.0 collective-permute-done.6.rest_7_
  19.9 0.4 collective-permute-done.8.rest_9_
  20.2 0.0 collective-permute-done.5.rest_6_
  20.2 0.3 copy-done.8
  20.5 0.1 copy-done.4
  20.6 0.3 copy-done.9
  20.9 0.7 copy-done.5
  21.6 39.1 %shard_map.57 = bf16[4,24,10368]{2,1,0:T(8,128)(2,1)} custom-call(s32[27,48]{1,0:T(8,128)} %fusion.4.cols, s32[27,48]{1,0:T(8,128)} %bitcast.5, s32[48]{0:T(128)} %agg.1, bf16[48,27,48,48]{3,2,1,0:T(8,128)(2,1)} %blk_hbm.1, bf16[48,128,128]{2,1,0:T(8,128)(2,1)} %shard_map.55.pro_hbm, bf16[1152,128]{1,0:T(8,128)(2,1)} %shard_map.56.rest_0_, ...), custom_call_target="tpu_custom_call" | custom-call | tf_op jit(solution)/shard_map/pallas_call | solution.py:130
  60.8 30.4 %all_to_all.10.x_ref = bf16[4,24,10368]{2,1,0:T(8,128)(2,1)} all-to-all(bf16[4,24,10368]{2,1,0:T(8,128)(2,1)} %shard_map.57), channel_id=1, replica_groups={{0,1,2,3},{4,5,6,7},{8,9,10,11},{12,13,14,15},{16,17,18,19},{20,21,22,2..., dimensions={0} | all-to-all | bytes 3981312 | tf_op jit(solution)/shard_map/all_to_all | solution.py:227
  91.1 3.2 %shard_map.58 = bf16[8,256,128]{2,1,0:T(8,128)(2,1)} custom-call(bf16[4,24,10368]{2,1,0:T(8,128)(2,1)} %all_to_all.10.x_ref), custom_call_target="tpu_custom_call" | custom-call | tf_op jit(solution)/shard_map/pallas_call | solution.py:174
  94.3 8.4 %all-to-all-start.1 = ((bf16[8,256,128]{2,1,0:T(8,128)(2,1)}), bf16[8,256,128]{2,1,0:T(8,128)(2,1)S(1)}, u32[]{:S(2)}, u32[]{:S(2)}) async-start(bf16[8,256,128]{2,1,0:T(8,128)(2,1)} %shard_map.58), calls=%async_computation.1 | async-start | bytes 1048576 | tf_op jit(solution)/shard_map/all_to_all | solution.py:229
  102.8 16.9 %all-to-all-done.1.x_ref = bf16[8,256,128]{2,1,0:T(8,128)(2,1)S(1)} async-done(((bf16[8,256,128]{2,1,0:T(8,128)(2,1)}), bf16[8,256,128]{2,1,0:T(8,128)(2,1)S(1)}, u32[]{:S(2)}, u32[]{:S(2)}) %all-to-all-start.1) | async-done | bytes 524320 | tf_op jit(solution)/shard_map/all_to_all | solution.py:229
  119.7 0.8 copy-done
  120.5 3.5 %shard_map.59 = f32[27,16,72]{2,1,0:T(8,128)} custom-call(s32[1]{0:T(128)} %bitcast.par_ref, bf16[8,256,128]{2,1,0:T(8,128)(2,1)} %copy-done), custom_call_target="tpu_custom_call" | custom-call | tf_op jit(solution)/shard_map/pallas_call | solution.py:199
  (19 shorter events, 0.1 us)
Async XLA Ops:
  0.0 19.0 %copy-start.10 = (s32[48,27]{0,1:T(8,128)S(1)}, s32[48,27]{0,1:T(8,128)}, u32[]{:S(2)}) copy-start(s32[48,27]{0,1:T(8,128)} %param.7) | copy-start | bytes 15556
  2.1 9.0 %collective-permute-start.1 = (bf16[1152,128]{1,0:T(8,128)(2,1)}, bf16[1152,128]{1,0:T(8,128)(2,1)S(1)}, u32[]{:S(2)}, u32[]{:S(2)}) collective-permute-start(bf16[1152,128]{1,0:T(8,128)(2,1)} %shard_map.56.rest_0_), channel_id=1, source_target_pairs={{0,64},{32,96},{64,128},{96,160},{128,192},{160,224},{192,0},{224,... | collective-permute-start | bytes 884744 | tf_op jit(solution)/shard_map/ppermute | solution.py:208
  3.6 9.1 %collective-permute-start = (bf16[1152,128]{1,0:T(8,128)(2,1)}, bf16[1152,128]{1,0:T(8,128)(2,1)S(1)}, u32[]{:S(2)}, u32[]{:S(2)}) collective-permute-start(bf16[1152,128]{1,0:T(8,128)(2,1)} %shard_map.56.rest_0_), channel_id=1, source_target_pairs={{0,192},{32,224},{64,0},{96,32},{128,64},{160,96},{192,128},{224,1... | collective-permute-start | bytes 884744 | tf_op jit(solution)/shard_map/ppermute | solution.py:208
  11.1 10.5 %copy-start.1 = (bf16[1152,128]{1,0:T(8,128)(2,1)}, bf16[1152,128]{1,0:T(8,128)(2,1)S(1)}, u32[]{:S(2)}) copy-start(bf16[1152,128]{1,0:T(8,128)(2,1)S(1)} %collective-permute-done.1.rest_2_) | copy-start | bytes 884740
  11.1 7.2 %collective-permute-start.2 = (bf16[576,128]{1,0:T(8,128)(2,1)S(1)}, bf16[576,128]{1,0:T(8,128)(2,1)S(1)}, u32[]{:S(2)}, u32[]{:S(2)}) collective-permute-start(bf16[576,128]{1,0:T(8,128)(2,1)S(1)} %slice.8), channel_id=1, source_target_pairs={{0,64},{32,96},{64,128},{96,160},{128,192},{160,224},{192,0},{224,... | collective-permute-start | bytes 442376 | tf_op jit(solution)/shard_map/ppermute | solution.py:208
  12.7 8.9 %copy-start.2 = (bf16[1152,128]{1,0:T(8,128)(2,1)}, bf16[1152,128]{1,0:T(8,128)(2,1)S(1)}, u32[]{:S(2)}) copy-start(bf16[1152,128]{1,0:T(8,128)(2,1)S(1)} %collective-permute-done.rest_1_) | copy-start | bytes 884740
  12.7 6.1 %collective-permute-start.3 = (bf16[576,128]{1,0:T(8,128)(2,1)S(1)}, bf16[576,128]{1,0:T(8,128)(2,1)S(1)}, u32[]{:S(2)}, u32[]{:S(2)}) collective-permute-start(bf16[576,128]{1,0:T(8,128)(2,1)S(1)} %slice.9), channel_id=1, source_target_pairs={{0,192},{32,224},{64,0},{96,32},{128,64},{160,96},{192,128},{224,1... | collective-permute-start | bytes 442376 | tf_op jit(solution)/shard_map/ppermute | solution.py:208
  13.3 6.3 %collective-permute-start.4 = (bf16[1152,128]{1,0:T(8,128)(2,1)}, bf16[1152,128]{1,0:T(8,128)(2,1)S(1)}, u32[]{:S(2)}, u32[]{:S(2)}) collective-permute-start(bf16[1152,128]{1,0:T(8,128)(2,1)} %shard_map.56.rest_0_), channel_id=1, source_target_pairs={{0,32},{32,0},{64,96},{96,64},{128,160},{160,128},{192,224},{224,1... | collective-permute-start | bytes 884744 | tf_op jit(solution)/shard_map/ppermute | solution.py:210
  13.3 6.5 %collective-permute-start.6 = (bf16[1152,128]{1,0:T(8,128)(2,1)S(1)}, bf16[1152,128]{1,0:T(8,128)(2,1)S(1)}, u32[]{:S(2)}, u32[]{:S(2)}) collective-permute-start(bf16[1152,128]{1,0:T(8,128)(2,1)S(1)} %collective-permute-done.1.rest_2_), channel_id=1, source_target_pairs={{0,32},{32,0},{64,96},{96,64},{128,160},{160,128},{192,224},{224,1... | collective-permute-start | bytes 884744 | tf_op jit(solution)/shard_map/ppermute | solution.py:210
  13.8 6.4 %collective-permute-start.5 = (bf16[1152,128]{1,0:T(8,128)(2,1)S(1)}, bf16[1152,128]{1,0:T(8,128)(2,1)S(1)}, u32[]{:S(2)}, u32[]{:S(2)}) collective-permute-start(bf16[1152,128]{1,0:T(8,128)(2,1)S(1)} %collective-permute-done.rest_1_), channel_id=1, source_target_pairs={{0,32},{32,0},{64,96},{96,64},{128,160},{160,128},{192,224},{224,1... | collective-permute-start | bytes 884744 | tf_op jit(solution)/shard_map/ppermute | solution.py:210
  18.3 1.9 %copy-start.6 = (bf16[576,128]{1,0:T(8,128)(2,1)}, bf16[576,128]{1,0:T(8,128)(2,1)S(1)}, u32[]{:S(2)}) copy-start(bf16[576,128]{1,0:T(8,128)(2,1)S(1)} %collective-permute-done.2.rest_3_) | copy-start | bytes 442372
  18.3 1.5 %collective-permute-start.7 = (bf16[576,128]{1,0:T(8,128)(2,1)S(1)}, bf16[576,128]{1,0:T(8,128)(2,1)S(1)}, u32[]{:S(2)}, u32[]{:S(2)}) collective-permute-start(bf16[576,128]{1,0:T(8,128)(2,1)S(1)} %collective-permute-done.2.rest_3_), channel_id=1, source_target_pairs={{0,32},{32,0},{64,96},{96,64},{128,160},{160,128},{192,224},{224,1... | collective-permute-start | bytes 442376 | tf_op jit(solution)/shard_map/ppermute | solution.py:210
  18.9 1.4 %copy-start.7 = (bf16[576,128]{1,0:T(8,128)(2,1)}, bf16[576,128]{1,0:T(8,128)(2,1)S(1)}, u32[]{:S(2)}) copy-start(bf16[576,128]{1,0:T(8,128)(2,1)S(1)} %collective-permute-done.3.rest_4_) | copy-start | bytes 442372
  18.9 1.4 %collective-permute-start.8 = (bf16[576,128]{1,0:T(8,128)(2,1)S(1)}, bf16[576,128]{1,0:T(8,128)(2,1)S(1)}, u32[]{:S(2)}, u32[]{:S(2)}) collective-permute-start(bf16[576,128]{1,0:T(8,128)(2,1)S(1)} %collective-permute-done.3.rest_4_), channel_id=1, source_target_pairs={{0,32},{32,0},{64,96},{96,64},{128,160},{160,128},{192,224},{224,1... | collective-permute-start | bytes 442376 | tf_op jit(solution)/shard_map/ppermute | solution.py:210
  19.6 2.0 %copy-start.3 = (bf16[1152,128]{1,0:T(8,128)(2,1)}, bf16[1152,128]{1,0:T(8,128)(2,1)S(1)}, u32[]{:S(2)}) copy-start(bf16[1152,128]{1,0:T(8,128)(2,1)S(1)} %collective-permute-done.4.rest_5_) | copy-start | bytes 884740
  19.9 0.7 copy-start.8
  19.9 0.8 copy-start.4
  20.2 0.7 copy-start.9
  20.9 0.7 copy-start.5
  94.3 25.3 %all-to-all-start.1 = ((bf16[8,256,128]{2,1,0:T(8,128)(2,1)}), bf16[8,256,128]{2,1,0:T(8,128)(2,1)S(1)}, u32[]{:S(2)}, u32[]{:S(2)}) async-start(bf16[8,256,128]{2,1,0:T(8,128)(2,1)} %shard_map.58), calls=%async_computation.1 | async-start | bytes 1048576 | tf_op jit(solution)/shard_map/all_to_all | solution.py:229
  119.7 0.8 copy-start

commit v3 on v0

v3 whole, which is shorter than its diff:
```python
import functools
import jax, jax.numpy as jnp
from jax import lax
from jax.experimental import pallas as pl
from jax.experimental.pallas import tpu as pltpu
bf, f32 = jnp.bfloat16, jnp.float32
B, K, KC, CR, R = 48, 27, 27, 16, 48
PAIRS = (K + 1) // 2
PIECE = R // 2 * B
HALF = B // 2
TILE = 8 * PIECE
FULL = (0, 2, 3, 5)
SPLIT = ((1, 0), (1, 1), (4, 0), (4, 1))

def slots_of(chunks):
    rows = CR // chunks
    return rows, -(-KC * rows // 16) * 16 // rows

def pack_kernel(p_ref, o_ref):
    pad = jnp.zeros((B, 128 - 2 * B), bf)
    for n in range(R // 2):
        o_ref[n * B:(n + 1) * B, :] = jnp.concatenate([p_ref[2 * n], p_ref[2 * n + 1], pad], axis=1)

def pack(p):
    return pl.pallas_call(pack_kernel, out_shape=jax.ShapeDtypeStruct((PIECE, 128), bf))(p)

def turn_kernel(p_ref, o_ref):
    row = lax.broadcasted_iota(jnp.int32, (B, B), 0)
    a = lax.broadcasted_iota(jnp.int32, (B, B), 1)
    pick = (row == (a % 6) * 8 + a // 6).astype(f32).astype(bf)
    for i in range(R):
        o_ref[i] = lax.dot_general(pick, p_ref[i], (((1,), (1,)), ((), ())), preferred_element_type=f32).astype(bf)

def turn(p):
    return pl.pallas_call(turn_kernel, out_shape=jax.ShapeDtypeStruct((R, B, B), bf),
                          cost_estimate=pl.CostEstimate(flops=10**7, bytes_accessed=2 * 10**6, transcendentals=0))(p)

def place_kernel_matrix(n, step, off):
    row = lax.broadcasted_iota(jnp.int32, (n * 128, 384), 0)
    col = lax.broadcasted_iota(jnp.int32, (n * 128, 384), 1)
    t, c = col // step, col % step
    return (row == (t // 2) * 128 + (t % 2) * B + off + c).astype(f32).astype(bf)

def main_kernel(q, chunks, cols, slots, agg, here, blk_hbm, turned_hbm, *rest):
    keeps = q == 0 and chunks > 1
    outs = 5 if keeps else 4
    npieces = len(rest) - 15 - outs
    pieces, (*sends, ), (out, osems, blk, turned, tile, lo, hi, bufa, bufb, only, full_ref, half_ref, todo, sems, psems) = (
        rest[:npieces], rest[npieces:npieces + outs], rest[npieces + outs:])
    crows, kslots = slots_of(chunks)
    total = crows * kslots
    first = []
    at = 0
    for n, piece in enumerate(pieces):
        first.append(pltpu.make_async_copy(piece, tile.at[pl.ds(at, piece.shape[0])], psems.at[n]))
        at += piece.shape[0]
    first.append(pltpu.make_async_copy(turned_hbm, turned, psems.at[npieces]))
    for c in first:
        c.start()

    def copy(r):
        return pltpu.make_async_copy(blk_hbm.at[todo[r]], blk.at[r], sems.at[r])
    todo[0] = 0
    def collect(i, n):
        ours = (agg[i] // crows == q)
        @pl.when(ours)
        def _():
            todo[n] = i
            copy(n).start()
        return n + ours.astype(jnp.int32)
    count = lax.fori_loop(0, R, collect, 0)

    def zero(n, c):
        z = pl.multiple_of(n * B * 4, 8)
        lo[pl.ds(z, B * 4), :] = jnp.zeros((B * 4, 128), f32)
        hi[pl.ds(z, B * 4), :] = jnp.zeros((B * 4, 128), f32)
        return c
    lax.fori_loop(0, total // 8, zero, 0)
    lane = lax.broadcasted_iota(jnp.int32, (32, 128), 1)
    row = lax.broadcasted_iota(jnp.int32, (32, 128), 0)
    only[...] = ((lane >= B * (row // 16)) & (lane < B * (row // 16) + B)).astype(f32).astype(bf)
    full_ref[...] = place_kernel_matrix(4, B, 0)
    for h in range(2):
        half_ref[h] = place_kernel_matrix(8, HALF, h * HALF)
    for c in first:
        c.wait()

    if q == 0:
        l0 = lax.broadcasted_iota(jnp.int32, (128, 128), 0)
        l1 = lax.broadcasted_iota(jnp.int32, (128, 128), 1)
        change = ((l0 < 2 * B) & (l1 == jnp.where(l0 < B, l0 + B, l0 - B))).astype(f32).astype(bf)
        def swap(n, c):
            z = pl.multiple_of(n * 1152, 1152)
            tile[pl.ds(TILE + z, 1152), :] = jnp.dot(tile[pl.ds(z, 1152), :], change, preferred_element_type=f32).astype(bf)
            return c
        lax.fori_loop(0, TILE // 1152, swap, 0)
        if keeps:
            keep = pltpu.make_async_copy(tile.at[pl.ds(TILE, TILE)], sends[4], psems.at[0])
            keep.start()

    def target(k, i, row):
        return slots[k, i] * crows + row

    def phase1(r, i, n, buf):
        row = agg[i] - q * crows
        ks = list(range(2 * n, min(2 * n + 2, K)))
        w = []
        for k in ks:
            j = cols[k, i]
            odd = target(k, i, row) & 1
            at = pl.multiple_of((j >> 1) * B + ((j & 1) ^ odd) * TILE, B)
            mask = only[pl.ds(pl.multiple_of(odd * 16, 16), 16), :]
            w.append(tile[pl.ds(at, B), :] * jnp.concatenate([mask] * 3, axis=0))
        if len(ks) == 2:
            none = jnp.zeros((B, 128), bf)
            lhs = jnp.concatenate([blk[r, ks[0]], blk[r, ks[1]]], axis=1)
            p = jnp.dot(lhs, jnp.concatenate([jnp.concatenate([w[0], none], axis=1), jnp.concatenate([none, w[1]], axis=1)], axis=0), preferred_element_type=f32)
            buf[:, n * 256:(n + 1) * 256] = p.astype(bf)
        else:
            for m, k in enumerate(ks):
                buf[:, k * 128:(k + 1) * 128] = jnp.dot(blk[r, k], w[m], preferred_element_type=f32).astype(bf)

    def phase2(i, real, row, n, buf):
        term = jnp.dot(turned[i], buf[:, n * 256:(n + 1) * 256], preferred_element_type=f32)
        for m in range(2):
            k = 2 * n + m
            if k < K:
                t = jnp.where(real, target(k, i, row) >> 1, total // 2)
                acc = hi if m & 1 else lo
                acc[pl.ds(pl.multiple_of(t * B, B), B), :] += term[:, m * 128:(m + 1) * 128]

    def both(r1, buf1, r2, buf2):
        r1 = jnp.minimum(r1, count - 1)
        i1, i2 = todo[r1], todo[jnp.minimum(r2, count - 1)]
        real = r2 < count
        row = agg[i2] - q * crows
        for n in range(PAIRS):
            phase2(i2, real, row, n, buf2)
            phase1(r1, i1, n, buf1)

    def arrived(r):
        @pl.when(r < count)
        def _():
            copy(r).wait()

    @pl.when(count > 0)
    def _():
        arrived(0)
        for n in range(PAIRS):
            phase1(0, todo[0], n, bufa)
        def rows(p, c):
            arrived(2 * p + 1)
            both(2 * p + 1, bufb, 2 * p, bufa)
            arrived(2 * p + 2)
            both(2 * p + 2, bufa, 2 * p + 1, bufb)
            return c
        lax.fori_loop(0, (count + 1) // 2, rows, 0)

    gf = 18 if chunks == 1 else 14
    gh = gf // 2
    def gathered(t2, u, each, groups):
        cols_ = []
        for n in range(each):
            rows_ = []
            for g in range(groups):
                at = pl.multiple_of((t2 + g * each + n) * B + 8 * u, 8)
                rows_.append(lo[pl.ds(at, 8), :] + hi[pl.ds(at, 8), :])
            cols_.append(jnp.concatenate(rows_, axis=0).astype(bf))
        return jnp.concatenate(cols_, axis=1)
    def flush(b, c):
        t2 = b * (gf * 4)
        for y, u in enumerate(FULL):
            x = jnp.dot(gathered(t2, u, 4, gf), full_ref[...], preferred_element_type=f32)
            for g in range(gf):
                for w in range(3):
                    at = pl.multiple_of(((b * gf + g) * 3 + w) * 128, 128)
                    out[y, :, pl.ds(at, 128)] = x[8 * g:8 * g + 8, w * 128:w * 128 + 128].astype(bf)
        for u in (1, 4):
            x0 = gathered(t2, u, 8, gh)
            for y, (v, h) in enumerate(SPLIT):
                if v == u:
                    x = jnp.dot(x0, half_ref[h], preferred_element_type=f32)
                    for g in range(gh):
                        for w in range(3):
                            at = pl.multiple_of((total * B // 128 + (b * gh + g) * 3 + w) * 128, 128)
                            out[y, :, pl.ds(at, 128)] = x[8 * g:8 * g + 8, w * 128:w * 128 + 128].astype(bf)
        return c
    lax.fori_loop(0, total // (8 * gf), flush, 0)
    away = [pltpu.make_async_copy(out.at[(here[0] + d) & 3], sends[d], osems.at[d]) for d in range(4)]
    for c in away:
        c.start()
    for c in away:
        c.wait()
    if keeps:
        keep.wait()

def main(q, chunks, colsT, slotsT, agg, here, blocks, turned, pieces):
    hbm = pl.BlockSpec(memory_space=pl.ANY)
    crows, kslots = slots_of(chunks)
    total = crows * kslots
    shape = [jax.ShapeDtypeStruct((8, total * 72), bf)] * 4 + [jax.ShapeDtypeStruct((TILE, 128), bf)] * (q == 0 and chunks > 1)
    return pl.pallas_call(
        functools.partial(main_kernel, q, chunks),
        out_shape=shape,
        in_specs=[pl.BlockSpec(memory_space=pltpu.SMEM)] * 4 + [hbm] * (2 + len(pieces)),
        out_specs=[hbm] * len(shape),
        scratch_shapes=[pltpu.VMEM((4, 8, total * 72), bf), pltpu.SemaphoreType.DMA((4,)), pltpu.VMEM((R, K, B, B), bf), pltpu.VMEM((R, B, B), bf), pltpu.VMEM((2 * TILE, 128), bf)]
            + [pltpu.VMEM(((total // 2 + 1) * B, 128), f32)] * 2 + [pltpu.VMEM((B, PAIRS * 256), bf)] * 2
            + [pltpu.VMEM((32, 128), bf), pltpu.VMEM((512, 384), bf), pltpu.VMEM((2, 1024, 384), bf)]
            + [pltpu.SMEM((R + 1,), jnp.int32), pltpu.SemaphoreType.DMA((R,)), pltpu.SemaphoreType.DMA((len(pieces) + 1,))],
        compiler_params=pltpu.CompilerParams(vmem_limit_bytes=60 << 20),
        cost_estimate=pl.CostEstimate(flops=2 * 10**10 // chunks, bytes_accessed=10**7, transcendentals=0),
    )(colsT, slotsT, agg, here, blocks, turned, *pieces)

def chunk_rows(chunks):
    crows, kslots = slots_of(chunks)
    rows = crows * kslots * 72 // 128
    return rows, -(-rows // 16) * 16

def sum_kernel(chunks, *refs):
    o_ref, buf = refs[-2:]
    rows, padded = chunk_rows(chunks)
    each = chunks * padded
    for q in range(chunks):
        x = refs[4 * q:4 * q + 4]
        def body(b, c):
            at = pl.multiple_of(b * 128, 128)
            s = (x[0][:, pl.ds(at, 128)].astype(f32) + x[1][:, pl.ds(at, 128)].astype(f32)) + (
                x[2][:, pl.ds(at, 128)].astype(f32) + x[3][:, pl.ds(at, 128)].astype(f32))
            buf[pl.ds(q * padded + b, 8, stride=each), :] = s
            return c
        lax.fori_loop(0, rows, body, 0, unroll=9)
    for z in range(8):
        o_ref[z] = buf[z * each:(z + 1) * each, :].astype(bf)

def sum_y(chunks, parts):
    each = chunks * chunk_rows(chunks)[1]
    return pl.pallas_call(functools.partial(sum_kernel, chunks), out_shape=jax.ShapeDtypeStruct((8, each, 128), bf),
                          scratch_shapes=[pltpu.VMEM((8 * each, 128), f32)])(*parts)

def final_kernel(chunks, par_ref, x_ref, o_ref, tot):
    crows, kslots = slots_of(chunks)
    total = crows * kslots
    padded = chunk_rows(chunks)[1]
    tot[...] = functools.reduce(lambda p, q: p + q, [x_ref[z].astype(f32) for z in range(8)])
    odd = par_ref[0]
    l0 = lax.broadcasted_iota(jnp.int32, (384, 128), 0)
    l1 = lax.broadcasted_iota(jnp.int32, (384, 128), 1)
    for q in range(chunks):
        acc = jnp.zeros((total, 128), f32)
        for step, start, place in ((B, 0, odd * HALF), (HALF, total * B // 128, (1 - odd) * B)):
            side = 384 // step
            groups = total // side
            pick = (l0 % step + place == l1).astype(f32).astype(bf)
            lane = lax.broadcasted_iota(jnp.int32, (1, side, 128), 2)
            which = lax.broadcasted_iota(jnp.int32, (1, side, 128), 1)
            xs = [tot[pl.ds(q * padded + start + w, groups, stride=3), :] for w in range(3)]
            for _ in range(3):
                wide = []
                for w in range(3):
                    top = xs[w].astype(bf).astype(f32)
                    xs[w] = xs[w] - top
                    mine = (lane + w * 128) // step == which
                    wide.append(jnp.where(mine, top[:, None, :], 0.0).reshape(total, 128).astype(bf))
                acc = acc + jnp.dot(jnp.concatenate(wide, axis=1), pick, preferred_element_type=f32)
        o_ref[:, q * crows:(q + 1) * crows, :] = acc[:KC * crows, :72].reshape(KC, crows, 72)

def final(chunks, par, x):
    each = chunks * chunk_rows(chunks)[1]
    return pl.pallas_call(functools.partial(final_kernel, chunks), out_shape=jax.ShapeDtypeStruct((KC, CR, 72), f32),
                          in_specs=[pl.BlockSpec(memory_space=pltpu.SMEM), pl.BlockSpec(memory_space=pltpu.VMEM)],
                          scratch_shapes=[pltpu.VMEM((each, 128), f32)])(par, x)

CHUNKS = 2
ZG = [[z * 4 + y for z in range(8)] for y in range(4)]

def gather(p):
    def along(by):
        return lax.ppermute(p, "row", [(i, (i + 2 * by) % 8) for i in range(8)])
    def across(x):
        return lax.ppermute(x, "row", [(i, i ^ 1) for i in range(8)])
    mine = [p, along(-1), along(1), along(2)]
    return mine + [across(q) for q in mine]

def places(columns):
    row = lax.axis_index("row")
    owner = columns // R
    apart = ((owner >> 1) - (row >> 1)) & 3
    at = jnp.where(apart == 3, 2, jnp.where(apart == 2, 3, apart)) + 4 * ((owner ^ row) & 1)
    return at * R + columns % R

def shards(blocks, prolong, columns, aggregate, slots):
    turned = turn(prolong)
    pieces = gather(pack(prolong))
    cols = places(columns).T
    y = lax.axis_index("col") & 3
    parts = []
    for q in range(CHUNKS):
        out = main(q, CHUNKS, cols, slots.T, aggregate, y.reshape(1), blocks, turned, pieces)
        if q == 0:
            pieces = pieces + list(out[4:])
        if q:
            parts, out = lax.optimization_barrier((parts, out))
            parts, out = list(parts), list(out)
        parts.append(out[0])
        for d in range(1, 4):
            parts.append(lax.ppermute(out[d], "col", [(4 * z + k, 4 * z + (k + d) % 4) for z in range(8) for k in range(4)]))
    summed = lax.all_to_all(sum_y(CHUNKS, parts), "col", 0, 0, axis_index_groups=ZG, tiled=True)
    return final(CHUNKS, (y & 1).reshape(1), summed).transpose(1, 0, 2)


def solution(mesh):
    return jax.shard_map(
        shards,
        mesh=mesh,
        in_specs=(
            jax.sharding.PartitionSpec(("row", "col"), None, None, None),
            jax.sharding.PartitionSpec(("row", "col"), None, None),
            jax.sharding.PartitionSpec(("row", "col"), None),
            jax.sharding.PartitionSpec(("row", "col")),
            jax.sharding.PartitionSpec(("row", "col"), None),
        ),
        out_specs=jax.sharding.PartitionSpec("row", None, "col"),
        check_vma=False,
    )
```

time: 374 us -> 119 us (0.32)
  the two profiles are of different devices: /device:TPU:2 before, /device:TPU:9 now
where the time goes in v3:
time: 119 us; the launch traced here: 118 us
  Pallas kernels  46.1 us (39%)
  starting transfers between devices  35.1 us (29%)
  waiting for transfers between devices  33.1 us (28%)
  local copies, waits for them, and re-layouts  2.56 us (2%)
  other arithmetic  1.35 us (1%)
    pallas_call x2, Pallas kernels, main(): pl.pallas_call(functools.partial(main_kernel, q, chunks), out_shape=shape...  35.6 us
    all_to_all x1, waiting for transfers between devices, shards(): lax.all_to_all(sum_y(CHUNKS, parts), 'col', 0, 0, axis_index_groups=ZG, t...  18 us
    ppermute x4, starting transfers between devices, across(): return lax.ppermute(x, 'row', [(i, i ^ 1) for i in range(8)])  12 us
    ppermute x6, waiting for transfers between devices, shards(): lax.ppermute(out[d], 'col', [(4 * z + k, 4 * z + (k + d) % 4) for z in ra...  11.6 us
    all_to_all x1, starting transfers between devices, shards(): lax.all_to_all(sum_y(CHUNKS, parts), 'col', 0, 0, axis_index_groups=ZG, t...  11.6 us
    ppermute x6, starting transfers between devices, shards(): lax.ppermute(out[d], 'col', [(4 * z + k, 4 * z + (k + d) % 4) for z in ra...  7.33 us
    ppermute x3, starting transfers between devices, along(): return lax.ppermute(p, 'row', [(i, (i + 2 * by) % 8) for i in range(8)])  4.21 us
    pallas_call x1, Pallas kernels, sum_y(): pl.pallas_call(functools.partial(sum_kernel, chunks), out_shape=jax.Shape...  3.55 us
  transfers between devices with their start and end apart: 14, of which 4 were waited for; matrix products, arithmetic and copies ran while one was open for 1% of the time, Pallas kernels for 16%

profile of v3, /device:TPU:9, one launch (start us, length us, event | category | flops | bytes accessed | tf_op | source)
XLA Modules:
  0.0 118.3 jit_solution(10970984668027558099)
XLA Ops:
  0.0 1.9 %shard_map.56.rest_0_ = bf16[1152,128]{1,0:T(8,128)(2,1)} custom-call(bf16[48,48,48]{2,1,0:T(8,128)(2,1)} %p_ref.3), custom_call_target="tpu_custom_call" | custom-call | tf_op jit(solution)/shard_map/pallas_call | solution.py:25
  1.9 2.5 %collective-permute-start = (bf16[1152,128]{1,0:T(8,128)(2,1)}, bf16[1152,128]{1,0:T(8,128)(2,1)S(1)}, u32[]{:S(2)}, u32[]{:S(2)}) collective-permute-start(bf16[1152,128]{1,0:T(8,128)(2,1)} %shard_map.56.rest_0_), channel_id=1, source_target_pairs={{0,192},{32,224},{64,0},{96,32},{128,64},{160,96},{192,128},{224,1... | collective-permute-start | bytes 884744 | tf_op jit(solution)/shard_map/ppermute | solution.py:279
  4.4 0.0 collective-permute-start.1
  4.4 1.7 %collective-permute-start.2 = (bf16[1152,128]{1,0:T(8,128)(2,1)}, bf16[1152,128]{1,0:T(8,128)(2,1)S(1)}, u32[]{:S(2)}, u32[]{:S(2)}) collective-permute-start(bf16[1152,128]{1,0:T(8,128)(2,1)} %shard_map.56.rest_0_), channel_id=1, source_target_pairs={{0,128},{32,160},{64,192},{96,224},{128,0},{160,32},{192,64},{224,... | collective-permute-start | bytes 884744 | tf_op jit(solution)/shard_map/ppermute | solution.py:279
  6.1 1.5 %collective-permute-start.3 = (bf16[1152,128]{1,0:T(8,128)(2,1)}, bf16[1152,128]{1,0:T(8,128)(2,1)S(1)}, u32[]{:S(2)}, u32[]{:S(2)}) collective-permute-start(bf16[1152,128]{1,0:T(8,128)(2,1)} %shard_map.56.rest_0_), channel_id=1, source_target_pairs={{0,32},{32,0},{64,96},{96,64},{128,160},{160,128},{192,224},{224,1... | collective-permute-start | bytes 884744 | tf_op jit(solution)/shard_map/ppermute | solution.py:281
  7.7 3.5 %collective-permute-done.rest_1_ = bf16[1152,128]{1,0:T(8,128)(2,1)S(1)} collective-permute-done((bf16[1152,128]{1,0:T(8,128)(2,1)}, bf16[1152,128]{1,0:T(8,128)(2,1)S(1)}, u32[]{:S(2)}, u32[]{:S(2)}) %collective-permute-start) | collective-permute-done | bytes 294944 | tf_op jit(solution)/shard_map/ppermute | solution.py:279
  11.2 7.1 %collective-permute-start.4 = (bf16[1152,128]{1,0:T(8,128)(2,1)S(1)}, bf16[1152,128]{1,0:T(8,128)(2,1)S(1)}, u32[]{:S(2)}, u32[]{:S(2)}) collective-permute-start(bf16[1152,128]{1,0:T(8,128)(2,1)S(1)} %collective-permute-done.rest_1_), channel_id=1, source_target_pairs={{0,32},{32,0},{64,96},{96,64},{128,160},{160,128},{192,224},{224,1... | collective-permute-start | bytes 884744 | tf_op jit(solution)/shard_map/ppermute | solution.py:281
  18.3 0.0 collective-permute-done.1.rest_2_
  18.3 3.3 %collective-permute-start.5 = (bf16[1152,128]{1,0:T(8,128)(2,1)S(1)}, bf16[1152,128]{1,0:T(8,128)(2,1)S(1)}, u32[]{:S(2)}, u32[]{:S(2)}) collective-permute-start(bf16[1152,128]{1,0:T(8,128)(2,1)S(1)} %collective-permute-done.1.rest_2_), channel_id=1, source_target_pairs={{0,32},{32,0},{64,96},{96,64},{128,160},{160,128},{192,224},{224,1... | collective-permute-start | bytes 884744 | tf_op jit(solution)/shard_map/ppermute | solution.py:281
  21.6 0.0 collective-permute-done.2.rest_3_
  21.6 0.1 collective-permute-start.6
  21.7 2.4 %shard_map.55.turned_hbm = bf16[48,48,48]{2,1,0:T(8,128)(2,1)} custom-call(bf16[48,48,48]{2,1,0:T(8,128)(2,1)} %p_ref.3), custom_call_target="tpu_custom_call" | custom-call | flops 10000000 | bytes 2000000 | tf_op jit(solution)/shard_map/pallas_call | solution.py:35
  24.0 1.4 %fusion.1.cols = s32[27,48]{1,0:T(8,128)} fusion(s32[48,27]{0,1:T(8,128)} %param.7, s32[]{:T(128)S(6)} %axis_index.25, s32[]{:T(128)S(6)} %shift_right_arithmetic.7), kind=kLoop, calls=%fused_computation.4 | loop fusion | flops 32400 | bytes 10376 | tf_op jit(solution)/shard_map/transpose | solution.py:295
  25.5 0.6 copy-done.10
  26.1 0.1 copy-done.11
  26.2 0.1 copy-done.12
  26.3 0.1 copy-done.13
  26.5 18.5 %shard_map.57 = (bf16[8,16128]{1,0:T(8,128)(2,1)}, bf16[8,16128]{1,0:T(8,128)(2,1)}, bf16[8,16128]{1,0:T(8,128)(2,1)}, bf16[8,16128]{1,0:T(8,128)(2,1)}, bf16[9216,128]{1,0:T(8,128)(2,1)}) custom-call(s32[27,48]{1,0:T(8,128)} %fusion.1.cols, s32[27,48]{1,0:T(8,128)} %bitcast.6, s32[48]{0:T(128)} %agg.3, s32[1]{0:T(128)} %bitcast.3.here, ...), custom_call_target="tpu_custom_call" | custom-call | flops 10000000000 | bytes 10000000 | tf_op jit(solution)/shard_map/pallas_call | solution.py:202
  45.0 0.6 collective-permute-start.7
  45.6 1.6 %collective-permute-start.8 = (bf16[8,16128]{1,0:T(8,128)(2,1)}, bf16[8,16128]{1,0:T(8,128)(2,1)S(1)}, u32[]{:S(2)}, u32[]{:S(2)}) collective-permute-start(bf16[8,16128]{1,0:T(8,128)(2,1)} %get-tuple-element.24), channel_id=1, source_target_pairs={{0,2},{1,3},{2,0},{3,1},{4,6},{5,7},{6,4},{7,5},{8,10},{9,11},{10,... | collective-permute-start | bytes 774152 | tf_op jit(solution)/shard_map/ppermute | solution.py:307
  47.2 2.0 %collective-permute-start.9 = (bf16[8,16128]{1,0:T(8,128)(2,1)}, bf16[8,16128]{1,0:T(8,128)(2,1)S(1)}, u32[]{:S(2)}, u32[]{:S(2)}) collective-permute-start(bf16[8,16128]{1,0:T(8,128)(2,1)} %get-tuple-element.25), channel_id=1, source_target_pairs={{0,3},{1,0},{2,1},{3,2},{4,7},{5,4},{6,5},{7,6},{8,11},{9,8},{10,9... | collective-permute-start | bytes 774152 | tf_op jit(solution)/shard_map/ppermute | solution.py:307
  49.1 17.1 %shard_map.58 = (bf16[8,16128]{1,0:T(8,128)(2,1)}, bf16[8,16128]{1,0:T(8,128)(2,1)}, bf16[8,16128]{1,0:T(8,128)(2,1)}, bf16[8,16128]{1,0:T(8,128)(2,1)}) custom-call(s32[27,48]{1,0:T(8,128)} %fusion.1.cols, s32[27,48]{1,0:T(8,128)} %bitcast.7, s32[48]{0:T(128)} %agg.3, s32[1]{0:T(128)} %bitcast.3.here, bf16[48,27,48,48]{3,2,1,0:T(8,128)(2,1)} %blk_hbm.3, ...), custom_call_target="tpu_custom_call" | custom-call | flops 10000000000 | bytes 10000000 | tf_op jit(solution)/shard_map/pallas_call | solution.py:202
  66.3 0.6 collective-permute-start.10
  66.9 2.6 %collective-permute-start.11 = (bf16[8,16128]{1,0:T(8,128)(2,1)}, bf16[8,16128]{1,0:T(8,128)(2,1)S(1)}, u32[]{:S(2)}, u32[]{:S(2)}) collective-permute-start(bf16[8,16128]{1,0:T(8,128)(2,1)} %get-tuple-element.37), channel_id=1, source_target_pairs={{0,2},{1,3},{2,0},{3,1},{4,6},{5,7},{6,4},{7,5},{8,10},{9,11},{10,... | collective-permute-start | bytes 774152 | tf_op jit(solution)/shard_map/ppermute | solution.py:307
  69.5 5.5 %collective-permute-done.10.refs_5_ = bf16[8,16128]{1,0:T(8,128)(2,1)S(1)} collective-permute-done((bf16[8,16128]{1,0:T(8,128)(2,1)}, bf16[8,16128]{1,0:T(8,128)(2,1)S(1)}, u32[]{:S(2)}, u32[]{:S(2)}) %collective-permute-start.10) | collective-permute-done | bytes 258080 | tf_op jit(solution)/shard_map/ppermute | solution.py:307
  75.0 6.1 %collective-permute-done.12.refs_7_ = bf16[8,16128]{1,0:T(8,128)(2,1)S(1)} collective-permute-done((bf16[8,16128]{1,0:T(8,128)(2,1)}, bf16[8,16128]{1,0:T(8,128)(2,1)S(1)}, u32[]{:S(2)}, u32[]{:S(2)}) %collective-permute-start.12) | collective-permute-done | bytes 258080 | tf_op jit(solution)/shard_map/ppermute | solution.py:307
  81.1 0.7 copy-done.6
  81.8 3.6 %shard_map.59 = bf16[8,256,128]{2,1,0:T(8,128)(2,1)} custom-call(bf16[8,16128]{1,0:T(8,128)(2,1)} %get-tuple-element.31.refs_0_, bf16[8,16128]{1,0:T(8,128)(2,1)} %copy-done.1, bf16[8,16128]{1,0:T(8,128)(2,1)} %copy-done.2, bf16[8,16128]{1,0:T(8,128)(2,1)} %copy-done.3, bf16[8,16128]{1,0:T(8,128)(2,1)} %get-tuple-element.35.refs_4_, ...), custom_call_target="tpu_custom_call" | custom-call | tf_op jit(solution)/shard_map/pallas_call | solution.py:238
  85.4 11.6 %all-to-all-start = ((bf16[8,256,128]{2,1,0:T(8,128)(2,1)}), bf16[8,256,128]{2,1,0:T(8,128)(2,1)S(1)}, u32[]{:S(2)}, u32[]{:S(2)}) async-start(bf16[8,256,128]{2,1,0:T(8,128)(2,1)} %shard_map.59), calls=%async_computation | async-start | bytes 1048576 | tf_op jit(solution)/shard_map/all_to_all | solution.py:308
  96.9 18.0 %all-to-all-done.x_ref = bf16[8,256,128]{2,1,0:T(8,128)(2,1)S(1)} async-done(((bf16[8,256,128]{2,1,0:T(8,128)(2,1)}), bf16[8,256,128]{2,1,0:T(8,128)(2,1)S(1)}, u32[]{:S(2)}, u32[]{:S(2)}) %all-to-all-start) | async-done | bytes 524320 | tf_op jit(solution)/shard_map/all_to_all | solution.py:308
  114.9 0.8 copy-done
  115.7 2.6 %shard_map.60 = f32[27,16,72]{2,1,0:T(8,128)} custom-call(s32[1]{0:T(128)} %bitcast.par_ref, bf16[8,256,128]{2,1,0:T(8,128)(2,1)} %copy-done), custom_call_target="tpu_custom_call" | custom-call | tf_op jit(solution)/shard_map/pallas_call | solution.py:270
  (31 shorter events, 0.1 us)
Async XLA Ops:
  1.9 9.3 %collective-permute-start = (bf16[1152,128]{1,0:T(8,128)(2,1)}, bf16[1152,128]{1,0:T(8,128)(2,1)S(1)}, u32[]{:S(2)}, u32[]{:S(2)}) collective-permute-start(bf16[1152,128]{1,0:T(8,128)(2,1)} %shard_map.56.rest_0_), channel_id=1, source_target_pairs={{0,192},{32,224},{64,0},{96,32},{128,64},{160,96},{192,128},{224,1... | collective-permute-start | bytes 884744 | tf_op jit(solution)/shard_map/ppermute | solution.py:279
  4.4 13.9 %collective-permute-start.1 = (bf16[1152,128]{1,0:T(8,128)(2,1)}, bf16[1152,128]{1,0:T(8,128)(2,1)S(1)}, u32[]{:S(2)}, u32[]{:S(2)}) collective-permute-start(bf16[1152,128]{1,0:T(8,128)(2,1)} %shard_map.56.rest_0_), channel_id=1, source_target_pairs={{0,64},{32,96},{64,128},{96,160},{128,192},{160,224},{192,0},{224,... | collective-permute-start | bytes 884744 | tf_op jit(solution)/shard_map/ppermute | solution.py:279
  4.4 17.2 %collective-permute-start.2 = (bf16[1152,128]{1,0:T(8,128)(2,1)}, bf16[1152,128]{1,0:T(8,128)(2,1)S(1)}, u32[]{:S(2)}, u32[]{:S(2)}) collective-permute-start(bf16[1152,128]{1,0:T(8,128)(2,1)} %shard_map.56.rest_0_), channel_id=1, source_target_pairs={{0,128},{32,160},{64,192},{96,224},{128,0},{160,32},{192,64},{224,... | collective-permute-start | bytes 884744 | tf_op jit(solution)/shard_map/ppermute | solution.py:279
  6.1 19.3 %collective-permute-start.3 = (bf16[1152,128]{1,0:T(8,128)(2,1)}, bf16[1152,128]{1,0:T(8,128)(2,1)S(1)}, u32[]{:S(2)}, u32[]{:S(2)}) collective-permute-start(bf16[1152,128]{1,0:T(8,128)(2,1)} %shard_map.56.rest_0_), channel_id=1, source_target_pairs={{0,32},{32,0},{64,96},{96,64},{128,160},{160,128},{192,224},{224,1... | collective-permute-start | bytes 884744 | tf_op jit(solution)/shard_map/ppermute | solution.py:281
  11.2 14.3 %copy-start.7 = (bf16[1152,128]{1,0:T(8,128)(2,1)}, bf16[1152,128]{1,0:T(8,128)(2,1)S(1)}, u32[]{:S(2)}) copy-start(bf16[1152,128]{1,0:T(8,128)(2,1)S(1)} %collective-permute-done.rest_1_) | copy-start | bytes 884740
  11.2 14.2 %collective-permute-start.4 = (bf16[1152,128]{1,0:T(8,128)(2,1)S(1)}, bf16[1152,128]{1,0:T(8,128)(2,1)S(1)}, u32[]{:S(2)}, u32[]{:S(2)}) collective-permute-start(bf16[1152,128]{1,0:T(8,128)(2,1)S(1)} %collective-permute-done.rest_1_), channel_id=1, source_target_pairs={{0,32},{32,0},{64,96},{96,64},{128,160},{160,128},{192,224},{224,1... | collective-permute-start | bytes 884744 | tf_op jit(solution)/shard_map/ppermute | solution.py:281
  18.3 7.2 %copy-start.8 = (bf16[1152,128]{1,0:T(8,128)(2,1)}, bf16[1152,128]{1,0:T(8,128)(2,1)S(1)}, u32[]{:S(2)}) copy-start(bf16[1152,128]{1,0:T(8,128)(2,1)S(1)} %collective-permute-done.1.rest_2_) | copy-start | bytes 884740
  18.3 7.1 %collective-permute-start.5 = (bf16[1152,128]{1,0:T(8,128)(2,1)S(1)}, bf16[1152,128]{1,0:T(8,128)(2,1)S(1)}, u32[]{:S(2)}, u32[]{:S(2)}) collective-permute-start(bf16[1152,128]{1,0:T(8,128)(2,1)S(1)} %collective-permute-done.1.rest_2_), channel_id=1, source_target_pairs={{0,32},{32,0},{64,96},{96,64},{128,160},{160,128},{192,224},{224,1... | collective-permute-start | bytes 884744 | tf_op jit(solution)/shard_map/ppermute | solution.py:281
  21.6 3.9 %copy-start.9 = (bf16[1152,128]{1,0:T(8,128)(2,1)}, bf16[1152,128]{1,0:T(8,128)(2,1)S(1)}, u32[]{:S(2)}) copy-start(bf16[1152,128]{1,0:T(8,128)(2,1)S(1)} %collective-permute-done.2.rest_3_) | copy-start | bytes 884740
  21.6 3.9 %collective-permute-start.6 = (bf16[1152,128]{1,0:T(8,128)(2,1)S(1)}, bf16[1152,128]{1,0:T(8,128)(2,1)S(1)}, u32[]{:S(2)}, u32[]{:S(2)}) collective-permute-start(bf16[1152,128]{1,0:T(8,128)(2,1)S(1)} %collective-permute-done.2.rest_3_), channel_id=1, source_target_pairs={{0,32},{32,0},{64,96},{96,64},{128,160},{160,128},{192,224},{224,1... | collective-permute-start | bytes 884744 | tf_op jit(solution)/shard_map/ppermute | solution.py:281
  25.4 0.7 copy-start.10
  25.4 0.8 copy-start.11
  25.4 0.9 copy-start.12
  25.4 1.0 copy-start.13
  45.0 21.3 %collective-permute-start.7 = (bf16[8,16128]{1,0:T(8,128)(2,1)}, bf16[8,16128]{1,0:T(8,128)(2,1)S(1)}, u32[]{:S(2)}, u32[]{:S(2)}) collective-permute-start(bf16[8,16128]{1,0:T(8,128)(2,1)} %get-tuple-element.23), channel_id=1, source_target_pairs={{0,1},{1,2},{2,3},{3,0},{4,5},{5,6},{6,7},{7,4},{8,9},{9,10},{10,1... | collective-permute-start | bytes 774152 | tf_op jit(solution)/shard_map/ppermute | solution.py:307
  45.6 20.7 %collective-permute-start.8 = (bf16[8,16128]{1,0:T(8,128)(2,1)}, bf16[8,16128]{1,0:T(8,128)(2,1)S(1)}, u32[]{:S(2)}, u32[]{:S(2)}) collective-permute-start(bf16[8,16128]{1,0:T(8,128)(2,1)} %get-tuple-element.24), channel_id=1, source_target_pairs={{0,2},{1,3},{2,0},{3,1},{4,6},{5,7},{6,4},{7,5},{8,10},{9,11},{10,... | collective-permute-start | bytes 774152 | tf_op jit(solution)/shard_map/ppermute | solution.py:307
  47.2 19.1 %collective-permute-start.9 = (bf16[8,16128]{1,0:T(8,128)(2,1)}, bf16[8,16128]{1,0:T(8,128)(2,1)S(1)}, u32[]{:S(2)}, u32[]{:S(2)}) collective-permute-start(bf16[8,16128]{1,0:T(8,128)(2,1)} %get-tuple-element.25), channel_id=1, source_target_pairs={{0,3},{1,0},{2,1},{3,2},{4,7},{5,4},{6,5},{7,6},{8,11},{9,8},{10,9... | collective-permute-start | bytes 774152 | tf_op jit(solution)/shard_map/ppermute | solution.py:307
  66.3 14.8 %copy-start.1 = (bf16[8,16128]{1,0:T(8,128)(2,1)}, bf16[8,16128]{1,0:T(8,128)(2,1)S(1)}, u32[]{:S(2)}) copy-start(bf16[8,16128]{1,0:T(8,128)(2,1)S(1)} %collective-permute-done.7.refs_1_) | copy-start | bytes 774148
  66.3 14.8 %copy-start.2 = (bf16[8,16128]{1,0:T(8,128)(2,1)}, bf16[8,16128]{1,0:T(8,128)(2,1)S(1)}, u32[]{:S(2)}) copy-start(bf16[8,16128]{1,0:T(8,128)(2,1)S(1)} %collective-permute-done.8.refs_2_) | copy-start | bytes 774148
  66.3 14.8 %copy-start.3 = (bf16[8,16128]{1,0:T(8,128)(2,1)}, bf16[8,16128]{1,0:T(8,128)(2,1)S(1)}, u32[]{:S(2)}) copy-start(bf16[8,16128]{1,0:T(8,128)(2,1)S(1)} %collective-permute-done.9.refs_3_) | copy-start | bytes 774148
  66.3 8.6 %collective-permute-start.10 = (bf16[8,16128]{1,0:T(8,128)(2,1)}, bf16[8,16128]{1,0:T(8,128)(2,1)S(1)}, u32[]{:S(2)}, u32[]{:S(2)}) collective-permute-start(bf16[8,16128]{1,0:T(8,128)(2,1)} %get-tuple-element.36), channel_id=1, source_target_pairs={{0,1},{1,2},{2,3},{3,0},{4,5},{5,6},{6,7},{7,4},{8,9},{9,10},{10,1... | collective-permute-start | bytes 774152 | tf_op jit(solution)/shard_map/ppermute | solution.py:307
  66.9 8.1 %collective-permute-start.11 = (bf16[8,16128]{1,0:T(8,128)(2,1)}, bf16[8,16128]{1,0:T(8,128)(2,1)S(1)}, u32[]{:S(2)}, u32[]{:S(2)}) collective-permute-start(bf16[8,16128]{1,0:T(8,128)(2,1)} %get-tuple-element.37), channel_id=1, source_target_pairs={{0,2},{1,3},{2,0},{3,1},{4,6},{5,7},{6,4},{7,5},{8,10},{9,11},{10,... | collective-permute-start | bytes 774152 | tf_op jit(solution)/shard_map/ppermute | solution.py:307
  69.5 11.6 %collective-permute-start.12 = (bf16[8,16128]{1,0:T(8,128)(2,1)}, bf16[8,16128]{1,0:T(8,128)(2,1)S(1)}, u32[]{:S(2)}, u32[]{:S(2)}) collective-permute-start(bf16[8,16128]{1,0:T(8,128)(2,1)} %get-tuple-element.38), channel_id=1, source_target_pairs={{0,3},{1,0},{2,1},{3,2},{4,7},{5,4},{6,5},{7,6},{8,11},{9,8},{10,9... | collective-permute-start | bytes 774152 | tf_op jit(solution)/shard_map/ppermute | solution.py:307
  75.0 6.1 %copy-start.4 = (bf16[8,16128]{1,0:T(8,128)(2,1)}, bf16[8,16128]{1,0:T(8,128)(2,1)S(1)}, u32[]{:S(2)}) copy-start(bf16[8,16128]{1,0:T(8,128)(2,1)S(1)} %collective-permute-done.10.refs_5_) | copy-start | bytes 774148
  75.0 6.1 %copy-start.5 = (bf16[8,16128]{1,0:T(8,128)(2,1)}, bf16[8,16128]{1,0:T(8,128)(2,1)S(1)}, u32[]{:S(2)}) copy-start(bf16[8,16128]{1,0:T(8,128)(2,1)S(1)} %collective-permute-done.11.refs_6_) | copy-start | bytes 774148
  81.1 0.7 copy-start.6
  85.4 29.5 %all-to-all-start = ((bf16[8,256,128]{2,1,0:T(8,128)(2,1)}), bf16[8,256,128]{2,1,0:T(8,128)(2,1)S(1)}, u32[]{:S(2)}, u32[]{:S(2)}) async-start(bf16[8,256,128]{2,1,0:T(8,128)(2,1)} %shard_map.59), calls=%async_computation | async-start | bytes 1048576 | tf_op jit(solution)/shard_map/all_to_all | solution.py:308
  114.9 0.8 copy-start

commit v4 on v0

v4 whole, which is shorter than its diff:
```python
import functools
import jax, jax.numpy as jnp
from jax import lax
from jax.experimental import pallas as pl
from jax.experimental.pallas import tpu as pltpu
bf, f32 = jnp.bfloat16, jnp.float32
B, K, KC, CR, R = 48, 27, 27, 16, 48
PAIRS = (K + 1) // 2
PIECE = R // 2 * B
HALF = B // 2
TILE = 8 * PIECE
FULL = (0, 2, 3, 5)
SPLIT = ((1, 0), (1, 1), (4, 0), (4, 1))

T = KC * CR
FIRST = 288
REST = T - FIRST
ROWS1 = FIRST * 72 // 128
PAD1 = 176
ROWS2 = REST * 72 // 128
PAD2 = 88

def pack_kernel(p_ref, o_ref):
    pad = jnp.zeros((B, 128 - 2 * B), bf)
    for n in range(R // 2):
        o_ref[n * B:(n + 1) * B, :] = jnp.concatenate([p_ref[2 * n], p_ref[2 * n + 1], pad], axis=1)

def pack(p):
    return pl.pallas_call(pack_kernel, out_shape=jax.ShapeDtypeStruct((PIECE, 128), bf))(p)

def turn_kernel(p_ref, o_ref):
    row = lax.broadcasted_iota(jnp.int32, (B, B), 0)
    a = lax.broadcasted_iota(jnp.int32, (B, B), 1)
    pick = (row == (a % 6) * 8 + a // 6).astype(f32).astype(bf)
    for i in range(R):
        o_ref[i] = lax.dot_general(pick, p_ref[i], (((1,), (1,)), ((), ())), preferred_element_type=f32).astype(bf)

def turn(p):
    return pl.pallas_call(turn_kernel, out_shape=jax.ShapeDtypeStruct((R, B, B), bf),
                          cost_estimate=pl.CostEstimate(flops=10**7, bytes_accessed=2 * 10**6, transcendentals=0))(p)

def place_kernel_matrix(n, step, off):
    row = lax.broadcasted_iota(jnp.int32, (n * 128, 384), 0)
    col = lax.broadcasted_iota(jnp.int32, (n * 128, 384), 1)
    t, c = col // step, col % step
    return (row == (t // 2) * 128 + (t % 2) * B + off + c).astype(f32).astype(bf)

def main_kernel(src, odd, dst, here, blk_hbm, turned_hbm, *rest):
    pieces, sends, out2, (out, buf2, osems, blk, turned, tile, lo, hi, bufa, bufb, only, full_ref, half_ref, sems, psems) = (
        rest[:8], rest[8:12], rest[12], rest[13:])
    first = [pltpu.make_async_copy(piece, tile.at[pl.ds(n * PIECE, PIECE)], psems.at[n]) for n, piece in enumerate(pieces)]
    first.append(pltpu.make_async_copy(turned_hbm, turned, psems.at[8]))
    CH = 4
    def copy(n):
        return pltpu.make_async_copy(blk_hbm.at[pl.ds(n * CH, CH)], blk.at[pl.ds(n * CH, CH)], sems.at[n])
    for c in first:
        c.start()
    for n in range(R // CH):
        copy(n).start()

    def zero(n, c):
        z = pl.multiple_of(n * 384, 8)
        lo[pl.ds(z, 384), :] = jnp.zeros((384, 128), f32)
        hi[pl.ds(z, 384), :] = jnp.zeros((384, 128), f32)
        return c
    lax.fori_loop(0, T // 2 * B // 384, zero, 0)
    lane = lax.broadcasted_iota(jnp.int32, (32, 128), 1)
    row = lax.broadcasted_iota(jnp.int32, (32, 128), 0)
    only[...] = ((lane >= B * (row // 16)) & (lane < B * (row // 16) + B)).astype(f32).astype(bf)
    full_ref[...] = place_kernel_matrix(4, B, 0)
    for h in range(2):
        half_ref[h] = place_kernel_matrix(8, HALF, h * HALF)

    l0 = lax.broadcasted_iota(jnp.int32, (128, 128), 0)
    l1 = lax.broadcasted_iota(jnp.int32, (128, 128), 1)
    change = ((l0 < 2 * B) & (l1 == jnp.where(l0 < B, l0 + B, l0 - B))).astype(f32).astype(bf)
    for n in range(8):
        first[n].wait()
        tile[TILE + n * PIECE:TILE + (n + 1) * PIECE, :] = jnp.dot(
            tile[n * PIECE:(n + 1) * PIECE, :], change, preferred_element_type=f32).astype(bf)
    first[8].wait()

    def phase1(i, n, buf):
        ks = list(range(2 * n, min(2 * n + 2, K)))
        w = []
        for k in ks:
            mask = only[pl.ds(pl.multiple_of(odd[k, i], 16), 16), :]
            w.append(tile[pl.ds(pl.multiple_of(src[k, i], B), B), :] * jnp.concatenate([mask] * 3, axis=0))
        if len(ks) == 2:
            none = jnp.zeros((B, 128), bf)
            lhs = jnp.concatenate([blk[i, ks[0]], blk[i, ks[1]]], axis=1)
            w = jnp.concatenate([jnp.concatenate([w[0], none], axis=1), jnp.concatenate([none, w[1]], axis=1)], axis=0)
            buf[:, n * 256:(n + 1) * 256] = jnp.dot(lhs, w, preferred_element_type=f32).astype(bf)
        else:
            buf[:, n * 256:n * 256 + 128] = jnp.dot(blk[i, ks[0]], w[0], preferred_element_type=f32).astype(bf)

    def phase2(i, n, buf):
        wide = 256 if 2 * n + 1 < K else 128
        term = jnp.dot(turned[i], buf[:, n * 256:n * 256 + wide], preferred_element_type=f32)
        for m in range(wide // 128):
            k = 2 * n + m
            acc = hi if m & 1 else lo
            acc[pl.ds(pl.multiple_of(dst[k, i], B), B), :] += term[:, m * 128:(m + 1) * 128]

    def both(i1, buf1, i2, buf2):
        for n in range(PAIRS):
            phase2(i2, n, buf2)
            phase1(i1, n, buf1)

    copy(0).wait()
    for n in range(PAIRS):
        phase1(0, n, bufa)
    def rows(p, c):
        both(2 * p + 1, bufb, 2 * p, bufa)
        @pl.when((p & 1 == 1) & (p < R // 2 - 1))
        def _():
            copy((p + 1) // 2).wait()
        both(jnp.minimum(2 * p + 2, R - 1), bufa, 2 * p + 1, bufb)
        return c
    lax.fori_loop(0, R // 2, rows, 0)

    def gathered(t2, u, each, groups):
        cols_ = []
        for n in range(each):
            rows_ = []
            for g in range(groups):
                at = (t2 + g * each + n) * B + 8 * u
                rows_.append(lo[at:at + 8, :] + hi[at:at + 8, :])
            cols_.append(jnp.concatenate(rows_, axis=0).astype(bf))
        return jnp.concatenate(cols_, axis=1)
    gf, gh = 18, 9
    def put(b, y, half, x):
        for g in range(gh if half else gf):
            for w in range(3):
                v = x[8 * g:8 * g + 8, w * 128:w * 128 + 128]
                if b < 2:
                    at = ((FIRST * B // 128 if half else 0) + (b * (gh if half else gf) + g) * 3 + w) * 128
                    out[y, :, at:at + 128] = v.astype(bf)
                else:
                    r = y * PAD2 + (REST * B // 128 if half else 0) + g * 3 + w
                    buf2[pl.ds(r, 8, stride=4 * PAD2), :] = v
    away = [pltpu.make_async_copy(out.at[(here[0] + d) & 3], sends[d], osems.at[d]) for d in range(4)]
    for b in range(3):
        t2 = b * (gf * 4)
        for y, u in enumerate(FULL):
            put(b, y, False, jnp.dot(gathered(t2, u, 4, gf), full_ref[...], preferred_element_type=f32))
        for u in (1, 4):
            x0 = gathered(t2, u, 8, gh)
            for y, (v, h) in enumerate(SPLIT):
                if v == u:
                    put(b, y, True, jnp.dot(x0, half_ref[h], preferred_element_type=f32))
        if b == 1:
            for c in away:
                c.start()
    for z in range(8):
        out2[z] = buf2[z * 4 * PAD2:(z + 1) * 4 * PAD2, :].astype(bf)
    for c in away:
        c.wait()

def main(src, odd, dst, here, blocks, turned, pieces):
    hbm = pl.BlockSpec(memory_space=pl.ANY)
    vmem = pl.BlockSpec(memory_space=pltpu.VMEM)
    return pl.pallas_call(
        main_kernel,
        out_shape=[jax.ShapeDtypeStruct((8, FIRST * 72), bf)] * 4 + [jax.ShapeDtypeStruct((8, 4 * PAD2, 128), bf)],
        in_specs=[pl.BlockSpec(memory_space=pltpu.SMEM)] * 4 + [hbm] * 10,
        out_specs=[hbm] * 4 + [vmem],
        scratch_shapes=[pltpu.VMEM((4, 8, FIRST * 72), bf), pltpu.VMEM((8 * 4 * PAD2, 128), f32), pltpu.SemaphoreType.DMA((4,)),
                        pltpu.VMEM((R, K, B, B), bf), pltpu.VMEM((R, B, B), bf), pltpu.VMEM((2 * TILE, 128), bf)]
            + [pltpu.VMEM((T // 2 * B, 128), f32)] * 2 + [pltpu.VMEM((B, PAIRS * 256), bf)] * 2
            + [pltpu.VMEM((32, 128), bf), pltpu.VMEM((512, 384), bf), pltpu.VMEM((2, 1024, 384), bf)]
            + [pltpu.SemaphoreType.DMA((12,)), pltpu.SemaphoreType.DMA((9,))],
        compiler_params=pltpu.CompilerParams(vmem_limit_bytes=58 << 20),
        cost_estimate=pl.CostEstimate(flops=2 * 10**10, bytes_accessed=10**7, transcendentals=0),
    )(src, odd, dst, here, blocks, turned, *pieces)

def sum_y_kernel(x0, x1, x2, x3, o_ref, buf):
    def body(b, c):
        at = pl.multiple_of(b * 128, 128)
        s = (x0[:, pl.ds(at, 128)].astype(f32) + x1[:, pl.ds(at, 128)].astype(f32)) + (
            x2[:, pl.ds(at, 128)].astype(f32) + x3[:, pl.ds(at, 128)].astype(f32))
        buf[pl.ds(b, 8, stride=PAD1), :] = s
        return c
    lax.fori_loop(0, ROWS1, body, 0, unroll=18)
    for z in range(8):
        o_ref[z] = buf[z * PAD1:(z + 1) * PAD1, :].astype(bf)

def sum_y(parts):
    return pl.pallas_call(sum_y_kernel, out_shape=jax.ShapeDtypeStruct((8, PAD1, 128), bf),
                          scratch_shapes=[pltpu.VMEM((8 * PAD1, 128), f32)])(*parts)

def sum_z_kernel(here, x_ref, *refs):
    outs, tot = refs[:4], refs[4]
    tot[...] = functools.reduce(lambda p, q: p + q, [x_ref[z].astype(f32) for z in range(8)])
    for d in range(4):
        outs[d][...] = tot[pl.ds(pl.multiple_of(((here[0] + d) & 3) * PAD2, 8), PAD2), :].astype(bf)

def sum_z(here, x):
    return pl.pallas_call(sum_z_kernel, out_shape=[jax.ShapeDtypeStruct((PAD2, 128), bf)] * 4,
                          in_specs=[pl.BlockSpec(memory_space=pltpu.SMEM), pl.BlockSpec(memory_space=pltpu.VMEM)],
                          scratch_shapes=[pltpu.VMEM((4 * PAD2, 128), f32)])(here, x)

def final_kernel(here, x_ref, y0, y1, y2, y3, o_ref, tot1, tot2):
    tot1[...] = functools.reduce(lambda p, q: p + q, [x_ref[z].astype(f32) for z in range(8)])
    tot2[...] = functools.reduce(lambda p, q: p + q, [y[...].astype(f32) for y in (y0, y1, y2, y3)])
    odd = here[0] & 1
    l0 = lax.broadcasted_iota(jnp.int32, (384, 128), 0)
    l1 = lax.broadcasted_iota(jnp.int32, (384, 128), 1)
    for tot, total, slot in ((tot1, FIRST, 0), (tot2, REST, FIRST // CR)):
        acc = jnp.zeros((total, 128), f32)
        for step, start, place in ((B, 0, odd * HALF), (HALF, total * B // 128, (1 - odd) * B)):
            side = 384 // step
            groups = total // side
            pick = (l0 % step + place == l1).astype(f32).astype(bf)
            lane = lax.broadcasted_iota(jnp.int32, (1, side, 128), 2)
            which = lax.broadcasted_iota(jnp.int32, (1, side, 128), 1)
            xs = [tot[pl.ds(start + w, groups, stride=3), :] for w in range(3)]
            for _ in range(3):
                wide = []
                for w in range(3):
                    top = xs[w].astype(bf).astype(f32)
                    xs[w] = xs[w] - top
                    mine = (lane + w * 128) // step == which
                    wide.append(jnp.where(mine, top[:, None, :], 0.0).reshape(total, 128).astype(bf))
                acc = acc + jnp.dot(jnp.concatenate(wide, axis=1), pick, preferred_element_type=f32)
        o_ref[slot:slot + total // CR] = acc[:, :72].reshape(total // CR, CR, 72)

def final(here, x, parts):
    return pl.pallas_call(final_kernel, out_shape=jax.ShapeDtypeStruct((KC, CR, 72), f32),
                          in_specs=[pl.BlockSpec(memory_space=pltpu.SMEM)] + [pl.BlockSpec(memory_space=pltpu.VMEM)] * 5,
                          scratch_shapes=[pltpu.VMEM((PAD1, 128), f32), pltpu.VMEM((PAD2, 128), f32)])(here, x, *parts)

ZG = [[z * 4 + y for z in range(8)] for y in range(4)]

def along_x(x, by):
    return lax.ppermute(x, "row", [(i, (i + 2 * by) % 8) for i in range(8)])

def across(x):
    return lax.ppermute(x, "row", [(i, i ^ 1) for i in range(8)])

def along_y(x, by):
    return lax.ppermute(x, "col", [(4 * z + y, 4 * z + (y + by) % 4) for z in range(8) for y in range(4)])

def exchange_z(x):
    return lax.all_to_all(x, "col", 0, 0, axis_index_groups=ZG, tiled=True)

def indices(columns, aggregate, slots):
    row = lax.axis_index("row")
    owner = columns // R
    apart = ((owner >> 1) - (row >> 1)) & 3
    j = (jnp.where(apart == 3, 2, jnp.where(apart == 2, 3, apart)) + 4 * ((owner ^ row) & 1)) * R + columns % R
    target = slots * CR + aggregate[:, None]
    odd = target & 1
    return ((j >> 1) * B + ((j ^ odd) & 1) * TILE).T, (odd * 16).T, ((target >> 1) * B).T

def shards(blocks, prolong, columns, aggregate, slots):
    packed = pack(prolong)
    mine = [packed, along_x(packed, -1), along_x(packed, 1), along_x(packed, 2)]
    index = indices(columns, aggregate, slots)
    turned = turn(prolong)
    *near, turned, index = lax.optimization_barrier((*mine, turned, index))
    pieces = near + [across(x) for x in near]
    here = (lax.axis_index("col") & 3).reshape(1)
    *sends, other = main(*index, here, blocks, turned, pieces)
    parts = [sends[0]] + [along_y(sends[d], d) for d in range(1, 4)]
    other = sum_z(here, exchange_z(other))
    first = exchange_z(sum_y(parts))
    other = [other[0]] + [along_y(other[d], d) for d in range(1, 4)]
    return final(here, first, other).transpose(1, 0, 2)


def solution(mesh):
    return jax.shard_map(
        shards,
        mesh=mesh,
        in_specs=(
            jax.sharding.PartitionSpec(("row", "col"), None, None, None),
            jax.sharding.PartitionSpec(("row", "col"), None, None),
            jax.sharding.PartitionSpec(("row", "col"), None),
            jax.sharding.PartitionSpec(("row", "col")),
            jax.sharding.PartitionSpec(("row", "col"), None),
        ),
        out_specs=jax.sharding.PartitionSpec("row", None, "col"),
        check_vma=False,
    )
```

time: 374 us -> 108 us (0.29)
  waiting for transfers between devices: 206 us -> 30.2 us
  local copies, waits for them, and re-layouts: 97.1 us -> 2.31 us
  Pallas kernels: 0 us -> 41.7 us
  starting transfers between devices: 0.04 us -> 31.5 us
  matrix products: 27.9 us -> 0 us
  other arithmetic: 27.1 us -> 1.4 us
  between operations: 13.4 us -> 0.1 us
    psum x1 -> x0, waiting for transfers between devices: 168 us -> none  [shards(): summed = lax.psum(partial_value, 'col')]
    pallas_call x0 -> x6, Pallas kernels: none -> 41.7 us  [the longest x1 30.3 us: main(): pl.pallas_call(main_kernel, out_shape=[jax.ShapeDtypeStruct((8, FIRST * 7...]
    all_gather x1 -> x0, waiting for transfers between devices: 37.4 us -> none  [shards(): tile = lax.all_gather(prolong, 'row', axis=0, tiled=True)]
    transpose x1 -> x0, local copies, waits for them, and re-layouts: 32.6 us -> none  [shards(): jnp.einsum('rba,rkbc->rkac', prolong, product, preferred_element_type=jnp...]
    gather x2 -> x0, local copies, waits for them, and re-layouts: 32.4 us -> none  [shards(): picked = jnp.take(tile, columns, axis=0)]
    reshape x2 -> x0, local copies, waits for them, and re-layouts: 29.6 us -> none  [the longest x1 25.7 us: shards(): term.reshape(-1, width * width)]
    dot_general x1 -> x0, matrix products: 27.9 us -> none  [shards(): jnp.einsum('rba,rkbc->rkac', prolong, product, preferred_element_type=jnp...]
    ppermute x0 -> x13, waiting for transfers between devices: none -> 24.2 us  [the longest x6 13.5 us: along_y(): lax.ppermute(x, 'col', [(4 * z + y, 4 * z + (y + by) % 4) for z in range(...]
  transfers between devices with their start and end apart: 2 -> 15, of which waited for: 2 -> 9; matrix products, arithmetic and copies ran while one was open for 1% -> 1% of each run, Pallas kernels for 0% -> 6%
where the time goes in v4:
time: 108 us; the launch traced here: 107 us
  Pallas kernels  41.7 us (39%)
  starting transfers between devices  31.5 us (29%)
  waiting for transfers between devices  30.2 us (28%)
  local copies, waits for them, and re-layouts  2.31 us (2%)
  other arithmetic  1.4 us (1%)
    pallas_call x1, Pallas kernels, main(): pl.pallas_call(main_kernel, out_shape=[jax.ShapeDtypeStruct((8, FIRST * 7...  30.3 us
    all_to_all x2, starting transfers between devices, exchange_z(): return lax.all_to_all(x, 'col', 0, 0, axis_index_groups=ZG, tiled=True)  15.4 us
    ppermute x6, waiting for transfers between devices, along_y(): lax.ppermute(x, 'col', [(4 * z + y, 4 * z + (y + by) % 4) for z in range(...  13.5 us
    ppermute x6, starting transfers between devices, along_y(): lax.ppermute(x, 'col', [(4 * z + y, 4 * z + (y + by) % 4) for z in range(...  10.9 us
    ppermute x3, waiting for transfers between devices, along_x(): return lax.ppermute(x, 'row', [(i, (i + 2 * by) % 8) for i in range(8)])  8.93 us
    all_to_all x2, waiting for transfers between devices, exchange_z(): return lax.all_to_all(x, 'col', 0, 0, axis_index_groups=ZG, tiled=True)  5.98 us
    ppermute x3, starting transfers between devices, along_x(): return lax.ppermute(x, 'row', [(i, (i + 2 * by) % 8) for i in range(8)])  4.15 us
    pallas_call x1, Pallas kernels, final(): pl.pallas_call(final_kernel, out_shape=jax.ShapeDtypeStruct((KC, CR, 72),...  2.63 us
  transfers between devices with their start and end apart: 15, of which 9 were waited for; matrix products, arithmetic and copies ran while one was open for 1% of the time, Pallas kernels for 6%

profile of v4, /device:TPU:2, one launch (start us, length us, event | category | flops | bytes accessed | tf_op | source)
XLA Modules:
  0.0 107.2 jit_solution(1072908168049555581)
XLA Ops:
  0.0 1.9 %shard_map.55.rest_0_ = bf16[1152,128]{1,0:T(8,128)(2,1)} custom-call(bf16[48,48,48]{2,1,0:T(8,128)(2,1)} %p_ref.3), custom_call_target="tpu_custom_call" | custom-call | tf_op jit(solution)/shard_map/pallas_call | solution.py:29
  1.9 2.1 %collective-permute-start.2 = (bf16[1152,128]{1,0:T(8,128)(2,1)}, bf16[1152,128]{1,0:T(8,128)(2,1)S(1)}, u32[]{:S(2)}, u32[]{:S(2)}) collective-permute-start(bf16[1152,128]{1,0:T(8,128)(2,1)} %shard_map.55.rest_0_), channel_id=1, source_target_pairs={{0,128},{32,160},{64,192},{96,224},{128,0},{160,32},{192,64},{224,... | collective-permute-start | bytes 884744 | tf_op jit(solution)/shard_map/ppermute | solution.py:236
  4.1 1.6 %collective-permute-start.1 = (bf16[1152,128]{1,0:T(8,128)(2,1)}, bf16[1152,128]{1,0:T(8,128)(2,1)S(1)}, u32[]{:S(2)}, u32[]{:S(2)}) collective-permute-start(bf16[1152,128]{1,0:T(8,128)(2,1)} %shard_map.55.rest_0_), channel_id=1, source_target_pairs={{0,64},{32,96},{64,128},{96,160},{128,192},{160,224},{192,0},{224,... | collective-permute-start | bytes 884744 | tf_op jit(solution)/shard_map/ppermute | solution.py:236
  5.7 0.4 collective-permute-start
  6.1 2.4 %shard_map.56.turned_hbm = bf16[48,48,48]{2,1,0:T(8,128)(2,1)} custom-call(bf16[48,48,48]{2,1,0:T(8,128)(2,1)} %p_ref.3), custom_call_target="tpu_custom_call" | custom-call | flops 10000000 | bytes 2000000 | tf_op jit(solution)/shard_map/pallas_call | solution.py:39
  8.5 1.4 %multiply_bitcast_fusion = (s32[27,48]{1,0:T(8,128)}, s32[27,48]{1,0:T(8,128)}, s32[27,48]{1,0:T(8,128)}) fusion(s32[48,27]{0,1:T(8,128)} %param.9, s32[48]{0:T(128)} %param.8, s32[]{:T(128)S(6)} %axis_index.25, s32[]{:T(128)S(6)} %shift_right_arithmetic.13, s32[48,27]{0,1:T(8,128)} %param.7), kind=kLoop, calls=%fused_computation.7 | loop fusion | flops 47952 | bytes 26120 | tf_op jit(solution)/shard_map/transpose | solution.py:254
  9.9 3.7 %collective-permute-done.2.rest_3_ = bf16[1152,128]{1,0:T(8,128)(2,1)S(1)} collective-permute-done((bf16[1152,128]{1,0:T(8,128)(2,1)}, bf16[1152,128]{1,0:T(8,128)(2,1)S(1)}, u32[]{:S(2)}, u32[]{:S(2)}) %collective-permute-start.2) | collective-permute-done | bytes 294944 | tf_op jit(solution)/shard_map/ppermute | solution.py:236
  13.6 5.2 %collective-permute-done.1.rest_2_ = bf16[1152,128]{1,0:T(8,128)(2,1)S(1)} collective-permute-done((bf16[1152,128]{1,0:T(8,128)(2,1)}, bf16[1152,128]{1,0:T(8,128)(2,1)S(1)}, u32[]{:S(2)}, u32[]{:S(2)}) %collective-permute-start.1) | collective-permute-done | bytes 294944 | tf_op jit(solution)/shard_map/ppermute | solution.py:236
  18.9 0.5 collective-permute-start.4
  19.5 0.4 collective-permute-start.6
  19.9 0.8 collective-permute-done.3.rest_4_
  20.9 0.4 collective-permute-done.5.rest_6_
  21.3 0.4 collective-permute-done.6.rest_7_
  21.8 0.3 copy-done.13
  22.0 0.4 copy-done.14
  22.4 30.3 %shard_map.57 = (bf16[8,20736]{1,0:T(8,128)(2,1)}, bf16[8,20736]{1,0:T(8,128)(2,1)}, bf16[8,20736]{1,0:T(8,128)(2,1)}, bf16[8,20736]{1,0:T(8,128)(2,1)}, bf16[8,352,128]{2,1,0:T(8,128)(2,1)}) custom-call(s32[27,48]{1,0:T(8,128)} %get-tuple-element.22.src, s32[27,48]{1,0:T(8,128)} %get-tuple-element.23.odd, s32[27,48]{1,0:T(8,128)} %get-tuple-element.24.dst, ...), custom_call_target="tpu_custom_call" | custom-call | flops 20000000000 | bytes 10000000 | tf_op jit(solution)/shard_map/pallas_call | solution.py:163
  52.7 8.4 %all-to-all-start.1 = ((bf16[8,352,128]{2,1,0:T(8,128)(2,1)}), bf16[8,352,128]{2,1,0:T(8,128)(2,1)S(1)}, u32[]{:S(2)}, u32[]{:S(2)}) async-start(bf16[8,352,128]{2,1,0:T(8,128)(2,1)} %get-tuple-element.34), calls=%async_computation.1 | async-start | bytes 1441792 | tf_op jit(solution)/shard_map/all_to_all | solution.py:245
  61.2 1.6 %collective-permute-start.7 = (bf16[8,20736]{1,0:T(8,128)(2,1)}, bf16[8,20736]{1,0:T(8,128)(2,1)S(1)}, u32[]{:S(2)}, u32[]{:S(2)}) collective-permute-start(bf16[8,20736]{1,0:T(8,128)(2,1)} %get-tuple-element.31), channel_id=1, source_target_pairs={{0,1},{1,2},{2,3},{3,0},{4,5},{5,6},{6,7},{7,4},{8,9},{9,10},{10,1... | collective-permute-start | bytes 995336 | tf_op jit(solution)/shard_map/ppermute | solution.py:242
  62.8 2.9 %collective-permute-start.8 = (bf16[8,20736]{1,0:T(8,128)(2,1)}, bf16[8,20736]{1,0:T(8,128)(2,1)S(1)}, u32[]{:S(2)}, u32[]{:S(2)}) collective-permute-start(bf16[8,20736]{1,0:T(8,128)(2,1)} %get-tuple-element.32), channel_id=1, source_target_pairs={{0,2},{1,3},{2,0},{3,1},{4,6},{5,7},{6,4},{7,5},{8,10},{9,11},{10,... | collective-permute-start | bytes 995336 | tf_op jit(solution)/shard_map/ppermute | solution.py:242
  65.6 1.4 %collective-permute-start.9 = (bf16[8,20736]{1,0:T(8,128)(2,1)}, bf16[8,20736]{1,0:T(8,128)(2,1)S(1)}, u32[]{:S(2)}, u32[]{:S(2)}) collective-permute-start(bf16[8,20736]{1,0:T(8,128)(2,1)} %get-tuple-element.33), channel_id=1, source_target_pairs={{0,3},{1,0},{2,1},{3,2},{4,7},{5,4},{6,5},{7,6},{8,11},{9,8},{10,9... | collective-permute-start | bytes 995336 | tf_op jit(solution)/shard_map/ppermute | solution.py:242
  67.0 5.2 %collective-permute-done.7.x1 = bf16[8,20736]{1,0:T(8,128)(2,1)S(1)} collective-permute-done((bf16[8,20736]{1,0:T(8,128)(2,1)}, bf16[8,20736]{1,0:T(8,128)(2,1)S(1)}, u32[]{:S(2)}, u32[]{:S(2)}) %collective-permute-start.7) | collective-permute-done | bytes 331808 | tf_op jit(solution)/shard_map/ppermute | solution.py:242
  72.2 8.3 %collective-permute-done.8.x2 = bf16[8,20736]{1,0:T(8,128)(2,1)S(1)} collective-permute-done((bf16[8,20736]{1,0:T(8,128)(2,1)}, bf16[8,20736]{1,0:T(8,128)(2,1)S(1)}, u32[]{:S(2)}, u32[]{:S(2)}) %collective-permute-start.8) | collective-permute-done | bytes 331808 | tf_op jit(solution)/shard_map/ppermute | solution.py:242
  80.5 0.7 copy-done.3
  81.4 2.6 %shard_map.58 = bf16[8,176,128]{2,1,0:T(8,128)(2,1)} custom-call(bf16[8,20736]{1,0:T(8,128)(2,1)} %get-tuple-element.30.x0, bf16[8,20736]{1,0:T(8,128)(2,1)} %copy-done.2, bf16[8,20736]{1,0:T(8,128)(2,1)} %copy-done.3, bf16[8,20736]{1,0:T(8,128)(2,1)} %copy-done.4), custom_call_target="tpu_custom_call" | custom-call | tf_op jit(solution)/shard_map/pallas_call | solution.py:189
  84.0 6.9 %all-to-all-start = ((bf16[8,176,128]{2,1,0:T(8,128)(2,1)}), bf16[8,176,128]{2,1,0:T(8,128)(2,1)S(1)}, u32[]{:S(2)}, u32[]{:S(2)}) async-start(bf16[8,176,128]{2,1,0:T(8,128)(2,1)} %shard_map.58), calls=%async_computation | async-start | bytes 720896 | tf_op jit(solution)/shard_map/all_to_all | solution.py:245
  90.9 1.9 %shard_map.59 = (bf16[88,128]{1,0:T(8,128)(2,1)}, bf16[88,128]{1,0:T(8,128)(2,1)}, bf16[88,128]{1,0:T(8,128)(2,1)}, bf16[88,128]{1,0:T(8,128)(2,1)}) custom-call(s32[1]{0:T(128)} %bitcast.here, bf16[8,352,128]{2,1,0:T(8,128)(2,1)} %copy-done), custom_call_target="tpu_custom_call" | custom-call | tf_op jit(solution)/shard_map/pallas_call | solution.py:199
  92.8 1.0 collective-permute-start.10
  93.8 2.4 %collective-permute-start.11 = (bf16[88,128]{1,0:T(8,128)(2,1)}, bf16[88,128]{1,0:T(8,128)(2,1)S(1)}, u32[]{:S(2)}, u32[]{:S(2)}) collective-permute-start(bf16[88,128]{1,0:T(8,128)(2,1)} %get-tuple-element.37), channel_id=1, source_target_pairs={{0,2},{1,3},{2,0},{3,1},{4,6},{5,7},{6,4},{7,5},{8,10},{9,11},{10,... | collective-permute-start | bytes 67592 | tf_op jit(solution)/shard_map/ppermute | solution.py:242
  96.2 1.6 %collective-permute-start.12 = (bf16[88,128]{1,0:T(8,128)(2,1)}, bf16[88,128]{1,0:T(8,128)(2,1)S(1)}, u32[]{:S(2)}, u32[]{:S(2)}) collective-permute-start(bf16[88,128]{1,0:T(8,128)(2,1)} %get-tuple-element.38), channel_id=1, source_target_pairs={{0,3},{1,0},{2,1},{3,2},{4,7},{5,4},{6,5},{7,6},{8,11},{9,8},{10,9... | collective-permute-start | bytes 67592 | tf_op jit(solution)/shard_map/ppermute | solution.py:242
  97.8 6.0 %all-to-all-done.x_ref = bf16[8,176,128]{2,1,0:T(8,128)(2,1)S(1)} async-done(((bf16[8,176,128]{2,1,0:T(8,128)(2,1)}), bf16[8,176,128]{2,1,0:T(8,128)(2,1)S(1)}, u32[]{:S(2)}, u32[]{:S(2)}) %all-to-all-start) | async-done | bytes 360480 | tf_op jit(solution)/shard_map/all_to_all | solution.py:245
  103.8 0.7 copy-done.1
  104.6 2.6 %shard_map.60 = f32[27,16,72]{2,1,0:T(8,128)} custom-call(s32[1]{0:T(128)} %bitcast.here, bf16[8,176,128]{2,1,0:T(8,128)(2,1)} %copy-done.1, bf16[88,128]{1,0:T(8,128)(2,1)} %get-tuple-element.35.y0, bf16[88,128]{1,0:T(8,128)(2,1)} %copy-done.5, bf16[88,128]{1,0:T(8,128)(2,1)} %copy-done.6, bf16[88,128]{1,0:T(8,128)(2,1)} %copy-done.7), custom_call_target="tpu_custom_call" | custom-call | tf_op jit(solution)/shard_map/pallas_call | solution.py:229
  (35 shorter events, 0.6 us)
Async XLA Ops:
  1.9 11.7 %collective-permute-start.2 = (bf16[1152,128]{1,0:T(8,128)(2,1)}, bf16[1152,128]{1,0:T(8,128)(2,1)S(1)}, u32[]{:S(2)}, u32[]{:S(2)}) collective-permute-start(bf16[1152,128]{1,0:T(8,128)(2,1)} %shard_map.55.rest_0_), channel_id=1, source_target_pairs={{0,128},{32,160},{64,192},{96,224},{128,0},{160,32},{192,64},{224,... | collective-permute-start | bytes 884744 | tf_op jit(solution)/shard_map/ppermute | solution.py:236
  4.1 14.7 %collective-permute-start.1 = (bf16[1152,128]{1,0:T(8,128)(2,1)}, bf16[1152,128]{1,0:T(8,128)(2,1)S(1)}, u32[]{:S(2)}, u32[]{:S(2)}) collective-permute-start(bf16[1152,128]{1,0:T(8,128)(2,1)} %shard_map.55.rest_0_), channel_id=1, source_target_pairs={{0,64},{32,96},{64,128},{96,160},{128,192},{160,224},{192,0},{224,... | collective-permute-start | bytes 884744 | tf_op jit(solution)/shard_map/ppermute | solution.py:236
  5.7 13.1 %collective-permute-start = (bf16[1152,128]{1,0:T(8,128)(2,1)}, bf16[1152,128]{1,0:T(8,128)(2,1)S(1)}, u32[]{:S(2)}, u32[]{:S(2)}) collective-permute-start(bf16[1152,128]{1,0:T(8,128)(2,1)} %shard_map.55.rest_0_), channel_id=1, source_target_pairs={{0,192},{32,224},{64,0},{96,32},{128,64},{160,96},{192,128},{224,1... | collective-permute-start | bytes 884744 | tf_op jit(solution)/shard_map/ppermute | solution.py:236
  13.6 8.1 %copy-start.8 = (bf16[1152,128]{1,0:T(8,128)(2,1)}, bf16[1152,128]{1,0:T(8,128)(2,1)S(1)}, u32[]{:S(2)}) copy-start(bf16[1152,128]{1,0:T(8,128)(2,1)S(1)} %collective-permute-done.2.rest_3_) | copy-start | bytes 884740
  18.8 2.9 %copy-start.9 = (bf16[1152,128]{1,0:T(8,128)(2,1)}, bf16[1152,128]{1,0:T(8,128)(2,1)S(1)}, u32[]{:S(2)}) copy-start(bf16[1152,128]{1,0:T(8,128)(2,1)S(1)} %collective-permute-done.1.rest_2_) | copy-start | bytes 884740
  18.8 2.9 %copy-start.10 = (bf16[1152,128]{1,0:T(8,128)(2,1)}, bf16[1152,128]{1,0:T(8,128)(2,1)S(1)}, u32[]{:S(2)}) copy-start(bf16[1152,128]{1,0:T(8,128)(2,1)S(1)} %collective-permute-done.rest_1_) | copy-start | bytes 884740
  18.8 1.9 %collective-permute-start.3 = (bf16[1152,128]{1,0:T(8,128)(2,1)}, bf16[1152,128]{1,0:T(8,128)(2,1)S(1)}, u32[]{:S(2)}, u32[]{:S(2)}) collective-permute-start(bf16[1152,128]{1,0:T(8,128)(2,1)} %shard_map.55.rest_0_), channel_id=1, source_target_pairs={{0,32},{32,0},{64,96},{96,64},{128,160},{160,128},{192,224},{224,1... | collective-permute-start | bytes 884744 | tf_op jit(solution)/shard_map/ppermute | solution.py:239
  18.9 2.0 %collective-permute-start.4 = (bf16[1152,128]{1,0:T(8,128)(2,1)S(1)}, bf16[1152,128]{1,0:T(8,128)(2,1)S(1)}, u32[]{:S(2)}, u32[]{:S(2)}) collective-permute-start(bf16[1152,128]{1,0:T(8,128)(2,1)S(1)} %collective-permute-done.rest_1_), channel_id=1, source_target_pairs={{0,32},{32,0},{64,96},{96,64},{128,160},{160,128},{192,224},{224,1... | collective-permute-start | bytes 884744 | tf_op jit(solution)/shard_map/ppermute | solution.py:239
  19.4 1.9 %collective-permute-start.5 = (bf16[1152,128]{1,0:T(8,128)(2,1)S(1)}, bf16[1152,128]{1,0:T(8,128)(2,1)S(1)}, u32[]{:S(2)}, u32[]{:S(2)}) collective-permute-start(bf16[1152,128]{1,0:T(8,128)(2,1)S(1)} %collective-permute-done.1.rest_2_), channel_id=1, source_target_pairs={{0,32},{32,0},{64,96},{96,64},{128,160},{160,128},{192,224},{224,1... | collective-permute-start | bytes 884744 | tf_op jit(solution)/shard_map/ppermute | solution.py:239
  19.5 2.2 %collective-permute-start.6 = (bf16[1152,128]{1,0:T(8,128)(2,1)S(1)}, bf16[1152,128]{1,0:T(8,128)(2,1)S(1)}, u32[]{:S(2)}, u32[]{:S(2)}) collective-permute-start(bf16[1152,128]{1,0:T(8,128)(2,1)S(1)} %collective-permute-done.2.rest_3_), channel_id=1, source_target_pairs={{0,32},{32,0},{64,96},{96,64},{128,160},{160,128},{192,224},{224,1... | collective-permute-start | bytes 884744 | tf_op jit(solution)/shard_map/ppermute | solution.py:239
  20.7 1.1 copy-start.11
  20.9 0.9 copy-start.12
  21.3 0.7 copy-start.13
  21.7 0.7 copy-start.14
  52.7 31.2 %all-to-all-start.1 = ((bf16[8,352,128]{2,1,0:T(8,128)(2,1)}), bf16[8,352,128]{2,1,0:T(8,128)(2,1)S(1)}, u32[]{:S(2)}, u32[]{:S(2)}) async-start(bf16[8,352,128]{2,1,0:T(8,128)(2,1)} %get-tuple-element.34), calls=%async_computation.1 | async-start | bytes 1441792 | tf_op jit(solution)/shard_map/all_to_all | solution.py:245
  61.2 11.1 %collective-permute-start.7 = (bf16[8,20736]{1,0:T(8,128)(2,1)}, bf16[8,20736]{1,0:T(8,128)(2,1)S(1)}, u32[]{:S(2)}, u32[]{:S(2)}) collective-permute-start(bf16[8,20736]{1,0:T(8,128)(2,1)} %get-tuple-element.31), channel_id=1, source_target_pairs={{0,1},{1,2},{2,3},{3,0},{4,5},{5,6},{6,7},{7,4},{8,9},{9,10},{10,1... | collective-permute-start | bytes 995336 | tf_op jit(solution)/shard_map/ppermute | solution.py:242
  62.8 17.8 %collective-permute-start.8 = (bf16[8,20736]{1,0:T(8,128)(2,1)}, bf16[8,20736]{1,0:T(8,128)(2,1)S(1)}, u32[]{:S(2)}, u32[]{:S(2)}) collective-permute-start(bf16[8,20736]{1,0:T(8,128)(2,1)} %get-tuple-element.32), channel_id=1, source_target_pairs={{0,2},{1,3},{2,0},{3,1},{4,6},{5,7},{6,4},{7,5},{8,10},{9,11},{10,... | collective-permute-start | bytes 995336 | tf_op jit(solution)/shard_map/ppermute | solution.py:242
  65.6 14.9 %collective-permute-start.9 = (bf16[8,20736]{1,0:T(8,128)(2,1)}, bf16[8,20736]{1,0:T(8,128)(2,1)S(1)}, u32[]{:S(2)}, u32[]{:S(2)}) collective-permute-start(bf16[8,20736]{1,0:T(8,128)(2,1)} %get-tuple-element.33), channel_id=1, source_target_pairs={{0,3},{1,0},{2,1},{3,2},{4,7},{5,4},{6,5},{7,6},{8,11},{9,8},{10,9... | collective-permute-start | bytes 995336 | tf_op jit(solution)/shard_map/ppermute | solution.py:242
  72.2 8.3 %copy-start.2 = (bf16[8,20736]{1,0:T(8,128)(2,1)}, bf16[8,20736]{1,0:T(8,128)(2,1)S(1)}, u32[]{:S(2)}) copy-start(bf16[8,20736]{1,0:T(8,128)(2,1)S(1)} %collective-permute-done.7.x1) | copy-start | bytes 995332
  80.5 0.7 copy-start.3
  80.5 0.9 copy-start.4
  84.0 6.9 %copy-start = (bf16[8,352,128]{2,1,0:T(8,128)(2,1)}, bf16[8,352,128]{2,1,0:T(8,128)(2,1)S(1)}, u32[]{:S(2)}) copy-start(bf16[8,352,128]{2,1,0:T(8,128)(2,1)S(1)} %all-to-all-done.1.x_ref) | copy-start | bytes 2162692
  84.0 19.8 %all-to-all-start = ((bf16[8,176,128]{2,1,0:T(8,128)(2,1)}), bf16[8,176,128]{2,1,0:T(8,128)(2,1)S(1)}, u32[]{:S(2)}, u32[]{:S(2)}) async-start(bf16[8,176,128]{2,1,0:T(8,128)(2,1)} %shard_map.58), calls=%async_computation | async-start | bytes 720896 | tf_op jit(solution)/shard_map/all_to_all | solution.py:245
  92.8 11.0 %collective-permute-start.10 = (bf16[88,128]{1,0:T(8,128)(2,1)}, bf16[88,128]{1,0:T(8,128)(2,1)S(1)}, u32[]{:S(2)}, u32[]{:S(2)}) collective-permute-start(bf16[88,128]{1,0:T(8,128)(2,1)} %get-tuple-element.36), channel_id=1, source_target_pairs={{0,1},{1,2},{2,3},{3,0},{4,5},{5,6},{6,7},{7,4},{8,9},{9,10},{10,1... | collective-permute-start | bytes 67592 | tf_op jit(solution)/shard_map/ppermute | solution.py:242
  93.8 10.0 %collective-permute-start.11 = (bf16[88,128]{1,0:T(8,128)(2,1)}, bf16[88,128]{1,0:T(8,128)(2,1)S(1)}, u32[]{:S(2)}, u32[]{:S(2)}) collective-permute-start(bf16[88,128]{1,0:T(8,128)(2,1)} %get-tuple-element.37), channel_id=1, source_target_pairs={{0,2},{1,3},{2,0},{3,1},{4,6},{5,7},{6,4},{7,5},{8,10},{9,11},{10,... | collective-permute-start | bytes 67592 | tf_op jit(solution)/shard_map/ppermute | solution.py:242
  96.2 7.6 %collective-permute-start.12 = (bf16[88,128]{1,0:T(8,128)(2,1)}, bf16[88,128]{1,0:T(8,128)(2,1)S(1)}, u32[]{:S(2)}, u32[]{:S(2)}) collective-permute-start(bf16[88,128]{1,0:T(8,128)(2,1)} %get-tuple-element.38), channel_id=1, source_target_pairs={{0,3},{1,0},{2,1},{3,2},{4,7},{5,4},{6,5},{7,6},{8,11},{9,8},{10,9... | collective-permute-start | bytes 67592 | tf_op jit(solution)/shard_map/ppermute | solution.py:242
  103.8 0.7 copy-start.1
  103.8 0.7 copy-start.5
  103.8 0.7 copy-start.6
  103.8 0.7 copy-start.7

commit v5 on v4

--- a/solution.py
+++ b/solution.py
@@ -21,12 +21,11 @@
 PAD2 = 88
 
 def pack_kernel(p_ref, o_ref):
-    pad = jnp.zeros((B, 128 - 2 * B), bf)
-    for n in range(R // 2):
-        o_ref[n * B:(n + 1) * B, :] = jnp.concatenate([p_ref[2 * n], p_ref[2 * n + 1], pad], axis=1)
+    for g in range(R // 8):
+        o_ref[g * B:(g + 1) * B, :] = jnp.concatenate([p_ref[8 * g + m] for m in range(8)], axis=1)
 
 def pack(p):
-    return pl.pallas_call(pack_kernel, out_shape=jax.ShapeDtypeStruct((PIECE, 128), bf))(p)
+    return pl.pallas_call(pack_kernel, out_shape=jax.ShapeDtypeStruct((R // 8 * B, 8 * B), bf))(p)
 
 def turn_kernel(p_ref, o_ref):
     row = lax.broadcasted_iota(jnp.int32, (B, B), 0)
@@ -46,9 +45,9 @@
     return (row == (t // 2) * 128 + (t % 2) * B + off + c).astype(f32).astype(bf)
 
 def main_kernel(src, odd, dst, here, blk_hbm, turned_hbm, *rest):
-    pieces, sends, out2, (out, buf2, osems, blk, turned, tile, lo, hi, bufa, bufb, only, full_ref, half_ref, sems, psems) = (
+    pieces, sends, out2, (stage, out, buf2, osems, blk, turned, tile, lo, hi, bufa, bufb, only, full_ref, half_ref, sems, psems) = (
         rest[:8], rest[8:12], rest[12], rest[13:])
-    first = [pltpu.make_async_copy(piece, tile.at[pl.ds(n * PIECE, PIECE)], psems.at[n]) for n, piece in enumerate(pieces)]
+    first = [pltpu.make_async_copy(piece, stage.at[n], psems.at[n]) for n, piece in enumerate(pieces)]
     first.append(pltpu.make_async_copy(turned_hbm, turned, psems.at[8]))
     CH = 4
     def copy(n):
@@ -71,13 +70,23 @@
     for h in range(2):
         half_ref[h] = place_kernel_matrix(8, HALF, h * HALF)
 
-    l0 = lax.broadcasted_iota(jnp.int32, (128, 128), 0)
-    l1 = lax.broadcasted_iota(jnp.int32, (128, 128), 1)
-    change = ((l0 < 2 * B) & (l1 == jnp.where(l0 < B, l0 + B, l0 - B))).astype(f32).astype(bf)
+    picks = []
+    for p in range(4):
+        start = 2 * B * p // 128 * 128
+        wide = min(256, 8 * B - start)
+        l0 = lax.broadcasted_iota(jnp.int32, (wide, 256), 0) + start - 2 * B * p
+        l1 = lax.broadcasted_iota(jnp.int32, (wide, 256), 1)
+        other = l1 - 128
+        keep = (l1 < 2 * B) & (l0 == l1)
+        change = (other >= 0) & (other < 2 * B) & (l0 == jnp.where(other < B, other + B, other - B))
+        picks.append((start, wide, (keep | change).astype(f32).astype(bf)))
     for n in range(8):
         first[n].wait()
-        tile[TILE + n * PIECE:TILE + (n + 1) * PIECE, :] = jnp.dot(
-            tile[n * PIECE:(n + 1) * PIECE, :], change, preferred_element_type=f32).astype(bf)
+        for p, (start, wide, pick) in enumerate(picks):
+            x = jnp.dot(stage[n, :, start:start + wide], pick, preferred_element_type=f32).astype(bf)
+            at = (4 * n + p) * (R // 8 * B)
+            tile[at:at + R // 8 * B, :] = x[:, :128]
+            tile[TILE + at:TILE + at + R // 8 * B, :] = x[:, 128:]
     first[8].wait()
 
     def phase1(i, n, buf):
@@ -165,7 +174,7 @@
         out_shape=[jax.ShapeDtypeStruct((8, FIRST * 72), bf)] * 4 + [jax.ShapeDtypeStruct((8, 4 * PAD2, 128), bf)],
         in_specs=[pl.BlockSpec(memory_space=pltpu.SMEM)] * 4 + [hbm] * 10,
         out_specs=[hbm] * 4 + [vmem],
-        scratch_shapes=[pltpu.VMEM((4, 8, FIRST * 72), bf), pltpu.VMEM((8 * 4 * PAD2, 128), f32), pltpu.SemaphoreType.DMA((4,)),
+        scratch_shapes=[pltpu.VMEM((8, R // 8 * B, 8 * B), bf), pltpu.VMEM((4, 8, FIRST * 72), bf), pltpu.VMEM((8 * 4 * PAD2, 128), f32), pltpu.SemaphoreType.DMA((4,)),
                         pltpu.VMEM((R, K, B, B), bf), pltpu.VMEM((R, B, B), bf), pltpu.VMEM((2 * TILE, 128), bf)]
             + [pltpu.VMEM((T // 2 * B, 128), f32)] * 2 + [pltpu.VMEM((B, PAIRS * 256), bf)] * 2
             + [pltpu.VMEM((32, 128), bf), pltpu.VMEM((512, 384), bf), pltpu.VMEM((2, 1024, 384), bf)]
@@ -187,7 +196,8 @@
 
 def sum_y(parts):
     return pl.pallas_call(sum_y_kernel, out_shape=jax.ShapeDtypeStruct((8, PAD1, 128), bf),
-                          scratch_shapes=[pltpu.VMEM((8 * PAD1, 128), f32)])(*parts)
+                          scratch_shapes=[pltpu.VMEM((8 * PAD1, 128), f32)],
+                          cost_estimate=pl.CostEstimate(flops=4 * 10**10, bytes_accessed=10**7, transcendentals=0))(*parts)
 
 def sum_z_kernel(here, x_ref, *refs):
     outs, tot = refs[:4], refs[4]
@@ -248,10 +258,12 @@
     row = lax.axis_index("row")
     owner = columns // R
     apart = ((owner >> 1) - (row >> 1)) & 3
-    j = (jnp.where(apart == 3, 2, jnp.where(apart == 2, 3, apart)) + 4 * ((owner ^ row) & 1)) * R + columns % R
+    piece = jnp.where(apart == 3, 2, jnp.where(apart == 2, 3, apart)) + 4 * ((owner ^ row) & 1)
+    t = columns % R
+    at = piece * (R // 2) + ((t & 7) >> 1) * (R // 8) + (t >> 3)
     target = slots * CR + aggregate[:, None]
     odd = target & 1
-    return ((j >> 1) * B + ((j ^ odd) & 1) * TILE).T, (odd * 16).T, ((target >> 1) * B).T
+    return (at * B + ((t ^ odd) & 1) * TILE).T, (odd * 16).T, ((target >> 1) * B).T
 
 def shards(blocks, prolong, columns, aggregate, slots):
     packed = pack(prolong)

time: 108 us -> 107 us (level)
  starting transfers between devices: 31.5 us -> 26.5 us
  waiting for transfers between devices: 30.2 us -> 34 us
    all_to_all x2, waiting for transfers between devices: 5.98 us -> 21.4 us  [exchange_z(): return lax.all_to_all(x, 'col', 0, 0, axis_index_groups=ZG, tiled=True)]
    ppermute x6, waiting for transfers between devices: 13.5 us -> 5.38 us  [along_y(): lax.ppermute(x, 'col', [(4 * z + y, 4 * z + (y + by) % 4) for z in range(...]
    all_to_all x2, starting transfers between devices: 15.4 us -> 11.9 us  [exchange_z(): return lax.all_to_all(x, 'col', 0, 0, axis_index_groups=ZG, tiled=True)]
    ppermute x3, waiting for transfers between devices: 8.93 us -> 5.79 us  [along_x(): return lax.ppermute(x, 'row', [(i, (i + 2 * by) % 8) for i in range(8)])]
    ppermute x6, starting transfers between devices: 10.9 us -> 9.32 us  [along_y(): lax.ppermute(x, 'col', [(4 * z + y, 4 * z + (y + by) % 4) for z in range(...]
where the time goes in v5:
time: 107 us; the launch traced here: 106 us
  Pallas kernels  41.4 us (39%)
  waiting for transfers between devices  34 us (32%)
  starting transfers between devices  26.5 us (25%)
  local copies, waits for them, and re-layouts  2.31 us (2%)
  other arithmetic  1.39 us (1%)
    pallas_call x1, Pallas kernels, main(): pl.pallas_call(main_kernel, out_shape=[jax.ShapeDtypeStruct((8, FIRST * 7...  30 us
    all_to_all x2, waiting for transfers between devices, exchange_z(): return lax.all_to_all(x, 'col', 0, 0, axis_index_groups=ZG, tiled=True)  21.4 us
    all_to_all x2, starting transfers between devices, exchange_z(): return lax.all_to_all(x, 'col', 0, 0, axis_index_groups=ZG, tiled=True)  11.9 us
    ppermute x6, starting transfers between devices, along_y(): lax.ppermute(x, 'col', [(4 * z + y, 4 * z + (y + by) % 4) for z in range(...  9.32 us
    ppermute x3, waiting for transfers between devices, along_x(): return lax.ppermute(x, 'row', [(i, (i + 2 * by) % 8) for i in range(8)])  5.79 us
    ppermute x6, waiting for transfers between devices, along_y(): lax.ppermute(x, 'col', [(4 * z + y, 4 * z + (y + by) % 4) for z in range(...  5.38 us
    ppermute x3, starting transfers between devices, along_x(): return lax.ppermute(x, 'row', [(i, (i + 2 * by) % 8) for i in range(8)])  4.15 us
    pallas_call x1, Pallas kernels, final(): pl.pallas_call(final_kernel, out_shape=jax.ShapeDtypeStruct((KC, CR, 72),...  2.63 us
  transfers between devices with their start and end apart: 15, of which 9 were waited for; matrix products, arithmetic and copies ran while one was open for 1% of the time, Pallas kernels for 6%

profile of v5, /device:TPU:2, one launch (start us, length us, event | category | flops | bytes accessed | tf_op | source)
XLA Modules:
  0.0 105.7 jit_solution(9275871665828531968)
XLA Ops:
  0.0 1.9 %shard_map.55.rest_0_ = bf16[288,384]{1,0:T(8,128)(2,1)} custom-call(bf16[48,48,48]{2,1,0:T(8,128)(2,1)} %p_ref.3), custom_call_target="tpu_custom_call" | custom-call | tf_op jit(solution)/shard_map/pallas_call | solution.py:28
  1.9 2.1 %collective-permute-start.2 = (bf16[288,384]{1,0:T(8,128)(2,1)}, bf16[288,384]{1,0:T(8,128)(2,1)S(1)}, u32[]{:S(2)}, u32[]{:S(2)}) collective-permute-start(bf16[288,384]{1,0:T(8,128)(2,1)} %shard_map.55.rest_0_), channel_id=1, source_target_pairs={{0,128},{32,160},{64,192},{96,224},{128,0},{160,32},{192,64},{224,... | collective-permute-start | bytes 663560 | tf_op jit(solution)/shard_map/ppermute | solution.py:246
  4.1 1.6 %collective-permute-start.1 = (bf16[288,384]{1,0:T(8,128)(2,1)}, bf16[288,384]{1,0:T(8,128)(2,1)S(1)}, u32[]{:S(2)}, u32[]{:S(2)}) collective-permute-start(bf16[288,384]{1,0:T(8,128)(2,1)} %shard_map.55.rest_0_), channel_id=1, source_target_pairs={{0,64},{32,96},{64,128},{96,160},{128,192},{160,224},{192,0},{224,... | collective-permute-start | bytes 663560 | tf_op jit(solution)/shard_map/ppermute | solution.py:246
  5.7 0.4 collective-permute-start
  6.1 2.4 %shard_map.56.turned_hbm = bf16[48,48,48]{2,1,0:T(8,128)(2,1)} custom-call(bf16[48,48,48]{2,1,0:T(8,128)(2,1)} %p_ref.3), custom_call_target="tpu_custom_call" | custom-call | flops 10000000 | bytes 2000000 | tf_op jit(solution)/shard_map/pallas_call | solution.py:38
  8.5 1.4 %multiply_bitcast_fusion = (s32[27,48]{1,0:T(8,128)}, s32[27,48]{1,0:T(8,128)}, s32[27,48]{1,0:T(8,128)}) fusion(s32[48,27]{0,1:T(8,128)} %param.9, s32[48]{0:T(128)} %param.8, s32[]{:T(128)S(6)} %axis_index.25, s32[]{:T(128)S(6)} %shift_right_arithmetic.16, s32[48,27]{0,1:T(8,128)} %param.7), kind=kLoop, calls=%fused_computation.11 | loop fusion | flops 53136 | bytes 26120 | tf_op jit(solution)/shard_map/transpose | solution.py:266
  9.9 2.2 %collective-permute-done.2.rest_3_ = bf16[288,384]{1,0:T(8,128)(2,1)S(1)} collective-permute-done((bf16[288,384]{1,0:T(8,128)(2,1)}, bf16[288,384]{1,0:T(8,128)(2,1)S(1)}, u32[]{:S(2)}, u32[]{:S(2)}) %collective-permute-start.2) | collective-permute-done | bytes 221216 | tf_op jit(solution)/shard_map/ppermute | solution.py:246
  12.0 3.6 %collective-permute-done.1.rest_2_ = bf16[288,384]{1,0:T(8,128)(2,1)S(1)} collective-permute-done((bf16[288,384]{1,0:T(8,128)(2,1)}, bf16[288,384]{1,0:T(8,128)(2,1)S(1)}, u32[]{:S(2)}, u32[]{:S(2)}) %collective-permute-start.1) | collective-permute-done | bytes 221216 | tf_op jit(solution)/shard_map/ppermute | solution.py:246
  15.8 0.5 collective-permute-start.4
  16.4 0.4 collective-permute-start.6
  16.8 0.7 collective-permute-done.3.rest_4_
  17.5 0.3 collective-permute-done.5.rest_6_
  17.9 0.3 collective-permute-done.6.rest_7_
  18.2 0.3 copy-done.13
  18.5 0.3 copy-done.14
  18.9 30.0 %shard_map.57 = (bf16[8,20736]{1,0:T(8,128)(2,1)}, bf16[8,20736]{1,0:T(8,128)(2,1)}, bf16[8,20736]{1,0:T(8,128)(2,1)}, bf16[8,20736]{1,0:T(8,128)(2,1)}, bf16[8,352,128]{2,1,0:T(8,128)(2,1)}) custom-call(s32[27,48]{1,0:T(8,128)} %get-tuple-element.22.src, s32[27,48]{1,0:T(8,128)} %get-tuple-element.23.odd, s32[27,48]{1,0:T(8,128)} %get-tuple-element.24.dst, ...), custom_call_target="tpu_custom_call" | custom-call | flops 20000000000 | bytes 10000000 | tf_op jit(solution)/shard_map/pallas_call | solution.py:172
  48.9 1.6 %collective-permute-start.7 = (bf16[8,20736]{1,0:T(8,128)(2,1)}, bf16[8,20736]{1,0:T(8,128)(2,1)S(1)}, u32[]{:S(2)}, u32[]{:S(2)}) collective-permute-start(bf16[8,20736]{1,0:T(8,128)(2,1)} %get-tuple-element.31), channel_id=1, source_target_pairs={{0,1},{1,2},{2,3},{3,0},{4,5},{5,6},{6,7},{7,4},{8,9},{9,10},{10,1... | collective-permute-start | bytes 995336 | tf_op jit(solution)/shard_map/ppermute | solution.py:252
  50.6 2.9 %collective-permute-start.8 = (bf16[8,20736]{1,0:T(8,128)(2,1)}, bf16[8,20736]{1,0:T(8,128)(2,1)S(1)}, u32[]{:S(2)}, u32[]{:S(2)}) collective-permute-start(bf16[8,20736]{1,0:T(8,128)(2,1)} %get-tuple-element.32), channel_id=1, source_target_pairs={{0,2},{1,3},{2,0},{3,1},{4,6},{5,7},{6,4},{7,5},{8,10},{9,11},{10,... | collective-permute-start | bytes 995336 | tf_op jit(solution)/shard_map/ppermute | solution.py:252
  53.5 1.4 %collective-permute-start.9 = (bf16[8,20736]{1,0:T(8,128)(2,1)}, bf16[8,20736]{1,0:T(8,128)(2,1)S(1)}, u32[]{:S(2)}, u32[]{:S(2)}) collective-permute-start(bf16[8,20736]{1,0:T(8,128)(2,1)} %get-tuple-element.33), channel_id=1, source_target_pairs={{0,3},{1,0},{2,1},{3,2},{4,7},{5,4},{6,5},{7,6},{8,11},{9,8},{10,9... | collective-permute-start | bytes 995336 | tf_op jit(solution)/shard_map/ppermute | solution.py:252
  54.9 8.5 %all-to-all-start.1 = ((bf16[8,352,128]{2,1,0:T(8,128)(2,1)}), bf16[8,352,128]{2,1,0:T(8,128)(2,1)S(1)}, u32[]{:S(2)}, u32[]{:S(2)}) async-start(bf16[8,352,128]{2,1,0:T(8,128)(2,1)} %get-tuple-element.34), calls=%async_computation.1 | async-start | bytes 1441792 | tf_op jit(solution)/shard_map/all_to_all | solution.py:255
  63.3 5.4 %collective-permute-done.8.x2 = bf16[8,20736]{1,0:T(8,128)(2,1)S(1)} collective-permute-done((bf16[8,20736]{1,0:T(8,128)(2,1)}, bf16[8,20736]{1,0:T(8,128)(2,1)S(1)}, u32[]{:S(2)}, u32[]{:S(2)}) %collective-permute-start.8) | collective-permute-done | bytes 331808 | tf_op jit(solution)/shard_map/ppermute | solution.py:252
  68.7 0.7 copy-done.6
  69.6 2.6 %shard_map.58 = bf16[8,176,128]{2,1,0:T(8,128)(2,1)} custom-call(bf16[8,20736]{1,0:T(8,128)(2,1)} %get-tuple-element.30.x0, bf16[8,20736]{1,0:T(8,128)(2,1)} %copy-done.5, bf16[8,20736]{1,0:T(8,128)(2,1)} %copy-done.6, bf16[8,20736]{1,0:T(8,128)(2,1)} %copy-done.7), custom_call_target="tpu_custom_call" | custom-call | flops 40000000000 | bytes 10000000 | tf_op jit(solution)/shard_map/pallas_call | solution.py:198
  72.2 12.3 %all-to-all-done.1.x_ref = bf16[8,352,128]{2,1,0:T(8,128)(2,1)S(1)} async-done(((bf16[8,352,128]{2,1,0:T(8,128)(2,1)}), bf16[8,352,128]{2,1,0:T(8,128)(2,1)S(1)}, u32[]{:S(2)}, u32[]{:S(2)}) %all-to-all-start.1) | async-done | bytes 720928 | tf_op jit(solution)/shard_map/all_to_all | solution.py:255
  84.5 3.4 %all-to-all-start = ((bf16[8,176,128]{2,1,0:T(8,128)(2,1)}), bf16[8,176,128]{2,1,0:T(8,128)(2,1)S(1)}, u32[]{:S(2)}, u32[]{:S(2)}) async-start(bf16[8,176,128]{2,1,0:T(8,128)(2,1)} %shard_map.58), calls=%async_computation | async-start | bytes 720896 | tf_op jit(solution)/shard_map/all_to_all | solution.py:255
  88.0 1.9 %shard_map.59 = (bf16[88,128]{1,0:T(8,128)(2,1)}, bf16[88,128]{1,0:T(8,128)(2,1)}, bf16[88,128]{1,0:T(8,128)(2,1)}, bf16[88,128]{1,0:T(8,128)(2,1)}) custom-call(s32[1]{0:T(128)} %bitcast.here, bf16[8,352,128]{2,1,0:T(8,128)(2,1)} %copy-done), custom_call_target="tpu_custom_call" | custom-call | tf_op jit(solution)/shard_map/pallas_call | solution.py:209
  89.8 0.7 collective-permute-start.10
  90.6 1.0 collective-permute-start.11
  91.6 1.6 %collective-permute-start.12 = (bf16[88,128]{1,0:T(8,128)(2,1)}, bf16[88,128]{1,0:T(8,128)(2,1)S(1)}, u32[]{:S(2)}, u32[]{:S(2)}) collective-permute-start(bf16[88,128]{1,0:T(8,128)(2,1)} %get-tuple-element.38), channel_id=1, source_target_pairs={{0,3},{1,0},{2,1},{3,2},{4,7},{5,4},{6,5},{7,6},{8,11},{9,8},{10,9... | collective-permute-start | bytes 67592 | tf_op jit(solution)/shard_map/ppermute | solution.py:252
  93.2 9.1 %all-to-all-done.x_ref = bf16[8,176,128]{2,1,0:T(8,128)(2,1)S(1)} async-done(((bf16[8,176,128]{2,1,0:T(8,128)(2,1)}), bf16[8,176,128]{2,1,0:T(8,128)(2,1)S(1)}, u32[]{:S(2)}, u32[]{:S(2)}) %all-to-all-start) | async-done | bytes 360480 | tf_op jit(solution)/shard_map/all_to_all | solution.py:255
  102.4 0.7 copy-done.1
  103.1 2.6 %shard_map.60 = f32[27,16,72]{2,1,0:T(8,128)} custom-call(s32[1]{0:T(128)} %bitcast.here, bf16[8,176,128]{2,1,0:T(8,128)(2,1)} %copy-done.1, bf16[88,128]{1,0:T(8,128)(2,1)} %get-tuple-element.35.y0, bf16[88,128]{1,0:T(8,128)(2,1)} %copy-done.2, bf16[88,128]{1,0:T(8,128)(2,1)} %copy-done.3, bf16[88,128]{1,0:T(8,128)(2,1)} %copy-done.4), custom_call_target="tpu_custom_call" | custom-call | tf_op jit(solution)/shard_map/pallas_call | solution.py:239
  (35 shorter events, 0.5 us)
Async XLA Ops:
  1.9 10.1 %collective-permute-start.2 = (bf16[288,384]{1,0:T(8,128)(2,1)}, bf16[288,384]{1,0:T(8,128)(2,1)S(1)}, u32[]{:S(2)}, u32[]{:S(2)}) collective-permute-start(bf16[288,384]{1,0:T(8,128)(2,1)} %shard_map.55.rest_0_), channel_id=1, source_target_pairs={{0,128},{32,160},{64,192},{96,224},{128,0},{160,32},{192,64},{224,... | collective-permute-start | bytes 663560 | tf_op jit(solution)/shard_map/ppermute | solution.py:246
  4.1 11.6 %collective-permute-start.1 = (bf16[288,384]{1,0:T(8,128)(2,1)}, bf16[288,384]{1,0:T(8,128)(2,1)S(1)}, u32[]{:S(2)}, u32[]{:S(2)}) collective-permute-start(bf16[288,384]{1,0:T(8,128)(2,1)} %shard_map.55.rest_0_), channel_id=1, source_target_pairs={{0,64},{32,96},{64,128},{96,160},{128,192},{160,224},{192,0},{224,... | collective-permute-start | bytes 663560 | tf_op jit(solution)/shard_map/ppermute | solution.py:246
  5.7 10.0 %collective-permute-start = (bf16[288,384]{1,0:T(8,128)(2,1)}, bf16[288,384]{1,0:T(8,128)(2,1)S(1)}, u32[]{:S(2)}, u32[]{:S(2)}) collective-permute-start(bf16[288,384]{1,0:T(8,128)(2,1)} %shard_map.55.rest_0_), channel_id=1, source_target_pairs={{0,192},{32,224},{64,0},{96,32},{128,64},{160,96},{192,128},{224,1... | collective-permute-start | bytes 663560 | tf_op jit(solution)/shard_map/ppermute | solution.py:246
  12.0 6.1 %copy-start.8 = (bf16[288,384]{1,0:T(8,128)(2,1)}, bf16[288,384]{1,0:T(8,128)(2,1)S(1)}, u32[]{:S(2)}) copy-start(bf16[288,384]{1,0:T(8,128)(2,1)S(1)} %collective-permute-done.2.rest_3_) | copy-start | bytes 663556
  15.6 2.5 %copy-start.9 = (bf16[288,384]{1,0:T(8,128)(2,1)}, bf16[288,384]{1,0:T(8,128)(2,1)S(1)}, u32[]{:S(2)}) copy-start(bf16[288,384]{1,0:T(8,128)(2,1)S(1)} %collective-permute-done.1.rest_2_) | copy-start | bytes 663556
  15.7 2.5 %copy-start.10 = (bf16[288,384]{1,0:T(8,128)(2,1)}, bf16[288,384]{1,0:T(8,128)(2,1)S(1)}, u32[]{:S(2)}) copy-start(bf16[288,384]{1,0:T(8,128)(2,1)S(1)} %collective-permute-done.rest_1_) | copy-start | bytes 663556
  15.7 1.8 %collective-permute-start.3 = (bf16[288,384]{1,0:T(8,128)(2,1)}, bf16[288,384]{1,0:T(8,128)(2,1)S(1)}, u32[]{:S(2)}, u32[]{:S(2)}) collective-permute-start(bf16[288,384]{1,0:T(8,128)(2,1)} %shard_map.55.rest_0_), channel_id=1, source_target_pairs={{0,32},{32,0},{64,96},{96,64},{128,160},{160,128},{192,224},{224,1... | collective-permute-start | bytes 663560 | tf_op jit(solution)/shard_map/ppermute | solution.py:249
  15.8 1.8 %collective-permute-start.4 = (bf16[288,384]{1,0:T(8,128)(2,1)S(1)}, bf16[288,384]{1,0:T(8,128)(2,1)S(1)}, u32[]{:S(2)}, u32[]{:S(2)}) collective-permute-start(bf16[288,384]{1,0:T(8,128)(2,1)S(1)} %collective-permute-done.rest_1_), channel_id=1, source_target_pairs={{0,32},{32,0},{64,96},{96,64},{128,160},{160,128},{192,224},{224,1... | collective-permute-start | bytes 663560 | tf_op jit(solution)/shard_map/ppermute | solution.py:249
  16.2 1.6 %collective-permute-start.5 = (bf16[288,384]{1,0:T(8,128)(2,1)S(1)}, bf16[288,384]{1,0:T(8,128)(2,1)S(1)}, u32[]{:S(2)}, u32[]{:S(2)}) collective-permute-start(bf16[288,384]{1,0:T(8,128)(2,1)S(1)} %collective-permute-done.1.rest_2_), channel_id=1, source_target_pairs={{0,32},{32,0},{64,96},{96,64},{128,160},{160,128},{192,224},{224,1... | collective-permute-start | bytes 663560 | tf_op jit(solution)/shard_map/ppermute | solution.py:249
  16.4 1.8 %collective-permute-start.6 = (bf16[288,384]{1,0:T(8,128)(2,1)S(1)}, bf16[288,384]{1,0:T(8,128)(2,1)S(1)}, u32[]{:S(2)}, u32[]{:S(2)}) collective-permute-start(bf16[288,384]{1,0:T(8,128)(2,1)S(1)} %collective-permute-done.2.rest_3_), channel_id=1, source_target_pairs={{0,32},{32,0},{64,96},{96,64},{128,160},{160,128},{192,224},{224,1... | collective-permute-start | bytes 663560 | tf_op jit(solution)/shard_map/ppermute | solution.py:249
  17.4 0.8 copy-start.11
  17.5 0.7 copy-start.12
  17.8 0.7 copy-start.13
  18.2 0.7 copy-start.14
  48.9 14.4 %collective-permute-start.7 = (bf16[8,20736]{1,0:T(8,128)(2,1)}, bf16[8,20736]{1,0:T(8,128)(2,1)S(1)}, u32[]{:S(2)}, u32[]{:S(2)}) collective-permute-start(bf16[8,20736]{1,0:T(8,128)(2,1)} %get-tuple-element.31), channel_id=1, source_target_pairs={{0,1},{1,2},{2,3},{3,0},{4,5},{5,6},{6,7},{7,4},{8,9},{9,10},{10,1... | collective-permute-start | bytes 995336 | tf_op jit(solution)/shard_map/ppermute | solution.py:252
  50.6 18.1 %collective-permute-start.8 = (bf16[8,20736]{1,0:T(8,128)(2,1)}, bf16[8,20736]{1,0:T(8,128)(2,1)S(1)}, u32[]{:S(2)}, u32[]{:S(2)}) collective-permute-start(bf16[8,20736]{1,0:T(8,128)(2,1)} %get-tuple-element.32), channel_id=1, source_target_pairs={{0,2},{1,3},{2,0},{3,1},{4,6},{5,7},{6,4},{7,5},{8,10},{9,11},{10,... | collective-permute-start | bytes 995336 | tf_op jit(solution)/shard_map/ppermute | solution.py:252
  53.5 15.2 %collective-permute-start.9 = (bf16[8,20736]{1,0:T(8,128)(2,1)}, bf16[8,20736]{1,0:T(8,128)(2,1)S(1)}, u32[]{:S(2)}, u32[]{:S(2)}) collective-permute-start(bf16[8,20736]{1,0:T(8,128)(2,1)} %get-tuple-element.33), channel_id=1, source_target_pairs={{0,3},{1,0},{2,1},{3,2},{4,7},{5,4},{6,5},{7,6},{8,11},{9,8},{10,9... | collective-permute-start | bytes 995336 | tf_op jit(solution)/shard_map/ppermute | solution.py:252
  54.9 29.6 %all-to-all-start.1 = ((bf16[8,352,128]{2,1,0:T(8,128)(2,1)}), bf16[8,352,128]{2,1,0:T(8,128)(2,1)S(1)}, u32[]{:S(2)}, u32[]{:S(2)}) async-start(bf16[8,352,128]{2,1,0:T(8,128)(2,1)} %get-tuple-element.34), calls=%async_computation.1 | async-start | bytes 1441792 | tf_op jit(solution)/shard_map/all_to_all | solution.py:255
  63.3 5.4 %copy-start.5 = (bf16[8,20736]{1,0:T(8,128)(2,1)}, bf16[8,20736]{1,0:T(8,128)(2,1)S(1)}, u32[]{:S(2)}) copy-start(bf16[8,20736]{1,0:T(8,128)(2,1)S(1)} %collective-permute-done.7.x1) | copy-start | bytes 995332
  68.7 0.7 copy-start.6
  68.7 0.9 copy-start.7
  84.5 3.5 %copy-start = (bf16[8,352,128]{2,1,0:T(8,128)(2,1)}, bf16[8,352,128]{2,1,0:T(8,128)(2,1)S(1)}, u32[]{:S(2)}) copy-start(bf16[8,352,128]{2,1,0:T(8,128)(2,1)S(1)} %all-to-all-done.1.x_ref) | copy-start | bytes 2162692
  84.5 17.8 %all-to-all-start = ((bf16[8,176,128]{2,1,0:T(8,128)(2,1)}), bf16[8,176,128]{2,1,0:T(8,128)(2,1)S(1)}, u32[]{:S(2)}, u32[]{:S(2)}) async-start(bf16[8,176,128]{2,1,0:T(8,128)(2,1)} %shard_map.58), calls=%async_computation | async-start | bytes 720896 | tf_op jit(solution)/shard_map/all_to_all | solution.py:255
  89.8 12.5 %collective-permute-start.10 = (bf16[88,128]{1,0:T(8,128)(2,1)}, bf16[88,128]{1,0:T(8,128)(2,1)S(1)}, u32[]{:S(2)}, u32[]{:S(2)}) collective-permute-start(bf16[88,128]{1,0:T(8,128)(2,1)} %get-tuple-element.36), channel_id=1, source_target_pairs={{0,1},{1,2},{2,3},{3,0},{4,5},{5,6},{6,7},{7,4},{8,9},{9,10},{10,1... | collective-permute-start | bytes 67592 | tf_op jit(solution)/shard_map/ppermute | solution.py:252
  90.6 11.8 %collective-permute-start.11 = (bf16[88,128]{1,0:T(8,128)(2,1)}, bf16[88,128]{1,0:T(8,128)(2,1)S(1)}, u32[]{:S(2)}, u32[]{:S(2)}) collective-permute-start(bf16[88,128]{1,0:T(8,128)(2,1)} %get-tuple-element.37), channel_id=1, source_target_pairs={{0,2},{1,3},{2,0},{3,1},{4,6},{5,7},{6,4},{7,5},{8,10},{9,11},{10,... | collective-permute-start | bytes 67592 | tf_op jit(solution)/shard_map/ppermute | solution.py:252
  91.6 10.7 %collective-permute-start.12 = (bf16[88,128]{1,0:T(8,128)(2,1)}, bf16[88,128]{1,0:T(8,128)(2,1)S(1)}, u32[]{:S(2)}, u32[]{:S(2)}) collective-permute-start(bf16[88,128]{1,0:T(8,128)(2,1)} %get-tuple-element.38), channel_id=1, source_target_pairs={{0,3},{1,0},{2,1},{3,2},{4,7},{5,4},{6,5},{7,6},{8,11},{9,8},{10,9... | collective-permute-start | bytes 67592 | tf_op jit(solution)/shard_map/ppermute | solution.py:252
  102.3 0.7 copy-start.1
  102.3 0.7 copy-start.2
  102.3 0.7 copy-start.3
  102.3 0.7 copy-start.4

commit v6 on v5

--- a/solution.py
+++ b/solution.py
@@ -13,12 +13,12 @@
 SPLIT = ((1, 0), (1, 1), (4, 0), (4, 1))
 
 T = KC * CR
-FIRST = 288
+FIRST = 336
 REST = T - FIRST
 ROWS1 = FIRST * 72 // 128
-PAD1 = 176
+PAD1 = 192
 ROWS2 = REST * 72 // 128
-PAD2 = 88
+PAD2 = 56
 
 def pack_kernel(p_ref, o_ref):
     for g in range(R // 8):
@@ -27,35 +27,42 @@
 def pack(p):
     return pl.pallas_call(pack_kernel, out_shape=jax.ShapeDtypeStruct((R // 8 * B, 8 * B), bf))(p)
 
-def turn_kernel(p_ref, o_ref):
+def placing(n, step, off):
+    row = lax.broadcasted_iota(jnp.int32, (n * 128, 384), 0)
+    col = lax.broadcasted_iota(jnp.int32, (n * 128, 384), 1)
+    t, c = col // step, col % step
+    return (row == (t // 2) * 128 + (t % 2) * B + off + c).astype(f32).astype(bf)
+
+def turn_kernel(p_ref, o_ref, full_ref, half_ref):
     row = lax.broadcasted_iota(jnp.int32, (B, B), 0)
     a = lax.broadcasted_iota(jnp.int32, (B, B), 1)
     pick = (row == (a % 6) * 8 + a // 6).astype(f32).astype(bf)
     for i in range(R):
         o_ref[i] = lax.dot_general(pick, p_ref[i], (((1,), (1,)), ((), ())), preferred_element_type=f32).astype(bf)
+    full_ref[...] = placing(4, B, 0)
+    for h in range(2):
+        half_ref[h] = placing(8, HALF, h * HALF)
 
 def turn(p):
-    return pl.pallas_call(turn_kernel, out_shape=jax.ShapeDtypeStruct((R, B, B), bf),
+    return pl.pallas_call(turn_kernel, out_shape=[jax.ShapeDtypeStruct((R, B, B), bf), jax.ShapeDtypeStruct((512, 384), bf),
+                                                  jax.ShapeDtypeStruct((2, 1024, 384), bf)],
                           cost_estimate=pl.CostEstimate(flops=10**7, bytes_accessed=2 * 10**6, transcendentals=0))(p)
 
-def place_kernel_matrix(n, step, off):
-    row = lax.broadcasted_iota(jnp.int32, (n * 128, 384), 0)
-    col = lax.broadcasted_iota(jnp.int32, (n * 128, 384), 1)
-    t, c = col // step, col % step
-    return (row == (t // 2) * 128 + (t % 2) * B + off + c).astype(f32).astype(bf)
-
-def main_kernel(src, odd, dst, here, blk_hbm, turned_hbm, *rest):
+def main_kernel(src, odd, dst, here, blk_hbm, turned_hbm, full_hbm, half_hbm, *rest):
     pieces, sends, out2, (stage, out, buf2, osems, blk, turned, tile, lo, hi, bufa, bufb, only, full_ref, half_ref, sems, psems) = (
         rest[:8], rest[8:12], rest[12], rest[13:])
-    first = [pltpu.make_async_copy(piece, stage.at[n], psems.at[n]) for n, piece in enumerate(pieces)]
+    first = [pltpu.make_async_copy(piece, stage.at[pl.ds(n * (R // 8 * B), R // 8 * B)], psems.at[n]) for n, piece in enumerate(pieces)]
     first.append(pltpu.make_async_copy(turned_hbm, turned, psems.at[8]))
     CH = 4
     def copy(n):
         return pltpu.make_async_copy(blk_hbm.at[pl.ds(n * CH, CH)], blk.at[pl.ds(n * CH, CH)], sems.at[n])
+    late = [pltpu.make_async_copy(full_hbm, full_ref, psems.at[9]), pltpu.make_async_copy(half_hbm, half_ref, psems.at[10])]
     for c in first:
         c.start()
     for n in range(R // CH):
         copy(n).start()
+    for c in late:
+        c.start()
 
     def zero(n, c):
         z = pl.multiple_of(n * 384, 8)
@@ -66,9 +73,6 @@
     lane = lax.broadcasted_iota(jnp.int32, (32, 128), 1)
     row = lax.broadcasted_iota(jnp.int32, (32, 128), 0)
     only[...] = ((lane >= B * (row // 16)) & (lane < B * (row // 16) + B)).astype(f32).astype(bf)
-    full_ref[...] = place_kernel_matrix(4, B, 0)
-    for h in range(2):
-        half_ref[h] = place_kernel_matrix(8, HALF, h * HALF)
 
     picks = []
     for p in range(4):
@@ -80,13 +84,16 @@
         keep = (l1 < 2 * B) & (l0 == l1)
         change = (other >= 0) & (other < 2 * B) & (l0 == jnp.where(other < B, other + B, other - B))
         picks.append((start, wide, (keep | change).astype(f32).astype(bf)))
-    for n in range(8):
-        first[n].wait()
+    side = R // 8 * B
+    for q in range(2):
+        for n in range(4 * q, 4 * q + 4):
+            first[n].wait()
         for p, (start, wide, pick) in enumerate(picks):
-            x = jnp.dot(stage[n, :, start:start + wide], pick, preferred_element_type=f32).astype(bf)
-            at = (4 * n + p) * (R // 8 * B)
-            tile[at:at + R // 8 * B, :] = x[:, :128]
-            tile[TILE + at:TILE + at + R // 8 * B, :] = x[:, 128:]
+            x = stage[4 * q * side:4 * (q + 1) * side, start:start + wide]
+            x = jnp.dot(x, pick, preferred_element_type=f32).astype(bf)
+            at = (2 * p + q) * 4 * side
+            tile[at:at + 4 * side, :] = x[:, :128]
+            tile[TILE + at:TILE + at + 4 * side, :] = x[:, 128:]
     first[8].wait()
 
     def phase1(i, n, buf):
@@ -136,52 +143,53 @@
                 at = (t2 + g * each + n) * B + 8 * u
                 rows_.append(lo[at:at + 8, :] + hi[at:at + 8, :])
             cols_.append(jnp.concatenate(rows_, axis=0).astype(bf))
-        return jnp.concatenate(cols_, axis=1)
-    gf, gh = 18, 9
-    def put(b, y, half, x):
-        for g in range(gh if half else gf):
-            for w in range(3):
-                v = x[8 * g:8 * g + 8, w * 128:w * 128 + 128]
-                if b < 2:
-                    at = ((FIRST * B // 128 if half else 0) + (b * (gh if half else gf) + g) * 3 + w) * 128
-                    out[y, :, at:at + 128] = v.astype(bf)
+        return cols_
+    def pack_rows(t, y, half, xs, place):
+        step = B if half else 2 * B
+        for w in range(3):
+            n0, n1 = 128 * w // step, (128 * w + 127) // step + 1
+            x = jnp.dot(jnp.concatenate(xs[n0:n1], axis=1), place[n0 * 128:n1 * 128, w * 128:w * 128 + 128], preferred_element_type=f32)
+            for g in range(x.shape[0] // 8):
+                v = x[8 * g:8 * g + 8, :]
+                if t < FIRST:
+                    at = (FIRST * B // 128 + t * HALF // 128 if half else t * B // 128) + g * 3 + w
+                    out[y, :, at * 128:at * 128 + 128] = v.astype(bf)
                 else:
-                    r = y * PAD2 + (REST * B // 128 if half else 0) + g * 3 + w
-                    buf2[pl.ds(r, 8, stride=4 * PAD2), :] = v
+                    buf2[pl.ds(y * PAD2 + (REST * B // 128 if half else 0) + g * 3 + w, 8, stride=4 * PAD2), :] = v
     away = [pltpu.make_async_copy(out.at[(here[0] + d) & 3], sends[d], osems.at[d]) for d in range(4)]
-    for b in range(3):
-        t2 = b * (gf * 4)
+    for c in late:
+        c.wait()
+    for t, count in ((FIRST, REST), (0, FIRST)):
         for y, u in enumerate(FULL):
-            put(b, y, False, jnp.dot(gathered(t2, u, 4, gf), full_ref[...], preferred_element_type=f32))
+            pack_rows(t, y, False, gathered(t // 2, u, 4, count // 8), full_ref)
         for u in (1, 4):
-            x0 = gathered(t2, u, 8, gh)
+            xs = gathered(t // 2, u, 8, count // 16)
             for y, (v, h) in enumerate(SPLIT):
                 if v == u:
-                    put(b, y, True, jnp.dot(x0, half_ref[h], preferred_element_type=f32))
-        if b == 1:
-            for c in away:
-                c.start()
+                    pack_rows(t, y, True, xs, half_ref.at[h])
+    for c in away:
+        c.start()
     for z in range(8):
         out2[z] = buf2[z * 4 * PAD2:(z + 1) * 4 * PAD2, :].astype(bf)
     for c in away:
         c.wait()
 
-def main(src, odd, dst, here, blocks, turned, pieces):
+def main(src, odd, dst, here, blocks, turned, full, half, pieces):
     hbm = pl.BlockSpec(memory_space=pl.ANY)
     vmem = pl.BlockSpec(memory_space=pltpu.VMEM)
     return pl.pallas_call(
         main_kernel,
         out_shape=[jax.ShapeDtypeStruct((8, FIRST * 72), bf)] * 4 + [jax.ShapeDtypeStruct((8, 4 * PAD2, 128), bf)],
-        in_specs=[pl.BlockSpec(memory_space=pltpu.SMEM)] * 4 + [hbm] * 10,
+        in_specs=[pl.BlockSpec(memory_space=pltpu.SMEM)] * 4 + [hbm] * 12,
         out_specs=[hbm] * 4 + [vmem],
-        scratch_shapes=[pltpu.VMEM((8, R // 8 * B, 8 * B), bf), pltpu.VMEM((4, 8, FIRST * 72), bf), pltpu.VMEM((8 * 4 * PAD2, 128), f32), pltpu.SemaphoreType.DMA((4,)),
+        scratch_shapes=[pltpu.VMEM((8 * (R // 8 * B), 8 * B), bf), pltpu.VMEM((4, 8, FIRST * 72), bf), pltpu.VMEM((8 * 4 * PAD2, 128), f32), pltpu.SemaphoreType.DMA((4,)),
                         pltpu.VMEM((R, K, B, B), bf), pltpu.VMEM((R, B, B), bf), pltpu.VMEM((2 * TILE, 128), bf)]
             + [pltpu.VMEM((T // 2 * B, 128), f32)] * 2 + [pltpu.VMEM((B, PAIRS * 256), bf)] * 2
             + [pltpu.VMEM((32, 128), bf), pltpu.VMEM((512, 384), bf), pltpu.VMEM((2, 1024, 384), bf)]
-            + [pltpu.SemaphoreType.DMA((12,)), pltpu.SemaphoreType.DMA((9,))],
+            + [pltpu.SemaphoreType.DMA((12,)), pltpu.SemaphoreType.DMA((11,))],
         compiler_params=pltpu.CompilerParams(vmem_limit_bytes=58 << 20),
         cost_estimate=pl.CostEstimate(flops=2 * 10**10, bytes_accessed=10**7, transcendentals=0),
-    )(src, odd, dst, here, blocks, turned, *pieces)
+    )(src, odd, dst, here, blocks, turned, full, half, *pieces)
 
 def sum_y_kernel(x0, x1, x2, x3, o_ref, buf):
     def body(b, c):
@@ -190,7 +198,7 @@
             x2[:, pl.ds(at, 128)].astype(f32) + x3[:, pl.ds(at, 128)].astype(f32))
         buf[pl.ds(b, 8, stride=PAD1), :] = s
         return c
-    lax.fori_loop(0, ROWS1, body, 0, unroll=18)
+    lax.fori_loop(0, ROWS1, body, 0, unroll=21)
     for z in range(8):
         o_ref[z] = buf[z * PAD1:(z + 1) * PAD1, :].astype(bf)
 
@@ -260,7 +268,7 @@
     apart = ((owner >> 1) - (row >> 1)) & 3
     piece = jnp.where(apart == 3, 2, jnp.where(apart == 2, 3, apart)) + 4 * ((owner ^ row) & 1)
     t = columns % R
-    at = piece * (R // 2) + ((t & 7) >> 1) * (R // 8) + (t >> 3)
+    at = ((t & 7) >> 1) * R + piece * (R // 8) + (t >> 3)
     target = slots * CR + aggregate[:, None]
     odd = target & 1
     return (at * B + ((t ^ odd) & 1) * TILE).T, (odd * 16).T, ((target >> 1) * B).T
@@ -270,10 +278,10 @@
     mine = [packed, along_x(packed, -1), along_x(packed, 1), along_x(packed, 2)]
     index = indices(columns, aggregate, slots)
     turned = turn(prolong)
-    *near, turned, index = lax.optimization_barrier((*mine, turned, index))
+    near, turned, index = lax.optimization_barrier((mine, turned, index))
     pieces = near + [across(x) for x in near]
     here = (lax.axis_index("col") & 3).reshape(1)
-    *sends, other = main(*index, here, blocks, turned, pieces)
+    *sends, other = main(*index, here, blocks, *turned, pieces)
     parts = [sends[0]] + [along_y(sends[d], d) for d in range(1, 4)]
     other = sum_z(here, exchange_z(other))
     first = exchange_z(sum_y(parts))

time: 107 us -> 101 us (0.944)
  waiting for transfers between devices: 34 us -> 25.4 us
  starting transfers between devices: 26.5 us -> 29.1 us
    all_to_all x2, waiting for transfers between devices: 21.4 us -> 9.16 us  [exchange_z(): return lax.all_to_all(x, 'col', 0, 0, axis_index_groups=ZG, tiled=True)]
    ppermute x6, waiting for transfers between devices: 5.38 us -> 10.1 us  [along_y(): lax.ppermute(x, 'col', [(4 * z + y, 4 * z + (y + by) % 4) for z in range(...]
    ppermute x6, starting transfers between devices: 9.32 us -> 10.9 us  [along_y(): lax.ppermute(x, 'col', [(4 * z + y, 4 * z + (y + by) % 4) for z in range(...]
    ppermute x3, waiting for transfers between devices: 5.79 us -> 4.71 us  [along_x(): return lax.ppermute(x, 'row', [(i, (i + 2 * by) % 8) for i in range(8)])]
    pallas_call x1, Pallas kernels: 2.37 us -> 3.45 us  [turn(): pl.pallas_call(turn_kernel, out_shape=[jax.ShapeDtypeStruct((R, B, B), bf...]
  transfers between devices with their start and end apart: 15 -> 15, of which waited for: 9 -> 12; matrix products, arithmetic and copies ran while one was open for 1% -> 1% of each run, Pallas kernels for 6% -> 8%
where the time goes in v6:
time: 101 us
  Pallas kernels  42.4 us (42%)
  starting transfers between devices  29.1 us (29%)
  waiting for transfers between devices  25.4 us (25%)
  local copies, waits for them, and re-layouts  2.33 us (2%)
  other arithmetic  1.39 us (1%)
    pallas_call x1, Pallas kernels, main(): pl.pallas_call(main_kernel, out_shape=[jax.ShapeDtypeStruct((8, FIRST * 7...  29.7 us
    all_to_all x2, starting transfers between devices, exchange_z(): return lax.all_to_all(x, 'col', 0, 0, axis_index_groups=ZG, tiled=True)  13 us
    ppermute x6, starting transfers between devices, along_y(): lax.ppermute(x, 'col', [(4 * z + y, 4 * z + (y + by) % 4) for z in range(...  10.9 us
    ppermute x6, waiting for transfers between devices, along_y(): lax.ppermute(x, 'col', [(4 * z + y, 4 * z + (y + by) % 4) for z in range(...  10.1 us
    all_to_all x2, waiting for transfers between devices, exchange_z(): return lax.all_to_all(x, 'col', 0, 0, axis_index_groups=ZG, tiled=True)  9.16 us
    ppermute x3, waiting for transfers between devices, along_x(): return lax.ppermute(x, 'row', [(i, (i + 2 * by) % 8) for i in range(8)])  4.71 us
    ppermute x3, starting transfers between devices, along_x(): return lax.ppermute(x, 'row', [(i, (i + 2 * by) % 8) for i in range(8)])  4.15 us
    pallas_call x1, Pallas kernels, turn(): pl.pallas_call(turn_kernel, out_shape=[jax.ShapeDtypeStruct((R, B, B), bf...  3.45 us
  transfers between devices with their start and end apart: 15, of which 12 were waited for; matrix products, arithmetic and copies ran while one was open for 1% of the time, Pallas kernels for 8%

profile of v6, /device:TPU:2, one launch (start us, length us, event | category | flops | bytes accessed | tf_op | source)
XLA Modules:
  0.0 100.7 jit_solution(1227503249796179153)
XLA Ops:
  0.0 1.9 %shard_map.55.rest_0_ = bf16[288,384]{1,0:T(8,128)(2,1)} custom-call(bf16[48,48,48]{2,1,0:T(8,128)(2,1)} %p_ref.3), custom_call_target="tpu_custom_call" | custom-call | tf_op jit(solution)/shard_map/pallas_call | solution.py:28
  1.9 2.1 %collective-permute-start.2 = (bf16[288,384]{1,0:T(8,128)(2,1)}, bf16[288,384]{1,0:T(8,128)(2,1)S(1)}, u32[]{:S(2)}, u32[]{:S(2)}) collective-permute-start(bf16[288,384]{1,0:T(8,128)(2,1)} %shard_map.55.rest_0_), channel_id=1, source_target_pairs={{0,128},{32,160},{64,192},{96,224},{128,0},{160,32},{192,64},{224,... | collective-permute-start | bytes 663560 | tf_op jit(solution)/shard_map/ppermute | solution.py:254
  4.1 1.6 %collective-permute-start.1 = (bf16[288,384]{1,0:T(8,128)(2,1)}, bf16[288,384]{1,0:T(8,128)(2,1)S(1)}, u32[]{:S(2)}, u32[]{:S(2)}) collective-permute-start(bf16[288,384]{1,0:T(8,128)(2,1)} %shard_map.55.rest_0_), channel_id=1, source_target_pairs={{0,64},{32,96},{64,128},{96,160},{128,192},{160,224},{192,0},{224,... | collective-permute-start | bytes 663560 | tf_op jit(solution)/shard_map/ppermute | solution.py:254
  5.7 0.4 collective-permute-start
  6.1 3.4 %shard_map.56 = (bf16[48,48,48]{2,1,0:T(8,128)(2,1)}, bf16[512,384]{1,0:T(8,128)(2,1)}, bf16[2,1024,384]{2,1,0:T(8,128)(2,1)}) custom-call(bf16[48,48,48]{2,1,0:T(8,128)(2,1)} %p_ref.3), custom_call_target="tpu_custom_call" | custom-call | flops 10000000 | bytes 2000000 | tf_op jit(solution)/shard_map/pallas_call | solution.py:47
  9.5 1.4 %multiply_bitcast_fusion = (s32[27,48]{1,0:T(8,128)}, s32[27,48]{1,0:T(8,128)}, s32[27,48]{1,0:T(8,128)}) fusion(s32[48,27]{0,1:T(8,128)} %param.9, s32[48]{0:T(128)} %param.8, s32[]{:T(128)S(6)} %axis_index.25, s32[]{:T(128)S(6)} %shift_right_arithmetic.17, s32[48,27]{0,1:T(8,128)} %param.7), kind=kLoop, calls=%fused_computation.11 | loop fusion | flops 53136 | bytes 26120 | tf_op jit(solution)/shard_map/transpose | solution.py:274
  10.9 1.1 %collective-permute-done.2.rest_3_ = bf16[288,384]{1,0:T(8,128)(2,1)S(1)} collective-permute-done((bf16[288,384]{1,0:T(8,128)(2,1)}, bf16[288,384]{1,0:T(8,128)(2,1)S(1)}, u32[]{:S(2)}, u32[]{:S(2)}) %collective-permute-start.2) | collective-permute-done | bytes 221216 | tf_op jit(solution)/shard_map/ppermute | solution.py:254
  12.0 3.6 %collective-permute-done.1.rest_2_ = bf16[288,384]{1,0:T(8,128)(2,1)S(1)} collective-permute-done((bf16[288,384]{1,0:T(8,128)(2,1)}, bf16[288,384]{1,0:T(8,128)(2,1)S(1)}, u32[]{:S(2)}, u32[]{:S(2)}) %collective-permute-start.1) | collective-permute-done | bytes 221216 | tf_op jit(solution)/shard_map/ppermute | solution.py:254
  15.8 0.5 collective-permute-start.4
  16.4 0.4 collective-permute-start.6
  16.8 0.7 collective-permute-done.3.rest_4_
  17.9 0.3 collective-permute-done.6.rest_7_
  18.2 0.3 copy-done.13
  18.9 29.7 %shard_map.57 = (bf16[8,24192]{1,0:T(8,128)(2,1)}, bf16[8,24192]{1,0:T(8,128)(2,1)}, bf16[8,24192]{1,0:T(8,128)(2,1)}, bf16[8,24192]{1,0:T(8,128)(2,1)}, bf16[8,224,128]{2,1,0:T(8,128)(2,1)}) custom-call(s32[27,48]{1,0:T(8,128)} %get-tuple-element.30.src, s32[27,48]{1,0:T(8,128)} %get-tuple-element.31.odd, s32[27,48]{1,0:T(8,128)} %get-tuple-element.32.dst, ...), custom_call_target="tpu_custom_call" | custom-call | flops 20000000000 | bytes 10000000 | tf_op jit(solution)/shard_map/pallas_call | solution.py:180
  48.5 1.7 %collective-permute-start.7 = (bf16[8,24192]{1,0:T(8,128)(2,1)}, bf16[8,24192]{1,0:T(8,128)(2,1)S(1)}, u32[]{:S(2)}, u32[]{:S(2)}) collective-permute-start(bf16[8,24192]{1,0:T(8,128)(2,1)} %get-tuple-element.41), channel_id=1, source_target_pairs={{0,1},{1,2},{2,3},{3,0},{4,5},{5,6},{6,7},{7,4},{8,9},{9,10},{10,1... | collective-permute-start | bytes 1161224 | tf_op jit(solution)/shard_map/ppermute | solution.py:260
  50.2 2.9 %collective-permute-start.8 = (bf16[8,24192]{1,0:T(8,128)(2,1)}, bf16[8,24192]{1,0:T(8,128)(2,1)S(1)}, u32[]{:S(2)}, u32[]{:S(2)}) collective-permute-start(bf16[8,24192]{1,0:T(8,128)(2,1)} %get-tuple-element.42), channel_id=1, source_target_pairs={{0,2},{1,3},{2,0},{3,1},{4,6},{5,7},{6,4},{7,5},{8,10},{9,11},{10,... | collective-permute-start | bytes 1161224 | tf_op jit(solution)/shard_map/ppermute | solution.py:260
  53.1 1.3 %collective-permute-start.9 = (bf16[8,24192]{1,0:T(8,128)(2,1)}, bf16[8,24192]{1,0:T(8,128)(2,1)S(1)}, u32[]{:S(2)}, u32[]{:S(2)}) collective-permute-start(bf16[8,24192]{1,0:T(8,128)(2,1)} %get-tuple-element.43), channel_id=1, source_target_pairs={{0,3},{1,0},{2,1},{3,2},{4,7},{5,4},{6,5},{7,6},{8,11},{9,8},{10,9... | collective-permute-start | bytes 1161224 | tf_op jit(solution)/shard_map/ppermute | solution.py:260
  54.4 8.5 %all-to-all-start.1 = ((bf16[8,224,128]{2,1,0:T(8,128)(2,1)}), bf16[8,224,128]{2,1,0:T(8,128)(2,1)S(1)}, u32[]{:S(2)}, u32[]{:S(2)}) async-start(bf16[8,224,128]{2,1,0:T(8,128)(2,1)} %get-tuple-element.44), calls=%async_computation.1 | async-start | bytes 917504 | tf_op jit(solution)/shard_map/all_to_all | solution.py:263
  62.9 7.7 %collective-permute-done.8.x2 = bf16[8,24192]{1,0:T(8,128)(2,1)S(1)} collective-permute-done((bf16[8,24192]{1,0:T(8,128)(2,1)}, bf16[8,24192]{1,0:T(8,128)(2,1)S(1)}, u32[]{:S(2)}, u32[]{:S(2)}) %collective-permute-start.8) | collective-permute-done | bytes 387104 | tf_op jit(solution)/shard_map/ppermute | solution.py:260
  70.6 0.7 copy-done.6
  71.5 2.9 %shard_map.58 = bf16[8,192,128]{2,1,0:T(8,128)(2,1)} custom-call(bf16[8,24192]{1,0:T(8,128)(2,1)} %get-tuple-element.40.x0, bf16[8,24192]{1,0:T(8,128)(2,1)} %copy-done.5, bf16[8,24192]{1,0:T(8,128)(2,1)} %copy-done.6, bf16[8,24192]{1,0:T(8,128)(2,1)} %copy-done.7), custom_call_target="tpu_custom_call" | custom-call | flops 40000000000 | bytes 10000000 | tf_op jit(solution)/shard_map/pallas_call | solution.py:206
  74.4 4.1 %all-to-all-done.1.x_ref = bf16[8,224,128]{2,1,0:T(8,128)(2,1)S(1)} async-done(((bf16[8,224,128]{2,1,0:T(8,128)(2,1)}), bf16[8,224,128]{2,1,0:T(8,128)(2,1)S(1)}, u32[]{:S(2)}, u32[]{:S(2)}) %all-to-all-start.1) | async-done | bytes 458784 | tf_op jit(solution)/shard_map/all_to_all | solution.py:263
  78.5 4.5 %all-to-all-start = ((bf16[8,192,128]{2,1,0:T(8,128)(2,1)}), bf16[8,192,128]{2,1,0:T(8,128)(2,1)S(1)}, u32[]{:S(2)}, u32[]{:S(2)}) async-start(bf16[8,192,128]{2,1,0:T(8,128)(2,1)} %shard_map.58), calls=%async_computation | async-start | bytes 786432 | tf_op jit(solution)/shard_map/all_to_all | solution.py:263
  83.0 1.7 %shard_map.59 = (bf16[56,128]{1,0:T(8,128)(2,1)}, bf16[56,128]{1,0:T(8,128)(2,1)}, bf16[56,128]{1,0:T(8,128)(2,1)}, bf16[56,128]{1,0:T(8,128)(2,1)}) custom-call(s32[1]{0:T(128)} %bitcast.here, bf16[8,224,128]{2,1,0:T(8,128)(2,1)} %copy-done), custom_call_target="tpu_custom_call" | custom-call | tf_op jit(solution)/shard_map/pallas_call | solution.py:217
  84.7 1.1 %collective-permute-start.10 = (bf16[56,128]{1,0:T(8,128)(2,1)}, bf16[56,128]{1,0:T(8,128)(2,1)S(1)}, u32[]{:S(2)}, u32[]{:S(2)}) collective-permute-start(bf16[56,128]{1,0:T(8,128)(2,1)} %get-tuple-element.46), channel_id=1, source_target_pairs={{0,1},{1,2},{2,3},{3,0},{4,5},{5,6},{6,7},{7,4},{8,9},{9,10},{10,1... | collective-permute-start | bytes 43016 | tf_op jit(solution)/shard_map/ppermute | solution.py:260
  85.8 2.4 %collective-permute-start.11 = (bf16[56,128]{1,0:T(8,128)(2,1)}, bf16[56,128]{1,0:T(8,128)(2,1)S(1)}, u32[]{:S(2)}, u32[]{:S(2)}) collective-permute-start(bf16[56,128]{1,0:T(8,128)(2,1)} %get-tuple-element.47), channel_id=1, source_target_pairs={{0,2},{1,3},{2,0},{3,1},{4,6},{5,7},{6,4},{7,5},{8,10},{9,11},{10,... | collective-permute-start | bytes 43016 | tf_op jit(solution)/shard_map/ppermute | solution.py:260
  88.2 1.5 %collective-permute-start.12 = (bf16[56,128]{1,0:T(8,128)(2,1)}, bf16[56,128]{1,0:T(8,128)(2,1)S(1)}, u32[]{:S(2)}, u32[]{:S(2)}) collective-permute-start(bf16[56,128]{1,0:T(8,128)(2,1)} %get-tuple-element.48), channel_id=1, source_target_pairs={{0,3},{1,0},{2,1},{3,2},{4,7},{5,4},{6,5},{7,6},{8,11},{9,8},{10,9... | collective-permute-start | bytes 43016 | tf_op jit(solution)/shard_map/ppermute | solution.py:260
  89.8 1.4 %collective-permute-done.11.y2 = bf16[56,128]{1,0:T(8,128)(2,1)S(1)} collective-permute-done((bf16[56,128]{1,0:T(8,128)(2,1)}, bf16[56,128]{1,0:T(8,128)(2,1)S(1)}, u32[]{:S(2)}, u32[]{:S(2)}) %collective-permute-start.11) | collective-permute-done | bytes 14368 | tf_op jit(solution)/shard_map/ppermute | solution.py:260
  91.2 0.9 collective-permute-done.12.y3
  92.1 5.1 %all-to-all-done.x_ref = bf16[8,192,128]{2,1,0:T(8,128)(2,1)S(1)} async-done(((bf16[8,192,128]{2,1,0:T(8,128)(2,1)}), bf16[8,192,128]{2,1,0:T(8,128)(2,1)S(1)}, u32[]{:S(2)}, u32[]{:S(2)}) %all-to-all-start) | async-done | bytes 393248 | tf_op jit(solution)/shard_map/all_to_all | solution.py:263
  97.2 0.7 copy-done.1
  98.0 2.7 %shard_map.60 = f32[27,16,72]{2,1,0:T(8,128)} custom-call(s32[1]{0:T(128)} %bitcast.here, bf16[8,192,128]{2,1,0:T(8,128)(2,1)} %copy-done.1, bf16[56,128]{1,0:T(8,128)(2,1)} %get-tuple-element.45.y0, bf16[56,128]{1,0:T(8,128)(2,1)} %copy-done.2, bf16[56,128]{1,0:T(8,128)(2,1)} %copy-done.3, bf16[56,128]{1,0:T(8,128)(2,1)} %copy-done.4), custom_call_target="tpu_custom_call" | custom-call | tf_op jit(solution)/shard_map/pallas_call | solution.py:247
  (35 shorter events, 1.3 us)
Async XLA Ops:
  1.9 10.1 %collective-permute-start.2 = (bf16[288,384]{1,0:T(8,128)(2,1)}, bf16[288,384]{1,0:T(8,128)(2,1)S(1)}, u32[]{:S(2)}, u32[]{:S(2)}) collective-permute-start(bf16[288,384]{1,0:T(8,128)(2,1)} %shard_map.55.rest_0_), channel_id=1, source_target_pairs={{0,128},{32,160},{64,192},{96,224},{128,0},{160,32},{192,64},{224,... | collective-permute-start | bytes 663560 | tf_op jit(solution)/shard_map/ppermute | solution.py:254
  4.1 11.6 %collective-permute-start.1 = (bf16[288,384]{1,0:T(8,128)(2,1)}, bf16[288,384]{1,0:T(8,128)(2,1)S(1)}, u32[]{:S(2)}, u32[]{:S(2)}) collective-permute-start(bf16[288,384]{1,0:T(8,128)(2,1)} %shard_map.55.rest_0_), channel_id=1, source_target_pairs={{0,64},{32,96},{64,128},{96,160},{128,192},{160,224},{192,0},{224,... | collective-permute-start | bytes 663560 | tf_op jit(solution)/shard_map/ppermute | solution.py:254
  5.7 10.0 %collective-permute-start = (bf16[288,384]{1,0:T(8,128)(2,1)}, bf16[288,384]{1,0:T(8,128)(2,1)S(1)}, u32[]{:S(2)}, u32[]{:S(2)}) collective-permute-start(bf16[288,384]{1,0:T(8,128)(2,1)} %shard_map.55.rest_0_), channel_id=1, source_target_pairs={{0,192},{32,224},{64,0},{96,32},{128,64},{160,96},{192,128},{224,1... | collective-permute-start | bytes 663560 | tf_op jit(solution)/shard_map/ppermute | solution.py:254
  12.0 6.1 %copy-start.8 = (bf16[288,384]{1,0:T(8,128)(2,1)}, bf16[288,384]{1,0:T(8,128)(2,1)S(1)}, u32[]{:S(2)}) copy-start(bf16[288,384]{1,0:T(8,128)(2,1)S(1)} %collective-permute-done.2.rest_3_) | copy-start | bytes 663556
  15.6 2.5 %copy-start.9 = (bf16[288,384]{1,0:T(8,128)(2,1)}, bf16[288,384]{1,0:T(8,128)(2,1)S(1)}, u32[]{:S(2)}) copy-start(bf16[288,384]{1,0:T(8,128)(2,1)S(1)} %collective-permute-done.1.rest_2_) | copy-start | bytes 663556
  15.7 2.5 %copy-start.10 = (bf16[288,384]{1,0:T(8,128)(2,1)}, bf16[288,384]{1,0:T(8,128)(2,1)S(1)}, u32[]{:S(2)}) copy-start(bf16[288,384]{1,0:T(8,128)(2,1)S(1)} %collective-permute-done.rest_1_) | copy-start | bytes 663556
  15.7 1.8 %collective-permute-start.3 = (bf16[288,384]{1,0:T(8,128)(2,1)}, bf16[288,384]{1,0:T(8,128)(2,1)S(1)}, u32[]{:S(2)}, u32[]{:S(2)}) collective-permute-start(bf16[288,384]{1,0:T(8,128)(2,1)} %shard_map.55.rest_0_), channel_id=1, source_target_pairs={{0,32},{32,0},{64,96},{96,64},{128,160},{160,128},{192,224},{224,1... | collective-permute-start | bytes 663560 | tf_op jit(solution)/shard_map/ppermute | solution.py:257
  15.8 1.8 %collective-permute-start.4 = (bf16[288,384]{1,0:T(8,128)(2,1)S(1)}, bf16[288,384]{1,0:T(8,128)(2,1)S(1)}, u32[]{:S(2)}, u32[]{:S(2)}) collective-permute-start(bf16[288,384]{1,0:T(8,128)(2,1)S(1)} %collective-permute-done.rest_1_), channel_id=1, source_target_pairs={{0,32},{32,0},{64,96},{96,64},{128,160},{160,128},{192,224},{224,1... | collective-permute-start | bytes 663560 | tf_op jit(solution)/shard_map/ppermute | solution.py:257
  16.2 1.6 %collective-permute-start.5 = (bf16[288,384]{1,0:T(8,128)(2,1)S(1)}, bf16[288,384]{1,0:T(8,128)(2,1)S(1)}, u32[]{:S(2)}, u32[]{:S(2)}) collective-permute-start(bf16[288,384]{1,0:T(8,128)(2,1)S(1)} %collective-permute-done.1.rest_2_), channel_id=1, source_target_pairs={{0,32},{32,0},{64,96},{96,64},{128,160},{160,128},{192,224},{224,1... | collective-permute-start | bytes 663560 | tf_op jit(solution)/shard_map/ppermute | solution.py:257
  16.4 1.8 %collective-permute-start.6 = (bf16[288,384]{1,0:T(8,128)(2,1)S(1)}, bf16[288,384]{1,0:T(8,128)(2,1)S(1)}, u32[]{:S(2)}, u32[]{:S(2)}) collective-permute-start(bf16[288,384]{1,0:T(8,128)(2,1)S(1)} %collective-permute-done.2.rest_3_), channel_id=1, source_target_pairs={{0,32},{32,0},{64,96},{96,64},{128,160},{160,128},{192,224},{224,1... | collective-permute-start | bytes 663560 | tf_op jit(solution)/shard_map/ppermute | solution.py:257
  17.4 0.8 copy-start.11
  17.5 0.7 copy-start.12
  17.8 0.7 copy-start.13
  18.2 0.7 copy-start.14
  48.5 14.4 %collective-permute-start.7 = (bf16[8,24192]{1,0:T(8,128)(2,1)}, bf16[8,24192]{1,0:T(8,128)(2,1)S(1)}, u32[]{:S(2)}, u32[]{:S(2)}) collective-permute-start(bf16[8,24192]{1,0:T(8,128)(2,1)} %get-tuple-element.41), channel_id=1, source_target_pairs={{0,1},{1,2},{2,3},{3,0},{4,5},{5,6},{6,7},{7,4},{8,9},{9,10},{10,1... | collective-permute-start | bytes 1161224 | tf_op jit(solution)/shard_map/ppermute | solution.py:260
  50.2 20.4 %collective-permute-start.8 = (bf16[8,24192]{1,0:T(8,128)(2,1)}, bf16[8,24192]{1,0:T(8,128)(2,1)S(1)}, u32[]{:S(2)}, u32[]{:S(2)}) collective-permute-start(bf16[8,24192]{1,0:T(8,128)(2,1)} %get-tuple-element.42), channel_id=1, source_target_pairs={{0,2},{1,3},{2,0},{3,1},{4,6},{5,7},{6,4},{7,5},{8,10},{9,11},{10,... | collective-permute-start | bytes 1161224 | tf_op jit(solution)/shard_map/ppermute | solution.py:260
  53.1 17.5 %collective-permute-start.9 = (bf16[8,24192]{1,0:T(8,128)(2,1)}, bf16[8,24192]{1,0:T(8,128)(2,1)S(1)}, u32[]{:S(2)}, u32[]{:S(2)}) collective-permute-start(bf16[8,24192]{1,0:T(8,128)(2,1)} %get-tuple-element.43), channel_id=1, source_target_pairs={{0,3},{1,0},{2,1},{3,2},{4,7},{5,4},{6,5},{7,6},{8,11},{9,8},{10,9... | collective-permute-start | bytes 1161224 | tf_op jit(solution)/shard_map/ppermute | solution.py:260
  54.4 24.0 %all-to-all-start.1 = ((bf16[8,224,128]{2,1,0:T(8,128)(2,1)}), bf16[8,224,128]{2,1,0:T(8,128)(2,1)S(1)}, u32[]{:S(2)}, u32[]{:S(2)}) async-start(bf16[8,224,128]{2,1,0:T(8,128)(2,1)} %get-tuple-element.44), calls=%async_computation.1 | async-start | bytes 917504 | tf_op jit(solution)/shard_map/all_to_all | solution.py:263
  62.9 7.7 %copy-start.5 = (bf16[8,24192]{1,0:T(8,128)(2,1)}, bf16[8,24192]{1,0:T(8,128)(2,1)S(1)}, u32[]{:S(2)}) copy-start(bf16[8,24192]{1,0:T(8,128)(2,1)S(1)} %collective-permute-done.7.x1) | copy-start | bytes 1161220
  70.6 0.7 copy-start.6
  70.6 0.9 copy-start.7
  78.5 4.5 %copy-start = (bf16[8,224,128]{2,1,0:T(8,128)(2,1)}, bf16[8,224,128]{2,1,0:T(8,128)(2,1)S(1)}, u32[]{:S(2)}) copy-start(bf16[8,224,128]{2,1,0:T(8,128)(2,1)S(1)} %all-to-all-done.1.x_ref) | copy-start | bytes 1376260
  78.5 18.7 %all-to-all-start = ((bf16[8,192,128]{2,1,0:T(8,128)(2,1)}), bf16[8,192,128]{2,1,0:T(8,128)(2,1)S(1)}, u32[]{:S(2)}, u32[]{:S(2)}) async-start(bf16[8,192,128]{2,1,0:T(8,128)(2,1)} %shard_map.58), calls=%async_computation | async-start | bytes 786432 | tf_op jit(solution)/shard_map/all_to_all | solution.py:263
  84.7 5.1 %collective-permute-start.10 = (bf16[56,128]{1,0:T(8,128)(2,1)}, bf16[56,128]{1,0:T(8,128)(2,1)S(1)}, u32[]{:S(2)}, u32[]{:S(2)}) collective-permute-start(bf16[56,128]{1,0:T(8,128)(2,1)} %get-tuple-element.46), channel_id=1, source_target_pairs={{0,1},{1,2},{2,3},{3,0},{4,5},{5,6},{6,7},{7,4},{8,9},{9,10},{10,1... | collective-permute-start | bytes 43016 | tf_op jit(solution)/shard_map/ppermute | solution.py:260
  85.8 5.4 %collective-permute-start.11 = (bf16[56,128]{1,0:T(8,128)(2,1)}, bf16[56,128]{1,0:T(8,128)(2,1)S(1)}, u32[]{:S(2)}, u32[]{:S(2)}) collective-permute-start(bf16[56,128]{1,0:T(8,128)(2,1)} %get-tuple-element.47), channel_id=1, source_target_pairs={{0,2},{1,3},{2,0},{3,1},{4,6},{5,7},{6,4},{7,5},{8,10},{9,11},{10,... | collective-permute-start | bytes 43016 | tf_op jit(solution)/shard_map/ppermute | solution.py:260
  88.2 3.9 %collective-permute-start.12 = (bf16[56,128]{1,0:T(8,128)(2,1)}, bf16[56,128]{1,0:T(8,128)(2,1)S(1)}, u32[]{:S(2)}, u32[]{:S(2)}) collective-permute-start(bf16[56,128]{1,0:T(8,128)(2,1)} %get-tuple-element.48), channel_id=1, source_target_pairs={{0,3},{1,0},{2,1},{3,2},{4,7},{5,4},{6,5},{7,6},{8,11},{9,8},{10,9... | collective-permute-start | bytes 43016 | tf_op jit(solution)/shard_map/ppermute | solution.py:260
  89.8 7.4 %copy-start.2 = (bf16[56,128]{1,0:T(8,128)(2,1)}, bf16[56,128]{1,0:T(8,128)(2,1)S(1)}, u32[]{:S(2)}) copy-start(bf16[56,128]{1,0:T(8,128)(2,1)S(1)} %collective-permute-done.10.y1) | copy-start | bytes 43012
  91.2 6.0 %copy-start.3 = (bf16[56,128]{1,0:T(8,128)(2,1)}, bf16[56,128]{1,0:T(8,128)(2,1)S(1)}, u32[]{:S(2)}) copy-start(bf16[56,128]{1,0:T(8,128)(2,1)S(1)} %collective-permute-done.11.y2) | copy-start | bytes 43012
  92.1 5.1 %copy-start.4 = (bf16[56,128]{1,0:T(8,128)(2,1)}, bf16[56,128]{1,0:T(8,128)(2,1)S(1)}, u32[]{:S(2)}) copy-start(bf16[56,128]{1,0:T(8,128)(2,1)S(1)} %collective-permute-done.12.y3) | copy-start | bytes 43012
  97.2 0.7 copy-start.1

commit v7 on v6

--- a/solution.py
+++ b/solution.py
@@ -59,10 +59,8 @@
     late = [pltpu.make_async_copy(full_hbm, full_ref, psems.at[9]), pltpu.make_async_copy(half_hbm, half_ref, psems.at[10])]
     for c in first:
         c.start()
-    for n in range(R // CH):
+    for n in range(2):
         copy(n).start()
-    for c in late:
-        c.start()
 
     def zero(n, c):
         z = pl.multiple_of(n * 384, 8)
@@ -88,6 +86,11 @@
     for q in range(2):
         for n in range(4 * q, 4 * q + 4):
             first[n].wait()
+        if q == 1:
+            for n in range(2, R // CH):
+                copy(n).start()
+            for c in late:
+                c.start()
         for p, (start, wide, pick) in enumerate(picks):
             x = stage[4 * q * side:4 * (q + 1) * side, start:start + wide]
             x = jnp.dot(x, pick, preferred_element_type=f32).astype(bf)

time: 101 us -> 98.7 us (0.977)
  Pallas kernels: 42.4 us -> 39.9 us
    pallas_call x1, Pallas kernels: 29.7 us -> 27.1 us  [main(): pl.pallas_call(main_kernel, out_shape=[jax.ShapeDtypeStruct((8, FIRST * 7...]
where the time goes in v7:
time: 98.7 us; the launch traced here: 98 us
  Pallas kernels  39.9 us (40%)
  starting transfers between devices  29.1 us (29%)
  waiting for transfers between devices  25.2 us (26%)
  local copies, waits for them, and re-layouts  2.33 us (2%)
  other arithmetic  1.39 us (1%)
    pallas_call x1, Pallas kernels, main(): pl.pallas_call(main_kernel, out_shape=[jax.ShapeDtypeStruct((8, FIRST * 7...  27.1 us
    all_to_all x2, starting transfers between devices, exchange_z(): return lax.all_to_all(x, 'col', 0, 0, axis_index_groups=ZG, tiled=True)  12.8 us
    ppermute x6, starting transfers between devices, along_y(): lax.ppermute(x, 'col', [(4 * z + y, 4 * z + (y + by) % 4) for z in range(...  11 us
    ppermute x6, waiting for transfers between devices, along_y(): lax.ppermute(x, 'col', [(4 * z + y, 4 * z + (y + by) % 4) for z in range(...  10.1 us
    all_to_all x2, waiting for transfers between devices, exchange_z(): return lax.all_to_all(x, 'col', 0, 0, axis_index_groups=ZG, tiled=True)  9.03 us
    ppermute x3, waiting for transfers between devices, along_x(): return lax.ppermute(x, 'row', [(i, (i + 2 * by) % 8) for i in range(8)])  4.71 us
    ppermute x3, starting transfers between devices, along_x(): return lax.ppermute(x, 'row', [(i, (i + 2 * by) % 8) for i in range(8)])  4.15 us
    pallas_call x1, Pallas kernels, turn(): pl.pallas_call(turn_kernel, out_shape=[jax.ShapeDtypeStruct((R, B, B), bf...  3.45 us
  transfers between devices with their start and end apart: 15, of which 12 were waited for; matrix products, arithmetic and copies ran while one was open for 1% of the time, Pallas kernels for 8%

profile of v7, /device:TPU:2, one launch (start us, length us, event | category | flops | bytes accessed | tf_op | source)
XLA Modules:
  0.0 98.0 jit_solution(15378923012665144086)
XLA Ops:
  0.0 1.9 %shard_map.55.rest_0_ = bf16[288,384]{1,0:T(8,128)(2,1)} custom-call(bf16[48,48,48]{2,1,0:T(8,128)(2,1)} %p_ref.3), custom_call_target="tpu_custom_call" | custom-call | tf_op jit(solution)/shard_map/pallas_call | solution.py:28
  1.9 2.1 %collective-permute-start.2 = (bf16[288,384]{1,0:T(8,128)(2,1)}, bf16[288,384]{1,0:T(8,128)(2,1)S(1)}, u32[]{:S(2)}, u32[]{:S(2)}) collective-permute-start(bf16[288,384]{1,0:T(8,128)(2,1)} %shard_map.55.rest_0_), channel_id=1, source_target_pairs={{0,128},{32,160},{64,192},{96,224},{128,0},{160,32},{192,64},{224,... | collective-permute-start | bytes 663560 | tf_op jit(solution)/shard_map/ppermute | solution.py:257
  4.1 1.6 %collective-permute-start.1 = (bf16[288,384]{1,0:T(8,128)(2,1)}, bf16[288,384]{1,0:T(8,128)(2,1)S(1)}, u32[]{:S(2)}, u32[]{:S(2)}) collective-permute-start(bf16[288,384]{1,0:T(8,128)(2,1)} %shard_map.55.rest_0_), channel_id=1, source_target_pairs={{0,64},{32,96},{64,128},{96,160},{128,192},{160,224},{192,0},{224,... | collective-permute-start | bytes 663560 | tf_op jit(solution)/shard_map/ppermute | solution.py:257
  5.7 0.4 collective-permute-start
  6.1 3.4 %shard_map.56 = (bf16[48,48,48]{2,1,0:T(8,128)(2,1)}, bf16[512,384]{1,0:T(8,128)(2,1)}, bf16[2,1024,384]{2,1,0:T(8,128)(2,1)}) custom-call(bf16[48,48,48]{2,1,0:T(8,128)(2,1)} %p_ref.3), custom_call_target="tpu_custom_call" | custom-call | flops 10000000 | bytes 2000000 | tf_op jit(solution)/shard_map/pallas_call | solution.py:47
  9.5 1.4 %multiply_bitcast_fusion = (s32[27,48]{1,0:T(8,128)}, s32[27,48]{1,0:T(8,128)}, s32[27,48]{1,0:T(8,128)}) fusion(s32[48,27]{0,1:T(8,128)} %param.9, s32[48]{0:T(128)} %param.8, s32[]{:T(128)S(6)} %axis_index.25, s32[]{:T(128)S(6)} %shift_right_arithmetic.17, s32[48,27]{0,1:T(8,128)} %param.7), kind=kLoop, calls=%fused_computation.11 | loop fusion | flops 53136 | bytes 26120 | tf_op jit(solution)/shard_map/transpose | solution.py:277
  10.9 1.1 %collective-permute-done.2.rest_3_ = bf16[288,384]{1,0:T(8,128)(2,1)S(1)} collective-permute-done((bf16[288,384]{1,0:T(8,128)(2,1)}, bf16[288,384]{1,0:T(8,128)(2,1)S(1)}, u32[]{:S(2)}, u32[]{:S(2)}) %collective-permute-start.2) | collective-permute-done | bytes 221216 | tf_op jit(solution)/shard_map/ppermute | solution.py:257
  12.0 3.6 %collective-permute-done.1.rest_2_ = bf16[288,384]{1,0:T(8,128)(2,1)S(1)} collective-permute-done((bf16[288,384]{1,0:T(8,128)(2,1)}, bf16[288,384]{1,0:T(8,128)(2,1)S(1)}, u32[]{:S(2)}, u32[]{:S(2)}) %collective-permute-start.1) | collective-permute-done | bytes 221216 | tf_op jit(solution)/shard_map/ppermute | solution.py:257
  15.8 0.5 collective-permute-start.4
  16.4 0.4 collective-permute-start.6
  16.8 0.7 collective-permute-done.3.rest_4_
  17.5 0.3 collective-permute-done.5.rest_6_
  18.2 0.3 copy-done.13
  18.9 27.1 %shard_map.57 = (bf16[8,24192]{1,0:T(8,128)(2,1)}, bf16[8,24192]{1,0:T(8,128)(2,1)}, bf16[8,24192]{1,0:T(8,128)(2,1)}, bf16[8,24192]{1,0:T(8,128)(2,1)}, bf16[8,224,128]{2,1,0:T(8,128)(2,1)}) custom-call(s32[27,48]{1,0:T(8,128)} %get-tuple-element.30.src, s32[27,48]{1,0:T(8,128)} %get-tuple-element.31.odd, s32[27,48]{1,0:T(8,128)} %get-tuple-element.32.dst, ...), custom_call_target="tpu_custom_call" | custom-call | flops 20000000000 | bytes 10000000 | tf_op jit(solution)/shard_map/pallas_call | solution.py:183
  46.0 1.7 %collective-permute-start.7 = (bf16[8,24192]{1,0:T(8,128)(2,1)}, bf16[8,24192]{1,0:T(8,128)(2,1)S(1)}, u32[]{:S(2)}, u32[]{:S(2)}) collective-permute-start(bf16[8,24192]{1,0:T(8,128)(2,1)} %get-tuple-element.41), channel_id=1, source_target_pairs={{0,1},{1,2},{2,3},{3,0},{4,5},{5,6},{6,7},{7,4},{8,9},{9,10},{10,1... | collective-permute-start | bytes 1161224 | tf_op jit(solution)/shard_map/ppermute | solution.py:263
  47.7 2.9 %collective-permute-start.8 = (bf16[8,24192]{1,0:T(8,128)(2,1)}, bf16[8,24192]{1,0:T(8,128)(2,1)S(1)}, u32[]{:S(2)}, u32[]{:S(2)}) collective-permute-start(bf16[8,24192]{1,0:T(8,128)(2,1)} %get-tuple-element.42), channel_id=1, source_target_pairs={{0,2},{1,3},{2,0},{3,1},{4,6},{5,7},{6,4},{7,5},{8,10},{9,11},{10,... | collective-permute-start | bytes 1161224 | tf_op jit(solution)/shard_map/ppermute | solution.py:263
  50.5 1.4 %collective-permute-start.9 = (bf16[8,24192]{1,0:T(8,128)(2,1)}, bf16[8,24192]{1,0:T(8,128)(2,1)S(1)}, u32[]{:S(2)}, u32[]{:S(2)}) collective-permute-start(bf16[8,24192]{1,0:T(8,128)(2,1)} %get-tuple-element.43), channel_id=1, source_target_pairs={{0,3},{1,0},{2,1},{3,2},{4,7},{5,4},{6,5},{7,6},{8,11},{9,8},{10,9... | collective-permute-start | bytes 1161224 | tf_op jit(solution)/shard_map/ppermute | solution.py:263
  51.9 8.4 %all-to-all-start.1 = ((bf16[8,224,128]{2,1,0:T(8,128)(2,1)}), bf16[8,224,128]{2,1,0:T(8,128)(2,1)S(1)}, u32[]{:S(2)}, u32[]{:S(2)}) async-start(bf16[8,224,128]{2,1,0:T(8,128)(2,1)} %get-tuple-element.44), calls=%async_computation.1 | async-start | bytes 917504 | tf_op jit(solution)/shard_map/all_to_all | solution.py:266
  60.4 7.8 %collective-permute-done.8.x2 = bf16[8,24192]{1,0:T(8,128)(2,1)S(1)} collective-permute-done((bf16[8,24192]{1,0:T(8,128)(2,1)}, bf16[8,24192]{1,0:T(8,128)(2,1)S(1)}, u32[]{:S(2)}, u32[]{:S(2)}) %collective-permute-start.8) | collective-permute-done | bytes 387104 | tf_op jit(solution)/shard_map/ppermute | solution.py:263
  68.2 0.7 copy-done.6
  69.0 2.9 %shard_map.58 = bf16[8,192,128]{2,1,0:T(8,128)(2,1)} custom-call(bf16[8,24192]{1,0:T(8,128)(2,1)} %get-tuple-element.40.x0, bf16[8,24192]{1,0:T(8,128)(2,1)} %copy-done.5, bf16[8,24192]{1,0:T(8,128)(2,1)} %copy-done.6, bf16[8,24192]{1,0:T(8,128)(2,1)} %copy-done.7), custom_call_target="tpu_custom_call" | custom-call | flops 40000000000 | bytes 10000000 | tf_op jit(solution)/shard_map/pallas_call | solution.py:209
  72.0 4.0 %all-to-all-done.1.x_ref = bf16[8,224,128]{2,1,0:T(8,128)(2,1)S(1)} async-done(((bf16[8,224,128]{2,1,0:T(8,128)(2,1)}), bf16[8,224,128]{2,1,0:T(8,128)(2,1)S(1)}, u32[]{:S(2)}, u32[]{:S(2)}) %all-to-all-start.1) | async-done | bytes 458784 | tf_op jit(solution)/shard_map/all_to_all | solution.py:266
  76.0 4.4 %all-to-all-start = ((bf16[8,192,128]{2,1,0:T(8,128)(2,1)}), bf16[8,192,128]{2,1,0:T(8,128)(2,1)S(1)}, u32[]{:S(2)}, u32[]{:S(2)}) async-start(bf16[8,192,128]{2,1,0:T(8,128)(2,1)} %shard_map.58), calls=%async_computation | async-start | bytes 786432 | tf_op jit(solution)/shard_map/all_to_all | solution.py:266
  80.4 1.7 %shard_map.59 = (bf16[56,128]{1,0:T(8,128)(2,1)}, bf16[56,128]{1,0:T(8,128)(2,1)}, bf16[56,128]{1,0:T(8,128)(2,1)}, bf16[56,128]{1,0:T(8,128)(2,1)}) custom-call(s32[1]{0:T(128)} %bitcast.here, bf16[8,224,128]{2,1,0:T(8,128)(2,1)} %copy-done), custom_call_target="tpu_custom_call" | custom-call | tf_op jit(solution)/shard_map/pallas_call | solution.py:220
  82.1 1.1 %collective-permute-start.10 = (bf16[56,128]{1,0:T(8,128)(2,1)}, bf16[56,128]{1,0:T(8,128)(2,1)S(1)}, u32[]{:S(2)}, u32[]{:S(2)}) collective-permute-start(bf16[56,128]{1,0:T(8,128)(2,1)} %get-tuple-element.46), channel_id=1, source_target_pairs={{0,1},{1,2},{2,3},{3,0},{4,5},{5,6},{6,7},{7,4},{8,9},{9,10},{10,1... | collective-permute-start | bytes 43016 | tf_op jit(solution)/shard_map/ppermute | solution.py:263
  83.2 2.4 %collective-permute-start.11 = (bf16[56,128]{1,0:T(8,128)(2,1)}, bf16[56,128]{1,0:T(8,128)(2,1)S(1)}, u32[]{:S(2)}, u32[]{:S(2)}) collective-permute-start(bf16[56,128]{1,0:T(8,128)(2,1)} %get-tuple-element.47), channel_id=1, source_target_pairs={{0,2},{1,3},{2,0},{3,1},{4,6},{5,7},{6,4},{7,5},{8,10},{9,11},{10,... | collective-permute-start | bytes 43016 | tf_op jit(solution)/shard_map/ppermute | solution.py:263
  85.6 1.6 %collective-permute-start.12 = (bf16[56,128]{1,0:T(8,128)(2,1)}, bf16[56,128]{1,0:T(8,128)(2,1)S(1)}, u32[]{:S(2)}, u32[]{:S(2)}) collective-permute-start(bf16[56,128]{1,0:T(8,128)(2,1)} %get-tuple-element.48), channel_id=1, source_target_pairs={{0,3},{1,0},{2,1},{3,2},{4,7},{5,4},{6,5},{7,6},{8,11},{9,8},{10,9... | collective-permute-start | bytes 43016 | tf_op jit(solution)/shard_map/ppermute | solution.py:263
  87.2 1.4 %collective-permute-done.11.y2 = bf16[56,128]{1,0:T(8,128)(2,1)S(1)} collective-permute-done((bf16[56,128]{1,0:T(8,128)(2,1)}, bf16[56,128]{1,0:T(8,128)(2,1)S(1)}, u32[]{:S(2)}, u32[]{:S(2)}) %collective-permute-start.11) | collective-permute-done | bytes 14368 | tf_op jit(solution)/shard_map/ppermute | solution.py:263
  88.6 0.9 collective-permute-done.12.y3
  89.5 5.0 %all-to-all-done.x_ref = bf16[8,192,128]{2,1,0:T(8,128)(2,1)S(1)} async-done(((bf16[8,192,128]{2,1,0:T(8,128)(2,1)}), bf16[8,192,128]{2,1,0:T(8,128)(2,1)S(1)}, u32[]{:S(2)}, u32[]{:S(2)}) %all-to-all-start) | async-done | bytes 393248 | tf_op jit(solution)/shard_map/all_to_all | solution.py:266
  94.5 0.7 copy-done.1
  95.3 2.7 %shard_map.60 = f32[27,16,72]{2,1,0:T(8,128)} custom-call(s32[1]{0:T(128)} %bitcast.here, bf16[8,192,128]{2,1,0:T(8,128)(2,1)} %copy-done.1, bf16[56,128]{1,0:T(8,128)(2,1)} %get-tuple-element.45.y0, bf16[56,128]{1,0:T(8,128)(2,1)} %copy-done.2, bf16[56,128]{1,0:T(8,128)(2,1)} %copy-done.3, bf16[56,128]{1,0:T(8,128)(2,1)} %copy-done.4), custom_call_target="tpu_custom_call" | custom-call | tf_op jit(solution)/shard_map/pallas_call | solution.py:250
  (35 shorter events, 1.2 us)
Async XLA Ops:
  1.9 10.1 %collective-permute-start.2 = (bf16[288,384]{1,0:T(8,128)(2,1)}, bf16[288,384]{1,0:T(8,128)(2,1)S(1)}, u32[]{:S(2)}, u32[]{:S(2)}) collective-permute-start(bf16[288,384]{1,0:T(8,128)(2,1)} %shard_map.55.rest_0_), channel_id=1, source_target_pairs={{0,128},{32,160},{64,192},{96,224},{128,0},{160,32},{192,64},{224,... | collective-permute-start | bytes 663560 | tf_op jit(solution)/shard_map/ppermute | solution.py:257
  4.1 11.6 %collective-permute-start.1 = (bf16[288,384]{1,0:T(8,128)(2,1)}, bf16[288,384]{1,0:T(8,128)(2,1)S(1)}, u32[]{:S(2)}, u32[]{:S(2)}) collective-permute-start(bf16[288,384]{1,0:T(8,128)(2,1)} %shard_map.55.rest_0_), channel_id=1, source_target_pairs={{0,64},{32,96},{64,128},{96,160},{128,192},{160,224},{192,0},{224,... | collective-permute-start | bytes 663560 | tf_op jit(solution)/shard_map/ppermute | solution.py:257
  5.7 10.0 %collective-permute-start = (bf16[288,384]{1,0:T(8,128)(2,1)}, bf16[288,384]{1,0:T(8,128)(2,1)S(1)}, u32[]{:S(2)}, u32[]{:S(2)}) collective-permute-start(bf16[288,384]{1,0:T(8,128)(2,1)} %shard_map.55.rest_0_), channel_id=1, source_target_pairs={{0,192},{32,224},{64,0},{96,32},{128,64},{160,96},{192,128},{224,1... | collective-permute-start | bytes 663560 | tf_op jit(solution)/shard_map/ppermute | solution.py:257
  12.0 6.1 %copy-start.8 = (bf16[288,384]{1,0:T(8,128)(2,1)}, bf16[288,384]{1,0:T(8,128)(2,1)S(1)}, u32[]{:S(2)}) copy-start(bf16[288,384]{1,0:T(8,128)(2,1)S(1)} %collective-permute-done.2.rest_3_) | copy-start | bytes 663556
  15.6 2.5 %copy-start.9 = (bf16[288,384]{1,0:T(8,128)(2,1)}, bf16[288,384]{1,0:T(8,128)(2,1)S(1)}, u32[]{:S(2)}) copy-start(bf16[288,384]{1,0:T(8,128)(2,1)S(1)} %collective-permute-done.1.rest_2_) | copy-start | bytes 663556
  15.7 2.5 %copy-start.10 = (bf16[288,384]{1,0:T(8,128)(2,1)}, bf16[288,384]{1,0:T(8,128)(2,1)S(1)}, u32[]{:S(2)}) copy-start(bf16[288,384]{1,0:T(8,128)(2,1)S(1)} %collective-permute-done.rest_1_) | copy-start | bytes 663556
  15.7 1.8 %collective-permute-start.3 = (bf16[288,384]{1,0:T(8,128)(2,1)}, bf16[288,384]{1,0:T(8,128)(2,1)S(1)}, u32[]{:S(2)}, u32[]{:S(2)}) collective-permute-start(bf16[288,384]{1,0:T(8,128)(2,1)} %shard_map.55.rest_0_), channel_id=1, source_target_pairs={{0,32},{32,0},{64,96},{96,64},{128,160},{160,128},{192,224},{224,1... | collective-permute-start | bytes 663560 | tf_op jit(solution)/shard_map/ppermute | solution.py:260
  15.8 1.8 %collective-permute-start.4 = (bf16[288,384]{1,0:T(8,128)(2,1)S(1)}, bf16[288,384]{1,0:T(8,128)(2,1)S(1)}, u32[]{:S(2)}, u32[]{:S(2)}) collective-permute-start(bf16[288,384]{1,0:T(8,128)(2,1)S(1)} %collective-permute-done.rest_1_), channel_id=1, source_target_pairs={{0,32},{32,0},{64,96},{96,64},{128,160},{160,128},{192,224},{224,1... | collective-permute-start | bytes 663560 | tf_op jit(solution)/shard_map/ppermute | solution.py:260
  16.2 1.6 %collective-permute-start.5 = (bf16[288,384]{1,0:T(8,128)(2,1)S(1)}, bf16[288,384]{1,0:T(8,128)(2,1)S(1)}, u32[]{:S(2)}, u32[]{:S(2)}) collective-permute-start(bf16[288,384]{1,0:T(8,128)(2,1)S(1)} %collective-permute-done.1.rest_2_), channel_id=1, source_target_pairs={{0,32},{32,0},{64,96},{96,64},{128,160},{160,128},{192,224},{224,1... | collective-permute-start | bytes 663560 | tf_op jit(solution)/shard_map/ppermute | solution.py:260
  16.4 1.8 %collective-permute-start.6 = (bf16[288,384]{1,0:T(8,128)(2,1)S(1)}, bf16[288,384]{1,0:T(8,128)(2,1)S(1)}, u32[]{:S(2)}, u32[]{:S(2)}) collective-permute-start(bf16[288,384]{1,0:T(8,128)(2,1)S(1)} %collective-permute-done.2.rest_3_), channel_id=1, source_target_pairs={{0,32},{32,0},{64,96},{96,64},{128,160},{160,128},{192,224},{224,1... | collective-permute-start | bytes 663560 | tf_op jit(solution)/shard_map/ppermute | solution.py:260
  17.4 0.8 copy-start.11
  17.5 0.7 copy-start.12
  17.8 0.7 copy-start.13
  18.2 0.7 copy-start.14
  46.0 14.4 %collective-permute-start.7 = (bf16[8,24192]{1,0:T(8,128)(2,1)}, bf16[8,24192]{1,0:T(8,128)(2,1)S(1)}, u32[]{:S(2)}, u32[]{:S(2)}) collective-permute-start(bf16[8,24192]{1,0:T(8,128)(2,1)} %get-tuple-element.41), channel_id=1, source_target_pairs={{0,1},{1,2},{2,3},{3,0},{4,5},{5,6},{6,7},{7,4},{8,9},{9,10},{10,1... | collective-permute-start | bytes 1161224 | tf_op jit(solution)/shard_map/ppermute | solution.py:263
  47.7 20.5 %collective-permute-start.8 = (bf16[8,24192]{1,0:T(8,128)(2,1)}, bf16[8,24192]{1,0:T(8,128)(2,1)S(1)}, u32[]{:S(2)}, u32[]{:S(2)}) collective-permute-start(bf16[8,24192]{1,0:T(8,128)(2,1)} %get-tuple-element.42), channel_id=1, source_target_pairs={{0,2},{1,3},{2,0},{3,1},{4,6},{5,7},{6,4},{7,5},{8,10},{9,11},{10,... | collective-permute-start | bytes 1161224 | tf_op jit(solution)/shard_map/ppermute | solution.py:263
  50.5 17.6 %collective-permute-start.9 = (bf16[8,24192]{1,0:T(8,128)(2,1)}, bf16[8,24192]{1,0:T(8,128)(2,1)S(1)}, u32[]{:S(2)}, u32[]{:S(2)}) collective-permute-start(bf16[8,24192]{1,0:T(8,128)(2,1)} %get-tuple-element.43), channel_id=1, source_target_pairs={{0,3},{1,0},{2,1},{3,2},{4,7},{5,4},{6,5},{7,6},{8,11},{9,8},{10,9... | collective-permute-start | bytes 1161224 | tf_op jit(solution)/shard_map/ppermute | solution.py:263
  51.9 24.0 %all-to-all-start.1 = ((bf16[8,224,128]{2,1,0:T(8,128)(2,1)}), bf16[8,224,128]{2,1,0:T(8,128)(2,1)S(1)}, u32[]{:S(2)}, u32[]{:S(2)}) async-start(bf16[8,224,128]{2,1,0:T(8,128)(2,1)} %get-tuple-element.44), calls=%async_computation.1 | async-start | bytes 917504 | tf_op jit(solution)/shard_map/all_to_all | solution.py:266
  60.4 7.8 %copy-start.5 = (bf16[8,24192]{1,0:T(8,128)(2,1)}, bf16[8,24192]{1,0:T(8,128)(2,1)S(1)}, u32[]{:S(2)}) copy-start(bf16[8,24192]{1,0:T(8,128)(2,1)S(1)} %collective-permute-done.7.x1) | copy-start | bytes 1161220
  68.1 0.7 copy-start.6
  68.1 0.9 copy-start.7
  76.0 4.4 %copy-start = (bf16[8,224,128]{2,1,0:T(8,128)(2,1)}, bf16[8,224,128]{2,1,0:T(8,128)(2,1)S(1)}, u32[]{:S(2)}) copy-start(bf16[8,224,128]{2,1,0:T(8,128)(2,1)S(1)} %all-to-all-done.1.x_ref) | copy-start | bytes 1376260
  76.0 18.6 %all-to-all-start = ((bf16[8,192,128]{2,1,0:T(8,128)(2,1)}), bf16[8,192,128]{2,1,0:T(8,128)(2,1)S(1)}, u32[]{:S(2)}, u32[]{:S(2)}) async-start(bf16[8,192,128]{2,1,0:T(8,128)(2,1)} %shard_map.58), calls=%async_computation | async-start | bytes 786432 | tf_op jit(solution)/shard_map/all_to_all | solution.py:266
  82.1 5.1 %collective-permute-start.10 = (bf16[56,128]{1,0:T(8,128)(2,1)}, bf16[56,128]{1,0:T(8,128)(2,1)S(1)}, u32[]{:S(2)}, u32[]{:S(2)}) collective-permute-start(bf16[56,128]{1,0:T(8,128)(2,1)} %get-tuple-element.46), channel_id=1, source_target_pairs={{0,1},{1,2},{2,3},{3,0},{4,5},{5,6},{6,7},{7,4},{8,9},{9,10},{10,1... | collective-permute-start | bytes 43016 | tf_op jit(solution)/shard_map/ppermute | solution.py:263
  83.2 5.4 %collective-permute-start.11 = (bf16[56,128]{1,0:T(8,128)(2,1)}, bf16[56,128]{1,0:T(8,128)(2,1)S(1)}, u32[]{:S(2)}, u32[]{:S(2)}) collective-permute-start(bf16[56,128]{1,0:T(8,128)(2,1)} %get-tuple-element.47), channel_id=1, source_target_pairs={{0,2},{1,3},{2,0},{3,1},{4,6},{5,7},{6,4},{7,5},{8,10},{9,11},{10,... | collective-permute-start | bytes 43016 | tf_op jit(solution)/shard_map/ppermute | solution.py:263
  85.6 3.9 %collective-permute-start.12 = (bf16[56,128]{1,0:T(8,128)(2,1)}, bf16[56,128]{1,0:T(8,128)(2,1)S(1)}, u32[]{:S(2)}, u32[]{:S(2)}) collective-permute-start(bf16[56,128]{1,0:T(8,128)(2,1)} %get-tuple-element.48), channel_id=1, source_target_pairs={{0,3},{1,0},{2,1},{3,2},{4,7},{5,4},{6,5},{7,6},{8,11},{9,8},{10,9... | collective-permute-start | bytes 43016 | tf_op jit(solution)/shard_map/ppermute | solution.py:263
  87.2 7.3 %copy-start.2 = (bf16[56,128]{1,0:T(8,128)(2,1)}, bf16[56,128]{1,0:T(8,128)(2,1)S(1)}, u32[]{:S(2)}) copy-start(bf16[56,128]{1,0:T(8,128)(2,1)S(1)} %collective-permute-done.10.y1) | copy-start | bytes 43012
  88.6 5.9 %copy-start.3 = (bf16[56,128]{1,0:T(8,128)(2,1)}, bf16[56,128]{1,0:T(8,128)(2,1)S(1)}, u32[]{:S(2)}) copy-start(bf16[56,128]{1,0:T(8,128)(2,1)S(1)} %collective-permute-done.11.y2) | copy-start | bytes 43012
  89.5 5.0 %copy-start.4 = (bf16[56,128]{1,0:T(8,128)(2,1)}, bf16[56,128]{1,0:T(8,128)(2,1)S(1)}, u32[]{:S(2)}) copy-start(bf16[56,128]{1,0:T(8,128)(2,1)S(1)} %collective-permute-done.12.y3) | copy-start | bytes 43012
  94.5 0.7 copy-start.1

commit v8 on v7

--- a/solution.py
+++ b/solution.py
@@ -59,8 +59,7 @@
     late = [pltpu.make_async_copy(full_hbm, full_ref, psems.at[9]), pltpu.make_async_copy(half_hbm, half_ref, psems.at[10])]
     for c in first:
         c.start()
-    for n in range(2):
-        copy(n).start()
+    copy(0).start()
 
     def zero(n, c):
         z = pl.multiple_of(n * 384, 8)
@@ -87,7 +86,7 @@
         for n in range(4 * q, 4 * q + 4):
             first[n].wait()
         if q == 1:
-            for n in range(2, R // CH):
+            for n in range(1, R // CH):
                 copy(n).start()
             for c in late:
                 c.start()
@@ -114,7 +113,7 @@
             buf[:, n * 256:n * 256 + 128] = jnp.dot(blk[i, ks[0]], w[0], preferred_element_type=f32).astype(bf)
 
     def phase2(i, n, buf):
-        wide = 256 if 2 * n + 1 < K else 128
+        wide = min(4, K - 2 * n) * 128
         term = jnp.dot(turned[i], buf[:, n * 256:n * 256 + wide], preferred_element_type=f32)
         for m in range(wide // 128):
             k = 2 * n + m
@@ -122,9 +121,10 @@
             acc[pl.ds(pl.multiple_of(dst[k, i], B), B), :] += term[:, m * 128:(m + 1) * 128]
 
     def both(i1, buf1, i2, buf2):
-        for n in range(PAIRS):
+        for n in range(0, PAIRS, 2):
             phase2(i2, n, buf2)
             phase1(i1, n, buf1)
+            phase1(i1, n + 1, buf1)
 
     copy(0).wait()
     for n in range(PAIRS):

time: 98.7 us -> 98.5 us (level)
  transfers between devices with their start and end apart: 15 -> 15, of which waited for: 12 -> 11; matrix products, arithmetic and copies ran while one was open for 1% -> 1% of each run, Pallas kernels for 8% -> 8%
where the time goes in v8:
time: 98.5 us; the launch traced here: 97.9 us
  Pallas kernels  39.8 us (40%)
  starting transfers between devices  29 us (29%)
  waiting for transfers between devices  25.4 us (26%)
  local copies, waits for them, and re-layouts  2.33 us (2%)
  other arithmetic  1.39 us (1%)
    pallas_call x1, Pallas kernels, main(): pl.pallas_call(main_kernel, out_shape=[jax.ShapeDtypeStruct((8, FIRST * 7...  27 us
    all_to_all x2, starting transfers between devices, exchange_z(): return lax.all_to_all(x, 'col', 0, 0, axis_index_groups=ZG, tiled=True)  12.8 us
    ppermute x6, starting transfers between devices, along_y(): lax.ppermute(x, 'col', [(4 * z + y, 4 * z + (y + by) % 4) for z in range(...  11 us
    ppermute x6, waiting for transfers between devices, along_y(): lax.ppermute(x, 'col', [(4 * z + y, 4 * z + (y + by) % 4) for z in range(...  10.1 us
    all_to_all x2, waiting for transfers between devices, exchange_z(): return lax.all_to_all(x, 'col', 0, 0, axis_index_groups=ZG, tiled=True)  9.16 us
    ppermute x3, waiting for transfers between devices, along_x(): return lax.ppermute(x, 'row', [(i, (i + 2 * by) % 8) for i in range(8)])  4.71 us
    ppermute x3, starting transfers between devices, along_x(): return lax.ppermute(x, 'row', [(i, (i + 2 * by) % 8) for i in range(8)])  4.15 us
    pallas_call x1, Pallas kernels, turn(): pl.pallas_call(turn_kernel, out_shape=[jax.ShapeDtypeStruct((R, B, B), bf...  3.45 us
  transfers between devices with their start and end apart: 15, of which 11 were waited for; matrix products, arithmetic and copies ran while one was open for 1% of the time, Pallas kernels for 8%

profile of v8, /device:TPU:2, one launch (start us, length us, event | category | flops | bytes accessed | tf_op | source)
XLA Modules:
  0.0 97.9 jit_solution(5480060385134791147)
XLA Ops:
  0.0 1.9 %shard_map.55.rest_0_ = bf16[288,384]{1,0:T(8,128)(2,1)} custom-call(bf16[48,48,48]{2,1,0:T(8,128)(2,1)} %p_ref.3), custom_call_target="tpu_custom_call" | custom-call | tf_op jit(solution)/shard_map/pallas_call | solution.py:28
  1.9 2.1 %collective-permute-start.2 = (bf16[288,384]{1,0:T(8,128)(2,1)}, bf16[288,384]{1,0:T(8,128)(2,1)S(1)}, u32[]{:S(2)}, u32[]{:S(2)}) collective-permute-start(bf16[288,384]{1,0:T(8,128)(2,1)} %shard_map.55.rest_0_), channel_id=1, source_target_pairs={{0,128},{32,160},{64,192},{96,224},{128,0},{160,32},{192,64},{224,... | collective-permute-start | bytes 663560 | tf_op jit(solution)/shard_map/ppermute | solution.py:257
  4.1 1.6 %collective-permute-start.1 = (bf16[288,384]{1,0:T(8,128)(2,1)}, bf16[288,384]{1,0:T(8,128)(2,1)S(1)}, u32[]{:S(2)}, u32[]{:S(2)}) collective-permute-start(bf16[288,384]{1,0:T(8,128)(2,1)} %shard_map.55.rest_0_), channel_id=1, source_target_pairs={{0,64},{32,96},{64,128},{96,160},{128,192},{160,224},{192,0},{224,... | collective-permute-start | bytes 663560 | tf_op jit(solution)/shard_map/ppermute | solution.py:257
  5.7 0.4 collective-permute-start
  6.1 3.4 %shard_map.56 = (bf16[48,48,48]{2,1,0:T(8,128)(2,1)}, bf16[512,384]{1,0:T(8,128)(2,1)}, bf16[2,1024,384]{2,1,0:T(8,128)(2,1)}) custom-call(bf16[48,48,48]{2,1,0:T(8,128)(2,1)} %p_ref.3), custom_call_target="tpu_custom_call" | custom-call | flops 10000000 | bytes 2000000 | tf_op jit(solution)/shard_map/pallas_call | solution.py:47
  9.5 1.4 %multiply_bitcast_fusion = (s32[27,48]{1,0:T(8,128)}, s32[27,48]{1,0:T(8,128)}, s32[27,48]{1,0:T(8,128)}) fusion(s32[48,27]{0,1:T(8,128)} %param.9, s32[48]{0:T(128)} %param.8, s32[]{:T(128)S(6)} %axis_index.25, s32[]{:T(128)S(6)} %shift_right_arithmetic.17, s32[48,27]{0,1:T(8,128)} %param.7), kind=kLoop, calls=%fused_computation.11 | loop fusion | flops 53136 | bytes 26120 | tf_op jit(solution)/shard_map/transpose | solution.py:277
  10.9 1.1 %collective-permute-done.2.rest_3_ = bf16[288,384]{1,0:T(8,128)(2,1)S(1)} collective-permute-done((bf16[288,384]{1,0:T(8,128)(2,1)}, bf16[288,384]{1,0:T(8,128)(2,1)S(1)}, u32[]{:S(2)}, u32[]{:S(2)}) %collective-permute-start.2) | collective-permute-done | bytes 221216 | tf_op jit(solution)/shard_map/ppermute | solution.py:257
  12.0 3.6 %collective-permute-done.1.rest_2_ = bf16[288,384]{1,0:T(8,128)(2,1)S(1)} collective-permute-done((bf16[288,384]{1,0:T(8,128)(2,1)}, bf16[288,384]{1,0:T(8,128)(2,1)S(1)}, u32[]{:S(2)}, u32[]{:S(2)}) %collective-permute-start.1) | collective-permute-done | bytes 221216 | tf_op jit(solution)/shard_map/ppermute | solution.py:257
  15.8 0.5 collective-permute-start.4
  16.4 0.4 collective-permute-start.6
  16.8 0.7 collective-permute-done.3.rest_4_
  17.9 0.3 collective-permute-done.6.rest_7_
  18.2 0.3 copy-done.13
  18.9 27.0 %shard_map.57 = (bf16[8,24192]{1,0:T(8,128)(2,1)}, bf16[8,24192]{1,0:T(8,128)(2,1)}, bf16[8,24192]{1,0:T(8,128)(2,1)}, bf16[8,24192]{1,0:T(8,128)(2,1)}, bf16[8,224,128]{2,1,0:T(8,128)(2,1)}) custom-call(s32[27,48]{1,0:T(8,128)} %get-tuple-element.30.src, s32[27,48]{1,0:T(8,128)} %get-tuple-element.31.odd, s32[27,48]{1,0:T(8,128)} %get-tuple-element.32.dst, ...), custom_call_target="tpu_custom_call" | custom-call | flops 20000000000 | bytes 10000000 | tf_op jit(solution)/shard_map/pallas_call | solution.py:183
  45.9 1.6 %collective-permute-start.7 = (bf16[8,24192]{1,0:T(8,128)(2,1)}, bf16[8,24192]{1,0:T(8,128)(2,1)S(1)}, u32[]{:S(2)}, u32[]{:S(2)}) collective-permute-start(bf16[8,24192]{1,0:T(8,128)(2,1)} %get-tuple-element.41), channel_id=1, source_target_pairs={{0,1},{1,2},{2,3},{3,0},{4,5},{5,6},{6,7},{7,4},{8,9},{9,10},{10,1... | collective-permute-start | bytes 1161224 | tf_op jit(solution)/shard_map/ppermute | solution.py:263
  47.5 2.9 %collective-permute-start.8 = (bf16[8,24192]{1,0:T(8,128)(2,1)}, bf16[8,24192]{1,0:T(8,128)(2,1)S(1)}, u32[]{:S(2)}, u32[]{:S(2)}) collective-permute-start(bf16[8,24192]{1,0:T(8,128)(2,1)} %get-tuple-element.42), channel_id=1, source_target_pairs={{0,2},{1,3},{2,0},{3,1},{4,6},{5,7},{6,4},{7,5},{8,10},{9,11},{10,... | collective-permute-start | bytes 1161224 | tf_op jit(solution)/shard_map/ppermute | solution.py:263
  50.4 1.4 %collective-permute-start.9 = (bf16[8,24192]{1,0:T(8,128)(2,1)}, bf16[8,24192]{1,0:T(8,128)(2,1)S(1)}, u32[]{:S(2)}, u32[]{:S(2)}) collective-permute-start(bf16[8,24192]{1,0:T(8,128)(2,1)} %get-tuple-element.43), channel_id=1, source_target_pairs={{0,3},{1,0},{2,1},{3,2},{4,7},{5,4},{6,5},{7,6},{8,11},{9,8},{10,9... | collective-permute-start | bytes 1161224 | tf_op jit(solution)/shard_map/ppermute | solution.py:263
  51.8 8.4 %all-to-all-start.1 = ((bf16[8,224,128]{2,1,0:T(8,128)(2,1)}), bf16[8,224,128]{2,1,0:T(8,128)(2,1)S(1)}, u32[]{:S(2)}, u32[]{:S(2)}) async-start(bf16[8,224,128]{2,1,0:T(8,128)(2,1)} %get-tuple-element.44), calls=%async_computation.1 | async-start | bytes 917504 | tf_op jit(solution)/shard_map/all_to_all | solution.py:266
  60.2 7.8 %collective-permute-done.8.x2 = bf16[8,24192]{1,0:T(8,128)(2,1)S(1)} collective-permute-done((bf16[8,24192]{1,0:T(8,128)(2,1)}, bf16[8,24192]{1,0:T(8,128)(2,1)S(1)}, u32[]{:S(2)}, u32[]{:S(2)}) %collective-permute-start.8) | collective-permute-done | bytes 387104 | tf_op jit(solution)/shard_map/ppermute | solution.py:263
  68.0 0.7 copy-done.6
  68.9 2.9 %shard_map.58 = bf16[8,192,128]{2,1,0:T(8,128)(2,1)} custom-call(bf16[8,24192]{1,0:T(8,128)(2,1)} %get-tuple-element.40.x0, bf16[8,24192]{1,0:T(8,128)(2,1)} %copy-done.5, bf16[8,24192]{1,0:T(8,128)(2,1)} %copy-done.6, bf16[8,24192]{1,0:T(8,128)(2,1)} %copy-done.7), custom_call_target="tpu_custom_call" | custom-call | flops 40000000000 | bytes 10000000 | tf_op jit(solution)/shard_map/pallas_call | solution.py:209
  71.8 4.1 %all-to-all-done.1.x_ref = bf16[8,224,128]{2,1,0:T(8,128)(2,1)S(1)} async-done(((bf16[8,224,128]{2,1,0:T(8,128)(2,1)}), bf16[8,224,128]{2,1,0:T(8,128)(2,1)S(1)}, u32[]{:S(2)}, u32[]{:S(2)}) %all-to-all-start.1) | async-done | bytes 458784 | tf_op jit(solution)/shard_map/all_to_all | solution.py:266
  75.9 4.4 %all-to-all-start = ((bf16[8,192,128]{2,1,0:T(8,128)(2,1)}), bf16[8,192,128]{2,1,0:T(8,128)(2,1)S(1)}, u32[]{:S(2)}, u32[]{:S(2)}) async-start(bf16[8,192,128]{2,1,0:T(8,128)(2,1)} %shard_map.58), calls=%async_computation | async-start | bytes 786432 | tf_op jit(solution)/shard_map/all_to_all | solution.py:266
  80.3 1.7 %shard_map.59 = (bf16[56,128]{1,0:T(8,128)(2,1)}, bf16[56,128]{1,0:T(8,128)(2,1)}, bf16[56,128]{1,0:T(8,128)(2,1)}, bf16[56,128]{1,0:T(8,128)(2,1)}) custom-call(s32[1]{0:T(128)} %bitcast.here, bf16[8,224,128]{2,1,0:T(8,128)(2,1)} %copy-done), custom_call_target="tpu_custom_call" | custom-call | tf_op jit(solution)/shard_map/pallas_call | solution.py:220
  82.0 1.1 %collective-permute-start.10 = (bf16[56,128]{1,0:T(8,128)(2,1)}, bf16[56,128]{1,0:T(8,128)(2,1)S(1)}, u32[]{:S(2)}, u32[]{:S(2)}) collective-permute-start(bf16[56,128]{1,0:T(8,128)(2,1)} %get-tuple-element.46), channel_id=1, source_target_pairs={{0,1},{1,2},{2,3},{3,0},{4,5},{5,6},{6,7},{7,4},{8,9},{9,10},{10,1... | collective-permute-start | bytes 43016 | tf_op jit(solution)/shard_map/ppermute | solution.py:263
  83.1 2.4 %collective-permute-start.11 = (bf16[56,128]{1,0:T(8,128)(2,1)}, bf16[56,128]{1,0:T(8,128)(2,1)S(1)}, u32[]{:S(2)}, u32[]{:S(2)}) collective-permute-start(bf16[56,128]{1,0:T(8,128)(2,1)} %get-tuple-element.47), channel_id=1, source_target_pairs={{0,2},{1,3},{2,0},{3,1},{4,6},{5,7},{6,4},{7,5},{8,10},{9,11},{10,... | collective-permute-start | bytes 43016 | tf_op jit(solution)/shard_map/ppermute | solution.py:263
  85.5 1.6 %collective-permute-start.12 = (bf16[56,128]{1,0:T(8,128)(2,1)}, bf16[56,128]{1,0:T(8,128)(2,1)S(1)}, u32[]{:S(2)}, u32[]{:S(2)}) collective-permute-start(bf16[56,128]{1,0:T(8,128)(2,1)} %get-tuple-element.48), channel_id=1, source_target_pairs={{0,3},{1,0},{2,1},{3,2},{4,7},{5,4},{6,5},{7,6},{8,11},{9,8},{10,9... | collective-permute-start | bytes 43016 | tf_op jit(solution)/shard_map/ppermute | solution.py:263
  87.1 1.4 %collective-permute-done.11.y2 = bf16[56,128]{1,0:T(8,128)(2,1)S(1)} collective-permute-done((bf16[56,128]{1,0:T(8,128)(2,1)}, bf16[56,128]{1,0:T(8,128)(2,1)S(1)}, u32[]{:S(2)}, u32[]{:S(2)}) %collective-permute-start.11) | collective-permute-done | bytes 14368 | tf_op jit(solution)/shard_map/ppermute | solution.py:263
  88.5 0.9 collective-permute-done.12.y3
  89.4 5.1 %all-to-all-done.x_ref = bf16[8,192,128]{2,1,0:T(8,128)(2,1)S(1)} async-done(((bf16[8,192,128]{2,1,0:T(8,128)(2,1)}), bf16[8,192,128]{2,1,0:T(8,128)(2,1)S(1)}, u32[]{:S(2)}, u32[]{:S(2)}) %all-to-all-start) | async-done | bytes 393248 | tf_op jit(solution)/shard_map/all_to_all | solution.py:266
  94.5 0.7 copy-done.1
  95.2 2.7 %shard_map.60 = f32[27,16,72]{2,1,0:T(8,128)} custom-call(s32[1]{0:T(128)} %bitcast.here, bf16[8,192,128]{2,1,0:T(8,128)(2,1)} %copy-done.1, bf16[56,128]{1,0:T(8,128)(2,1)} %get-tuple-element.45.y0, bf16[56,128]{1,0:T(8,128)(2,1)} %copy-done.2, bf16[56,128]{1,0:T(8,128)(2,1)} %copy-done.3, bf16[56,128]{1,0:T(8,128)(2,1)} %copy-done.4), custom_call_target="tpu_custom_call" | custom-call | tf_op jit(solution)/shard_map/pallas_call | solution.py:250
  (35 shorter events, 1.2 us)
Async XLA Ops:
  1.9 10.1 %collective-permute-start.2 = (bf16[288,384]{1,0:T(8,128)(2,1)}, bf16[288,384]{1,0:T(8,128)(2,1)S(1)}, u32[]{:S(2)}, u32[]{:S(2)}) collective-permute-start(bf16[288,384]{1,0:T(8,128)(2,1)} %shard_map.55.rest_0_), channel_id=1, source_target_pairs={{0,128},{32,160},{64,192},{96,224},{128,0},{160,32},{192,64},{224,... | collective-permute-start | bytes 663560 | tf_op jit(solution)/shard_map/ppermute | solution.py:257
  4.1 11.6 %collective-permute-start.1 = (bf16[288,384]{1,0:T(8,128)(2,1)}, bf16[288,384]{1,0:T(8,128)(2,1)S(1)}, u32[]{:S(2)}, u32[]{:S(2)}) collective-permute-start(bf16[288,384]{1,0:T(8,128)(2,1)} %shard_map.55.rest_0_), channel_id=1, source_target_pairs={{0,64},{32,96},{64,128},{96,160},{128,192},{160,224},{192,0},{224,... | collective-permute-start | bytes 663560 | tf_op jit(solution)/shard_map/ppermute | solution.py:257
  5.7 10.0 %collective-permute-start = (bf16[288,384]{1,0:T(8,128)(2,1)}, bf16[288,384]{1,0:T(8,128)(2,1)S(1)}, u32[]{:S(2)}, u32[]{:S(2)}) collective-permute-start(bf16[288,384]{1,0:T(8,128)(2,1)} %shard_map.55.rest_0_), channel_id=1, source_target_pairs={{0,192},{32,224},{64,0},{96,32},{128,64},{160,96},{192,128},{224,1... | collective-permute-start | bytes 663560 | tf_op jit(solution)/shard_map/ppermute | solution.py:257
  12.0 6.1 %copy-start.8 = (bf16[288,384]{1,0:T(8,128)(2,1)}, bf16[288,384]{1,0:T(8,128)(2,1)S(1)}, u32[]{:S(2)}) copy-start(bf16[288,384]{1,0:T(8,128)(2,1)S(1)} %collective-permute-done.2.rest_3_) | copy-start | bytes 663556
  15.6 2.5 %copy-start.9 = (bf16[288,384]{1,0:T(8,128)(2,1)}, bf16[288,384]{1,0:T(8,128)(2,1)S(1)}, u32[]{:S(2)}) copy-start(bf16[288,384]{1,0:T(8,128)(2,1)S(1)} %collective-permute-done.1.rest_2_) | copy-start | bytes 663556
  15.7 2.5 %copy-start.10 = (bf16[288,384]{1,0:T(8,128)(2,1)}, bf16[288,384]{1,0:T(8,128)(2,1)S(1)}, u32[]{:S(2)}) copy-start(bf16[288,384]{1,0:T(8,128)(2,1)S(1)} %collective-permute-done.rest_1_) | copy-start | bytes 663556
  15.7 1.8 %collective-permute-start.3 = (bf16[288,384]{1,0:T(8,128)(2,1)}, bf16[288,384]{1,0:T(8,128)(2,1)S(1)}, u32[]{:S(2)}, u32[]{:S(2)}) collective-permute-start(bf16[288,384]{1,0:T(8,128)(2,1)} %shard_map.55.rest_0_), channel_id=1, source_target_pairs={{0,32},{32,0},{64,96},{96,64},{128,160},{160,128},{192,224},{224,1... | collective-permute-start | bytes 663560 | tf_op jit(solution)/shard_map/ppermute | solution.py:260
  15.8 1.8 %collective-permute-start.4 = (bf16[288,384]{1,0:T(8,128)(2,1)S(1)}, bf16[288,384]{1,0:T(8,128)(2,1)S(1)}, u32[]{:S(2)}, u32[]{:S(2)}) collective-permute-start(bf16[288,384]{1,0:T(8,128)(2,1)S(1)} %collective-permute-done.rest_1_), channel_id=1, source_target_pairs={{0,32},{32,0},{64,96},{96,64},{128,160},{160,128},{192,224},{224,1... | collective-permute-start | bytes 663560 | tf_op jit(solution)/shard_map/ppermute | solution.py:260
  16.2 1.6 %collective-permute-start.5 = (bf16[288,384]{1,0:T(8,128)(2,1)S(1)}, bf16[288,384]{1,0:T(8,128)(2,1)S(1)}, u32[]{:S(2)}, u32[]{:S(2)}) collective-permute-start(bf16[288,384]{1,0:T(8,128)(2,1)S(1)} %collective-permute-done.1.rest_2_), channel_id=1, source_target_pairs={{0,32},{32,0},{64,96},{96,64},{128,160},{160,128},{192,224},{224,1... | collective-permute-start | bytes 663560 | tf_op jit(solution)/shard_map/ppermute | solution.py:260
  16.4 1.8 %collective-permute-start.6 = (bf16[288,384]{1,0:T(8,128)(2,1)S(1)}, bf16[288,384]{1,0:T(8,128)(2,1)S(1)}, u32[]{:S(2)}, u32[]{:S(2)}) collective-permute-start(bf16[288,384]{1,0:T(8,128)(2,1)S(1)} %collective-permute-done.2.rest_3_), channel_id=1, source_target_pairs={{0,32},{32,0},{64,96},{96,64},{128,160},{160,128},{192,224},{224,1... | collective-permute-start | bytes 663560 | tf_op jit(solution)/shard_map/ppermute | solution.py:260
  17.4 0.8 copy-start.11
  17.5 0.7 copy-start.12
  17.8 0.7 copy-start.13
  18.2 0.7 copy-start.14
  45.9 14.3 %collective-permute-start.7 = (bf16[8,24192]{1,0:T(8,128)(2,1)}, bf16[8,24192]{1,0:T(8,128)(2,1)S(1)}, u32[]{:S(2)}, u32[]{:S(2)}) collective-permute-start(bf16[8,24192]{1,0:T(8,128)(2,1)} %get-tuple-element.41), channel_id=1, source_target_pairs={{0,1},{1,2},{2,3},{3,0},{4,5},{5,6},{6,7},{7,4},{8,9},{9,10},{10,1... | collective-permute-start | bytes 1161224 | tf_op jit(solution)/shard_map/ppermute | solution.py:263
  47.5 20.4 %collective-permute-start.8 = (bf16[8,24192]{1,0:T(8,128)(2,1)}, bf16[8,24192]{1,0:T(8,128)(2,1)S(1)}, u32[]{:S(2)}, u32[]{:S(2)}) collective-permute-start(bf16[8,24192]{1,0:T(8,128)(2,1)} %get-tuple-element.42), channel_id=1, source_target_pairs={{0,2},{1,3},{2,0},{3,1},{4,6},{5,7},{6,4},{7,5},{8,10},{9,11},{10,... | collective-permute-start | bytes 1161224 | tf_op jit(solution)/shard_map/ppermute | solution.py:263
  50.4 17.6 %collective-permute-start.9 = (bf16[8,24192]{1,0:T(8,128)(2,1)}, bf16[8,24192]{1,0:T(8,128)(2,1)S(1)}, u32[]{:S(2)}, u32[]{:S(2)}) collective-permute-start(bf16[8,24192]{1,0:T(8,128)(2,1)} %get-tuple-element.43), channel_id=1, source_target_pairs={{0,3},{1,0},{2,1},{3,2},{4,7},{5,4},{6,5},{7,6},{8,11},{9,8},{10,9... | collective-permute-start | bytes 1161224 | tf_op jit(solution)/shard_map/ppermute | solution.py:263
  51.8 24.1 %all-to-all-start.1 = ((bf16[8,224,128]{2,1,0:T(8,128)(2,1)}), bf16[8,224,128]{2,1,0:T(8,128)(2,1)S(1)}, u32[]{:S(2)}, u32[]{:S(2)}) async-start(bf16[8,224,128]{2,1,0:T(8,128)(2,1)} %get-tuple-element.44), calls=%async_computation.1 | async-start | bytes 917504 | tf_op jit(solution)/shard_map/all_to_all | solution.py:266
  60.2 7.8 %copy-start.5 = (bf16[8,24192]{1,0:T(8,128)(2,1)}, bf16[8,24192]{1,0:T(8,128)(2,1)S(1)}, u32[]{:S(2)}) copy-start(bf16[8,24192]{1,0:T(8,128)(2,1)S(1)} %collective-permute-done.7.x1) | copy-start | bytes 1161220
  68.0 0.7 copy-start.6
  68.0 0.9 copy-start.7
  75.9 4.4 %copy-start = (bf16[8,224,128]{2,1,0:T(8,128)(2,1)}, bf16[8,224,128]{2,1,0:T(8,128)(2,1)S(1)}, u32[]{:S(2)}) copy-start(bf16[8,224,128]{2,1,0:T(8,128)(2,1)S(1)} %all-to-all-done.1.x_ref) | copy-start | bytes 1376260
  75.9 18.6 %all-to-all-start = ((bf16[8,192,128]{2,1,0:T(8,128)(2,1)}), bf16[8,192,128]{2,1,0:T(8,128)(2,1)S(1)}, u32[]{:S(2)}, u32[]{:S(2)}) async-start(bf16[8,192,128]{2,1,0:T(8,128)(2,1)} %shard_map.58), calls=%async_computation | async-start | bytes 786432 | tf_op jit(solution)/shard_map/all_to_all | solution.py:266
  82.0 5.1 %collective-permute-start.10 = (bf16[56,128]{1,0:T(8,128)(2,1)}, bf16[56,128]{1,0:T(8,128)(2,1)S(1)}, u32[]{:S(2)}, u32[]{:S(2)}) collective-permute-start(bf16[56,128]{1,0:T(8,128)(2,1)} %get-tuple-element.46), channel_id=1, source_target_pairs={{0,1},{1,2},{2,3},{3,0},{4,5},{5,6},{6,7},{7,4},{8,9},{9,10},{10,1... | collective-permute-start | bytes 43016 | tf_op jit(solution)/shard_map/ppermute | solution.py:263
  83.1 5.4 %collective-permute-start.11 = (bf16[56,128]{1,0:T(8,128)(2,1)}, bf16[56,128]{1,0:T(8,128)(2,1)S(1)}, u32[]{:S(2)}, u32[]{:S(2)}) collective-permute-start(bf16[56,128]{1,0:T(8,128)(2,1)} %get-tuple-element.47), channel_id=1, source_target_pairs={{0,2},{1,3},{2,0},{3,1},{4,6},{5,7},{6,4},{7,5},{8,10},{9,11},{10,... | collective-permute-start | bytes 43016 | tf_op jit(solution)/shard_map/ppermute | solution.py:263
  85.5 3.9 %collective-permute-start.12 = (bf16[56,128]{1,0:T(8,128)(2,1)}, bf16[56,128]{1,0:T(8,128)(2,1)S(1)}, u32[]{:S(2)}, u32[]{:S(2)}) collective-permute-start(bf16[56,128]{1,0:T(8,128)(2,1)} %get-tuple-element.48), channel_id=1, source_target_pairs={{0,3},{1,0},{2,1},{3,2},{4,7},{5,4},{6,5},{7,6},{8,11},{9,8},{10,9... | collective-permute-start | bytes 43016 | tf_op jit(solution)/shard_map/ppermute | solution.py:263
  87.1 7.4 %copy-start.2 = (bf16[56,128]{1,0:T(8,128)(2,1)}, bf16[56,128]{1,0:T(8,128)(2,1)S(1)}, u32[]{:S(2)}) copy-start(bf16[56,128]{1,0:T(8,128)(2,1)S(1)} %collective-permute-done.10.y1) | copy-start | bytes 43012
  88.5 6.0 %copy-start.3 = (bf16[56,128]{1,0:T(8,128)(2,1)}, bf16[56,128]{1,0:T(8,128)(2,1)S(1)}, u32[]{:S(2)}) copy-start(bf16[56,128]{1,0:T(8,128)(2,1)S(1)} %collective-permute-done.11.y2) | copy-start | bytes 43012
  89.4 5.1 %copy-start.4 = (bf16[56,128]{1,0:T(8,128)(2,1)}, bf16[56,128]{1,0:T(8,128)(2,1)S(1)}, u32[]{:S(2)}) copy-start(bf16[56,128]{1,0:T(8,128)(2,1)S(1)} %collective-permute-done.12.y3) | copy-start | bytes 43012
  94.5 0.7 copy-start.1

commit v9 on v8

--- a/solution.py
+++ b/solution.py
@@ -162,7 +162,7 @@
     away = [pltpu.make_async_copy(out.at[(here[0] + d) & 3], sends[d], osems.at[d]) for d in range(4)]
     for c in late:
         c.wait()
-    for t, count in ((FIRST, REST), (0, FIRST)):
+    for t, count in ((0, FIRST), (FIRST, REST)):
         for y, u in enumerate(FULL):
             pack_rows(t, y, False, gathered(t // 2, u, 4, count // 8), full_ref)
         for u in (1, 4):
@@ -170,8 +170,9 @@
             for y, (v, h) in enumerate(SPLIT):
                 if v == u:
                     pack_rows(t, y, True, xs, half_ref.at[h])
-    for c in away:
-        c.start()
+        if t == 0:
+            for c in away:
+                c.start()
     for z in range(8):
         out2[z] = buf2[z * 4 * PAD2:(z + 1) * 4 * PAD2, :].astype(bf)
     for c in away:

time: 98.5 us -> 97.7 us (level)
  transfers between devices with their start and end apart: 15 -> 15, of which waited for: 11 -> 12; matrix products, arithmetic and copies ran while one was open for 1% -> 1% of each run, Pallas kernels for 8% -> 8%
where the time goes in v9:
time: 97.7 us; the launch traced here: 97.1 us
  Pallas kernels  38.9 us (40%)
  starting transfers between devices  29.1 us (30%)
  waiting for transfers between devices  25.3 us (26%)
  local copies, waits for them, and re-layouts  2.33 us (2%)
  other arithmetic  1.39 us (1%)
    pallas_call x1, Pallas kernels, main(): pl.pallas_call(main_kernel, out_shape=[jax.ShapeDtypeStruct((8, FIRST * 7...  26.2 us
    all_to_all x2, starting transfers between devices, exchange_z(): return lax.all_to_all(x, 'col', 0, 0, axis_index_groups=ZG, tiled=True)  12.9 us
    ppermute x6, starting transfers between devices, along_y(): lax.ppermute(x, 'col', [(4 * z + y, 4 * z + (y + by) % 4) for z in range(...  11 us
    ppermute x6, waiting for transfers between devices, along_y(): lax.ppermute(x, 'col', [(4 * z + y, 4 * z + (y + by) % 4) for z in range(...  10.1 us
    all_to_all x2, waiting for transfers between devices, exchange_z(): return lax.all_to_all(x, 'col', 0, 0, axis_index_groups=ZG, tiled=True)  9.06 us
    ppermute x3, waiting for transfers between devices, along_x(): return lax.ppermute(x, 'row', [(i, (i + 2 * by) % 8) for i in range(8)])  4.71 us
    ppermute x3, starting transfers between devices, along_x(): return lax.ppermute(x, 'row', [(i, (i + 2 * by) % 8) for i in range(8)])  4.15 us
    pallas_call x1, Pallas kernels, turn(): pl.pallas_call(turn_kernel, out_shape=[jax.ShapeDtypeStruct((R, B, B), bf...  3.45 us
  transfers between devices with their start and end apart: 15, of which 12 were waited for; matrix products, arithmetic and copies ran while one was open for 1% of the time, Pallas kernels for 8%

profile of v9, /device:TPU:2, one launch (start us, length us, event | category | flops | bytes accessed | tf_op | source)
XLA Modules:
  0.0 97.1 jit_solution(8815345212959233091)
XLA Ops:
  0.0 1.9 %shard_map.55.rest_0_ = bf16[288,384]{1,0:T(8,128)(2,1)} custom-call(bf16[48,48,48]{2,1,0:T(8,128)(2,1)} %p_ref.3), custom_call_target="tpu_custom_call" | custom-call | tf_op jit(solution)/shard_map/pallas_call | solution.py:28
  1.9 2.1 %collective-permute-start.2 = (bf16[288,384]{1,0:T(8,128)(2,1)}, bf16[288,384]{1,0:T(8,128)(2,1)S(1)}, u32[]{:S(2)}, u32[]{:S(2)}) collective-permute-start(bf16[288,384]{1,0:T(8,128)(2,1)} %shard_map.55.rest_0_), channel_id=1, source_target_pairs={{0,128},{32,160},{64,192},{96,224},{128,0},{160,32},{192,64},{224,... | collective-permute-start | bytes 663560 | tf_op jit(solution)/shard_map/ppermute | solution.py:258
  4.1 1.6 %collective-permute-start.1 = (bf16[288,384]{1,0:T(8,128)(2,1)}, bf16[288,384]{1,0:T(8,128)(2,1)S(1)}, u32[]{:S(2)}, u32[]{:S(2)}) collective-permute-start(bf16[288,384]{1,0:T(8,128)(2,1)} %shard_map.55.rest_0_), channel_id=1, source_target_pairs={{0,64},{32,96},{64,128},{96,160},{128,192},{160,224},{192,0},{224,... | collective-permute-start | bytes 663560 | tf_op jit(solution)/shard_map/ppermute | solution.py:258
  5.7 0.4 collective-permute-start
  6.1 3.4 %shard_map.56 = (bf16[48,48,48]{2,1,0:T(8,128)(2,1)}, bf16[512,384]{1,0:T(8,128)(2,1)}, bf16[2,1024,384]{2,1,0:T(8,128)(2,1)}) custom-call(bf16[48,48,48]{2,1,0:T(8,128)(2,1)} %p_ref.3), custom_call_target="tpu_custom_call" | custom-call | flops 10000000 | bytes 2000000 | tf_op jit(solution)/shard_map/pallas_call | solution.py:47
  9.5 1.4 %multiply_bitcast_fusion = (s32[27,48]{1,0:T(8,128)}, s32[27,48]{1,0:T(8,128)}, s32[27,48]{1,0:T(8,128)}) fusion(s32[48,27]{0,1:T(8,128)} %param.9, s32[48]{0:T(128)} %param.8, s32[]{:T(128)S(6)} %axis_index.25, s32[]{:T(128)S(6)} %shift_right_arithmetic.17, s32[48,27]{0,1:T(8,128)} %param.7), kind=kLoop, calls=%fused_computation.11 | loop fusion | flops 53136 | bytes 26120 | tf_op jit(solution)/shard_map/transpose | solution.py:278
  10.9 1.1 %collective-permute-done.2.rest_3_ = bf16[288,384]{1,0:T(8,128)(2,1)S(1)} collective-permute-done((bf16[288,384]{1,0:T(8,128)(2,1)}, bf16[288,384]{1,0:T(8,128)(2,1)S(1)}, u32[]{:S(2)}, u32[]{:S(2)}) %collective-permute-start.2) | collective-permute-done | bytes 221216 | tf_op jit(solution)/shard_map/ppermute | solution.py:258
  12.0 3.6 %collective-permute-done.1.rest_2_ = bf16[288,384]{1,0:T(8,128)(2,1)S(1)} collective-permute-done((bf16[288,384]{1,0:T(8,128)(2,1)}, bf16[288,384]{1,0:T(8,128)(2,1)S(1)}, u32[]{:S(2)}, u32[]{:S(2)}) %collective-permute-start.1) | collective-permute-done | bytes 221216 | tf_op jit(solution)/shard_map/ppermute | solution.py:258
  15.8 0.5 collective-permute-start.4
  16.4 0.4 collective-permute-start.6
  16.8 0.7 collective-permute-done.3.rest_4_
  17.5 0.3 collective-permute-done.5.rest_6_
  18.2 0.3 copy-done.13
  18.9 26.2 %shard_map.57 = (bf16[8,24192]{1,0:T(8,128)(2,1)}, bf16[8,24192]{1,0:T(8,128)(2,1)}, bf16[8,24192]{1,0:T(8,128)(2,1)}, bf16[8,24192]{1,0:T(8,128)(2,1)}, bf16[8,224,128]{2,1,0:T(8,128)(2,1)}) custom-call(s32[27,48]{1,0:T(8,128)} %get-tuple-element.30.src, s32[27,48]{1,0:T(8,128)} %get-tuple-element.31.odd, s32[27,48]{1,0:T(8,128)} %get-tuple-element.32.dst, ...), custom_call_target="tpu_custom_call" | custom-call | flops 20000000000 | bytes 10000000 | tf_op jit(solution)/shard_map/pallas_call | solution.py:184
  45.0 1.7 %collective-permute-start.7 = (bf16[8,24192]{1,0:T(8,128)(2,1)}, bf16[8,24192]{1,0:T(8,128)(2,1)S(1)}, u32[]{:S(2)}, u32[]{:S(2)}) collective-permute-start(bf16[8,24192]{1,0:T(8,128)(2,1)} %get-tuple-element.41), channel_id=1, source_target_pairs={{0,1},{1,2},{2,3},{3,0},{4,5},{5,6},{6,7},{7,4},{8,9},{9,10},{10,1... | collective-permute-start | bytes 1161224 | tf_op jit(solution)/shard_map/ppermute | solution.py:264
  46.7 2.9 %collective-permute-start.8 = (bf16[8,24192]{1,0:T(8,128)(2,1)}, bf16[8,24192]{1,0:T(8,128)(2,1)S(1)}, u32[]{:S(2)}, u32[]{:S(2)}) collective-permute-start(bf16[8,24192]{1,0:T(8,128)(2,1)} %get-tuple-element.42), channel_id=1, source_target_pairs={{0,2},{1,3},{2,0},{3,1},{4,6},{5,7},{6,4},{7,5},{8,10},{9,11},{10,... | collective-permute-start | bytes 1161224 | tf_op jit(solution)/shard_map/ppermute | solution.py:264
  49.6 1.4 %collective-permute-start.9 = (bf16[8,24192]{1,0:T(8,128)(2,1)}, bf16[8,24192]{1,0:T(8,128)(2,1)S(1)}, u32[]{:S(2)}, u32[]{:S(2)}) collective-permute-start(bf16[8,24192]{1,0:T(8,128)(2,1)} %get-tuple-element.43), channel_id=1, source_target_pairs={{0,3},{1,0},{2,1},{3,2},{4,7},{5,4},{6,5},{7,6},{8,11},{9,8},{10,9... | collective-permute-start | bytes 1161224 | tf_op jit(solution)/shard_map/ppermute | solution.py:264
  51.0 8.5 %all-to-all-start.1 = ((bf16[8,224,128]{2,1,0:T(8,128)(2,1)}), bf16[8,224,128]{2,1,0:T(8,128)(2,1)S(1)}, u32[]{:S(2)}, u32[]{:S(2)}) async-start(bf16[8,224,128]{2,1,0:T(8,128)(2,1)} %get-tuple-element.44), calls=%async_computation.1 | async-start | bytes 917504 | tf_op jit(solution)/shard_map/all_to_all | solution.py:267
  59.4 7.7 %collective-permute-done.8.x2 = bf16[8,24192]{1,0:T(8,128)(2,1)S(1)} collective-permute-done((bf16[8,24192]{1,0:T(8,128)(2,1)}, bf16[8,24192]{1,0:T(8,128)(2,1)S(1)}, u32[]{:S(2)}, u32[]{:S(2)}) %collective-permute-start.8) | collective-permute-done | bytes 387104 | tf_op jit(solution)/shard_map/ppermute | solution.py:264
  67.2 0.7 copy-done.6
  68.1 2.9 %shard_map.58 = bf16[8,192,128]{2,1,0:T(8,128)(2,1)} custom-call(bf16[8,24192]{1,0:T(8,128)(2,1)} %get-tuple-element.40.x0, bf16[8,24192]{1,0:T(8,128)(2,1)} %copy-done.5, bf16[8,24192]{1,0:T(8,128)(2,1)} %copy-done.6, bf16[8,24192]{1,0:T(8,128)(2,1)} %copy-done.7), custom_call_target="tpu_custom_call" | custom-call | flops 40000000000 | bytes 10000000 | tf_op jit(solution)/shard_map/pallas_call | solution.py:210
  71.0 4.0 %all-to-all-done.1.x_ref = bf16[8,224,128]{2,1,0:T(8,128)(2,1)S(1)} async-done(((bf16[8,224,128]{2,1,0:T(8,128)(2,1)}), bf16[8,224,128]{2,1,0:T(8,128)(2,1)S(1)}, u32[]{:S(2)}, u32[]{:S(2)}) %all-to-all-start.1) | async-done | bytes 458784 | tf_op jit(solution)/shard_map/all_to_all | solution.py:267
  75.0 4.4 %all-to-all-start = ((bf16[8,192,128]{2,1,0:T(8,128)(2,1)}), bf16[8,192,128]{2,1,0:T(8,128)(2,1)S(1)}, u32[]{:S(2)}, u32[]{:S(2)}) async-start(bf16[8,192,128]{2,1,0:T(8,128)(2,1)} %shard_map.58), calls=%async_computation | async-start | bytes 786432 | tf_op jit(solution)/shard_map/all_to_all | solution.py:267
  79.4 1.7 %shard_map.59 = (bf16[56,128]{1,0:T(8,128)(2,1)}, bf16[56,128]{1,0:T(8,128)(2,1)}, bf16[56,128]{1,0:T(8,128)(2,1)}, bf16[56,128]{1,0:T(8,128)(2,1)}) custom-call(s32[1]{0:T(128)} %bitcast.here, bf16[8,224,128]{2,1,0:T(8,128)(2,1)} %copy-done), custom_call_target="tpu_custom_call" | custom-call | tf_op jit(solution)/shard_map/pallas_call | solution.py:221
  81.1 1.1 %collective-permute-start.10 = (bf16[56,128]{1,0:T(8,128)(2,1)}, bf16[56,128]{1,0:T(8,128)(2,1)S(1)}, u32[]{:S(2)}, u32[]{:S(2)}) collective-permute-start(bf16[56,128]{1,0:T(8,128)(2,1)} %get-tuple-element.46), channel_id=1, source_target_pairs={{0,1},{1,2},{2,3},{3,0},{4,5},{5,6},{6,7},{7,4},{8,9},{9,10},{10,1... | collective-permute-start | bytes 43016 | tf_op jit(solution)/shard_map/ppermute | solution.py:264
  82.2 2.4 %collective-permute-start.11 = (bf16[56,128]{1,0:T(8,128)(2,1)}, bf16[56,128]{1,0:T(8,128)(2,1)S(1)}, u32[]{:S(2)}, u32[]{:S(2)}) collective-permute-start(bf16[56,128]{1,0:T(8,128)(2,1)} %get-tuple-element.47), channel_id=1, source_target_pairs={{0,2},{1,3},{2,0},{3,1},{4,6},{5,7},{6,4},{7,5},{8,10},{9,11},{10,... | collective-permute-start | bytes 43016 | tf_op jit(solution)/shard_map/ppermute | solution.py:264
  84.6 1.6 %collective-permute-start.12 = (bf16[56,128]{1,0:T(8,128)(2,1)}, bf16[56,128]{1,0:T(8,128)(2,1)S(1)}, u32[]{:S(2)}, u32[]{:S(2)}) collective-permute-start(bf16[56,128]{1,0:T(8,128)(2,1)} %get-tuple-element.48), channel_id=1, source_target_pairs={{0,3},{1,0},{2,1},{3,2},{4,7},{5,4},{6,5},{7,6},{8,11},{9,8},{10,9... | collective-permute-start | bytes 43016 | tf_op jit(solution)/shard_map/ppermute | solution.py:264
  86.3 1.4 %collective-permute-done.11.y2 = bf16[56,128]{1,0:T(8,128)(2,1)S(1)} collective-permute-done((bf16[56,128]{1,0:T(8,128)(2,1)}, bf16[56,128]{1,0:T(8,128)(2,1)S(1)}, u32[]{:S(2)}, u32[]{:S(2)}) %collective-permute-start.11) | collective-permute-done | bytes 14368 | tf_op jit(solution)/shard_map/ppermute | solution.py:264
  87.7 0.9 collective-permute-done.12.y3
  88.6 5.1 %all-to-all-done.x_ref = bf16[8,192,128]{2,1,0:T(8,128)(2,1)S(1)} async-done(((bf16[8,192,128]{2,1,0:T(8,128)(2,1)}), bf16[8,192,128]{2,1,0:T(8,128)(2,1)S(1)}, u32[]{:S(2)}, u32[]{:S(2)}) %all-to-all-start) | async-done | bytes 393248 | tf_op jit(solution)/shard_map/all_to_all | solution.py:267
  93.6 0.7 copy-done.1
  94.4 2.7 %shard_map.60 = f32[27,16,72]{2,1,0:T(8,128)} custom-call(s32[1]{0:T(128)} %bitcast.here, bf16[8,192,128]{2,1,0:T(8,128)(2,1)} %copy-done.1, bf16[56,128]{1,0:T(8,128)(2,1)} %get-tuple-element.45.y0, bf16[56,128]{1,0:T(8,128)(2,1)} %copy-done.2, bf16[56,128]{1,0:T(8,128)(2,1)} %copy-done.3, bf16[56,128]{1,0:T(8,128)(2,1)} %copy-done.4), custom_call_target="tpu_custom_call" | custom-call | tf_op jit(solution)/shard_map/pallas_call | solution.py:251
  (35 shorter events, 1.2 us)
Async XLA Ops:
  1.9 10.1 %collective-permute-start.2 = (bf16[288,384]{1,0:T(8,128)(2,1)}, bf16[288,384]{1,0:T(8,128)(2,1)S(1)}, u32[]{:S(2)}, u32[]{:S(2)}) collective-permute-start(bf16[288,384]{1,0:T(8,128)(2,1)} %shard_map.55.rest_0_), channel_id=1, source_target_pairs={{0,128},{32,160},{64,192},{96,224},{128,0},{160,32},{192,64},{224,... | collective-permute-start | bytes 663560 | tf_op jit(solution)/shard_map/ppermute | solution.py:258
  4.1 11.6 %collective-permute-start.1 = (bf16[288,384]{1,0:T(8,128)(2,1)}, bf16[288,384]{1,0:T(8,128)(2,1)S(1)}, u32[]{:S(2)}, u32[]{:S(2)}) collective-permute-start(bf16[288,384]{1,0:T(8,128)(2,1)} %shard_map.55.rest_0_), channel_id=1, source_target_pairs={{0,64},{32,96},{64,128},{96,160},{128,192},{160,224},{192,0},{224,... | collective-permute-start | bytes 663560 | tf_op jit(solution)/shard_map/ppermute | solution.py:258
  5.7 10.0 %collective-permute-start = (bf16[288,384]{1,0:T(8,128)(2,1)}, bf16[288,384]{1,0:T(8,128)(2,1)S(1)}, u32[]{:S(2)}, u32[]{:S(2)}) collective-permute-start(bf16[288,384]{1,0:T(8,128)(2,1)} %shard_map.55.rest_0_), channel_id=1, source_target_pairs={{0,192},{32,224},{64,0},{96,32},{128,64},{160,96},{192,128},{224,1... | collective-permute-start | bytes 663560 | tf_op jit(solution)/shard_map/ppermute | solution.py:258
  12.0 6.1 %copy-start.8 = (bf16[288,384]{1,0:T(8,128)(2,1)}, bf16[288,384]{1,0:T(8,128)(2,1)S(1)}, u32[]{:S(2)}) copy-start(bf16[288,384]{1,0:T(8,128)(2,1)S(1)} %collective-permute-done.2.rest_3_) | copy-start | bytes 663556
  15.6 2.5 %copy-start.9 = (bf16[288,384]{1,0:T(8,128)(2,1)}, bf16[288,384]{1,0:T(8,128)(2,1)S(1)}, u32[]{:S(2)}) copy-start(bf16[288,384]{1,0:T(8,128)(2,1)S(1)} %collective-permute-done.1.rest_2_) | copy-start | bytes 663556
  15.7 2.5 %copy-start.10 = (bf16[288,384]{1,0:T(8,128)(2,1)}, bf16[288,384]{1,0:T(8,128)(2,1)S(1)}, u32[]{:S(2)}) copy-start(bf16[288,384]{1,0:T(8,128)(2,1)S(1)} %collective-permute-done.rest_1_) | copy-start | bytes 663556
  15.7 1.8 %collective-permute-start.3 = (bf16[288,384]{1,0:T(8,128)(2,1)}, bf16[288,384]{1,0:T(8,128)(2,1)S(1)}, u32[]{:S(2)}, u32[]{:S(2)}) collective-permute-start(bf16[288,384]{1,0:T(8,128)(2,1)} %shard_map.55.rest_0_), channel_id=1, source_target_pairs={{0,32},{32,0},{64,96},{96,64},{128,160},{160,128},{192,224},{224,1... | collective-permute-start | bytes 663560 | tf_op jit(solution)/shard_map/ppermute | solution.py:261
  15.8 1.8 %collective-permute-start.4 = (bf16[288,384]{1,0:T(8,128)(2,1)S(1)}, bf16[288,384]{1,0:T(8,128)(2,1)S(1)}, u32[]{:S(2)}, u32[]{:S(2)}) collective-permute-start(bf16[288,384]{1,0:T(8,128)(2,1)S(1)} %collective-permute-done.rest_1_), channel_id=1, source_target_pairs={{0,32},{32,0},{64,96},{96,64},{128,160},{160,128},{192,224},{224,1... | collective-permute-start | bytes 663560 | tf_op jit(solution)/shard_map/ppermute | solution.py:261
  16.2 1.6 %collective-permute-start.5 = (bf16[288,384]{1,0:T(8,128)(2,1)S(1)}, bf16[288,384]{1,0:T(8,128)(2,1)S(1)}, u32[]{:S(2)}, u32[]{:S(2)}) collective-permute-start(bf16[288,384]{1,0:T(8,128)(2,1)S(1)} %collective-permute-done.1.rest_2_), channel_id=1, source_target_pairs={{0,32},{32,0},{64,96},{96,64},{128,160},{160,128},{192,224},{224,1... | collective-permute-start | bytes 663560 | tf_op jit(solution)/shard_map/ppermute | solution.py:261
  16.4 1.8 %collective-permute-start.6 = (bf16[288,384]{1,0:T(8,128)(2,1)S(1)}, bf16[288,384]{1,0:T(8,128)(2,1)S(1)}, u32[]{:S(2)}, u32[]{:S(2)}) collective-permute-start(bf16[288,384]{1,0:T(8,128)(2,1)S(1)} %collective-permute-done.2.rest_3_), channel_id=1, source_target_pairs={{0,32},{32,0},{64,96},{96,64},{128,160},{160,128},{192,224},{224,1... | collective-permute-start | bytes 663560 | tf_op jit(solution)/shard_map/ppermute | solution.py:261
  17.4 0.8 copy-start.11
  17.5 0.7 copy-start.12
  17.8 0.7 copy-start.13
  18.2 0.7 copy-start.14
  45.0 14.4 %collective-permute-start.7 = (bf16[8,24192]{1,0:T(8,128)(2,1)}, bf16[8,24192]{1,0:T(8,128)(2,1)S(1)}, u32[]{:S(2)}, u32[]{:S(2)}) collective-permute-start(bf16[8,24192]{1,0:T(8,128)(2,1)} %get-tuple-element.41), channel_id=1, source_target_pairs={{0,1},{1,2},{2,3},{3,0},{4,5},{5,6},{6,7},{7,4},{8,9},{9,10},{10,1... | collective-permute-start | bytes 1161224 | tf_op jit(solution)/shard_map/ppermute | solution.py:264
  46.7 20.5 %collective-permute-start.8 = (bf16[8,24192]{1,0:T(8,128)(2,1)}, bf16[8,24192]{1,0:T(8,128)(2,1)S(1)}, u32[]{:S(2)}, u32[]{:S(2)}) collective-permute-start(bf16[8,24192]{1,0:T(8,128)(2,1)} %get-tuple-element.42), channel_id=1, source_target_pairs={{0,2},{1,3},{2,0},{3,1},{4,6},{5,7},{6,4},{7,5},{8,10},{9,11},{10,... | collective-permute-start | bytes 1161224 | tf_op jit(solution)/shard_map/ppermute | solution.py:264
  49.6 17.6 %collective-permute-start.9 = (bf16[8,24192]{1,0:T(8,128)(2,1)}, bf16[8,24192]{1,0:T(8,128)(2,1)S(1)}, u32[]{:S(2)}, u32[]{:S(2)}) collective-permute-start(bf16[8,24192]{1,0:T(8,128)(2,1)} %get-tuple-element.43), channel_id=1, source_target_pairs={{0,3},{1,0},{2,1},{3,2},{4,7},{5,4},{6,5},{7,6},{8,11},{9,8},{10,9... | collective-permute-start | bytes 1161224 | tf_op jit(solution)/shard_map/ppermute | solution.py:264
  51.0 24.0 %all-to-all-start.1 = ((bf16[8,224,128]{2,1,0:T(8,128)(2,1)}), bf16[8,224,128]{2,1,0:T(8,128)(2,1)S(1)}, u32[]{:S(2)}, u32[]{:S(2)}) async-start(bf16[8,224,128]{2,1,0:T(8,128)(2,1)} %get-tuple-element.44), calls=%async_computation.1 | async-start | bytes 917504 | tf_op jit(solution)/shard_map/all_to_all | solution.py:267
  59.4 7.8 %copy-start.5 = (bf16[8,24192]{1,0:T(8,128)(2,1)}, bf16[8,24192]{1,0:T(8,128)(2,1)S(1)}, u32[]{:S(2)}) copy-start(bf16[8,24192]{1,0:T(8,128)(2,1)S(1)} %collective-permute-done.7.x1) | copy-start | bytes 1161220
  67.2 0.7 copy-start.6
  67.2 0.9 copy-start.7
  75.0 4.4 %copy-start = (bf16[8,224,128]{2,1,0:T(8,128)(2,1)}, bf16[8,224,128]{2,1,0:T(8,128)(2,1)S(1)}, u32[]{:S(2)}) copy-start(bf16[8,224,128]{2,1,0:T(8,128)(2,1)S(1)} %all-to-all-done.1.x_ref) | copy-start | bytes 1376260
  75.0 18.6 %all-to-all-start = ((bf16[8,192,128]{2,1,0:T(8,128)(2,1)}), bf16[8,192,128]{2,1,0:T(8,128)(2,1)S(1)}, u32[]{:S(2)}, u32[]{:S(2)}) async-start(bf16[8,192,128]{2,1,0:T(8,128)(2,1)} %shard_map.58), calls=%async_computation | async-start | bytes 786432 | tf_op jit(solution)/shard_map/all_to_all | solution.py:267
  81.1 5.1 %collective-permute-start.10 = (bf16[56,128]{1,0:T(8,128)(2,1)}, bf16[56,128]{1,0:T(8,128)(2,1)S(1)}, u32[]{:S(2)}, u32[]{:S(2)}) collective-permute-start(bf16[56,128]{1,0:T(8,128)(2,1)} %get-tuple-element.46), channel_id=1, source_target_pairs={{0,1},{1,2},{2,3},{3,0},{4,5},{5,6},{6,7},{7,4},{8,9},{9,10},{10,1... | collective-permute-start | bytes 43016 | tf_op jit(solution)/shard_map/ppermute | solution.py:264
  82.2 5.4 %collective-permute-start.11 = (bf16[56,128]{1,0:T(8,128)(2,1)}, bf16[56,128]{1,0:T(8,128)(2,1)S(1)}, u32[]{:S(2)}, u32[]{:S(2)}) collective-permute-start(bf16[56,128]{1,0:T(8,128)(2,1)} %get-tuple-element.47), channel_id=1, source_target_pairs={{0,2},{1,3},{2,0},{3,1},{4,6},{5,7},{6,4},{7,5},{8,10},{9,11},{10,... | collective-permute-start | bytes 43016 | tf_op jit(solution)/shard_map/ppermute | solution.py:264
  84.6 3.9 %collective-permute-start.12 = (bf16[56,128]{1,0:T(8,128)(2,1)}, bf16[56,128]{1,0:T(8,128)(2,1)S(1)}, u32[]{:S(2)}, u32[]{:S(2)}) collective-permute-start(bf16[56,128]{1,0:T(8,128)(2,1)} %get-tuple-element.48), channel_id=1, source_target_pairs={{0,3},{1,0},{2,1},{3,2},{4,7},{5,4},{6,5},{7,6},{8,11},{9,8},{10,9... | collective-permute-start | bytes 43016 | tf_op jit(solution)/shard_map/ppermute | solution.py:264
  86.3 7.3 %copy-start.2 = (bf16[56,128]{1,0:T(8,128)(2,1)}, bf16[56,128]{1,0:T(8,128)(2,1)S(1)}, u32[]{:S(2)}) copy-start(bf16[56,128]{1,0:T(8,128)(2,1)S(1)} %collective-permute-done.10.y1) | copy-start | bytes 43012
  87.7 5.9 %copy-start.3 = (bf16[56,128]{1,0:T(8,128)(2,1)}, bf16[56,128]{1,0:T(8,128)(2,1)S(1)}, u32[]{:S(2)}) copy-start(bf16[56,128]{1,0:T(8,128)(2,1)S(1)} %collective-permute-done.11.y2) | copy-start | bytes 43012
  88.6 5.1 %copy-start.4 = (bf16[56,128]{1,0:T(8,128)(2,1)}, bf16[56,128]{1,0:T(8,128)(2,1)S(1)}, u32[]{:S(2)}) copy-start(bf16[56,128]{1,0:T(8,128)(2,1)S(1)} %collective-permute-done.12.y3) | copy-start | bytes 43012
  93.6 0.7 copy-start.1
